TPU v7x, 512 devices: a whole 4x8x8 slice. The times are simulated.
512 devices in a mesh: row: 16 (over z_hi, x), col: 32 (over z_lo, y, core).
Axes of the slice: x: 4, y: 8, z: 8 (z_hi: 4, z_lo: 2; z = z_hi * 2 + z_lo), core: 2. Of those that a mesh axis runs over, the one named last changes fastest.
Arguments:
- query_sketches: bfloat16 [512, 16384], P('row', 'col'), may hold values from -200 to 200
- fisher_inverse: bfloat16 [16384, 16384], P('row', 'col'), may hold values from -1 to 3, as said below
- index_tiles: bfloat16 [32768, 16384], P('col', 'row'), may hold values from -6 to 6
Outputs:
- scores: float32 [512, 32768], P('row', 'col')
Inputs may be any that keep to these rules, and one draw needn't show every extreme that they name: `fisher_inverse`: symmetric.
All inputs are finite; a program needn't handle non-finite values.
Results may differ from a plain program's by a relative error of at most 0.0029.
Values may be sent and summed in bfloat16 or wider, within the bound.
No kernel may reach another device: no remote copies, remote signals or barrier semaphores. Data moves between devices by JAX's collectives and lax.ppermute only.
A program may use at most 64 MiB of HBM per device.

v0:
```python
import jax
import jax.numpy as jnp
from jax import lax
from jax.sharding import PartitionSpec as P


def local(query_sketches, fisher_inverse, index_tiles):
    query_wide = lax.all_gather(query_sketches, "col", axis=1, tiled=True)
    query_block = lax.all_to_all(query_wide, "row", split_axis=1, concat_axis=0, tiled=True)
    picked = query_block
    partial_rows = lax.psum_scatter(
        jnp.dot(picked, fisher_inverse, preferred_element_type=jnp.float32),
        "row",
        scatter_dimension=0,
        tiled=True,
    )
    sketch_wide = lax.all_gather(partial_rows, "col", axis=1, tiled=True)
    squares = jnp.sum(sketch_wide * sketch_wide, axis=1, keepdims=True)
    unit_wide = (sketch_wide / jnp.sqrt(squares + 1e-06)).astype(jnp.bfloat16)
    unit_block = lax.all_to_all(unit_wide, "row", split_axis=1, concat_axis=0, tiled=True)
    picked = unit_block
    return lax.psum_scatter(
        lax.dot_general(
            picked, index_tiles, (((1,), (1,)), ((), ())), preferred_element_type=jnp.float32
        ),
        "row",
        scatter_dimension=0,
        tiled=True,
    )


def solution(mesh):
    placed = (P("row", "col"), P("row", "col"), P("col", "row"))
    return jax.shard_map(
        local, mesh=mesh, in_specs=placed, out_specs=P("row", "col"), check_vma=False
    )
```

profile of v0, /device:TPU:1, one launch (start us, length us, event | category | flops | bytes accessed | tf_op | source)
XLA Modules:
  0.0 417.8 jit_solution(11564219588661952687)
XLA Ops:
  6.5 0.0 copy-start
  6.5 0.0 all-gather.3.cloned.1.call-start
  6.5 0.7 all-gather.3.cloned.1.call-update
  7.3 0.0 reduce-scatter.3.cloned.1.call-start
  7.3 74.4 %all-gather.3.cloned.1.call-done = bf16[32,16384]{1,0:T(8,128)(2,1)} async-done(((bf16[32,512]{1,0:T(8,128)(2,1)}), bf16[32,16384]{1,0:T(8,128)(2,1)}) %all-gather.3.cloned.1.call-update) | async-done | bytes 1048592 | tf_op jit(solution)/shard_map/all_gather | solution.py:8
  81.7 1.4 copy.14
  83.1 33.6 %all_to_all.38 = bf16[32,16,1024]{2,0,1:T(8,128)(2,1)S(1)} all-to-all(bf16[32,16,1024]{2,0,1:T(8,128)(2,1)S(1)} %bitcast.19), channel_id=1, replica_groups=mesh['row'=16,'col'=32] {'row'}, dimensions={1} | all-to-all | bytes 2097152 | tf_op jit(solution)/shard_map/all_to_all | solution.py:9
  116.7 0.0 copy-done.2
  116.7 1.7 fusion
  118.3 0.0 reduce-scatter.3.cloned.1.call-update
  118.4 0.0 all-gather.5.cloned.1.call-start
  118.4 91.2 %reduce-scatter.3.cloned.1.call-done = f32[32,512]{1,0:T(8,128)} async-done(((f32[512,512]{1,0:T(8,128)}), f32[32,512]{1,0:T(8,128)}) %reduce-scatter.3.cloned.1.call-update) | async-done | bytes 65552 | tf_op jit(solution)/shard_map/reduce_scatter | solution.py:11
  209.7 0.0 all-gather.5.cloned.1.call-update
  209.7 0.0 reduce-scatter.5.cloned.1.call-start
  209.7 68.9 %all-gather.5.cloned.1.call-done = f32[32,16384]{1,0:T(8,128)} async-done(((f32[32,512]{1,0:T(8,128)}), f32[32,16384]{1,0:T(8,128)}) %all-gather.5.cloned.1.call-update) | async-done | bytes 2097168 | tf_op jit(solution)/shard_map/all_gather | solution.py:17
  278.6 2.0 multiply_reduce_fusion
  280.6 0.2 copy-done.1
  280.9 0.2 divide_convert_fusion
  281.0 0.1 copy.13
  281.1 34.5 %all_to_all.39 = bf16[32,16,1024]{2,0,1:T(8,128)(2,1)S(1)} all-to-all(bf16[32,16,1024]{2,0,1:T(8,128)(2,1)S(1)} %bitcast.20), channel_id=1, replica_groups=mesh['row'=16,'col'=32] {'row'}, dimensions={1} | all-to-all | bytes 2097152 | tf_op jit(solution)/shard_map/all_to_all | solution.py:20
  315.7 0.0 copy-done
  315.7 2.6 fusion.1
  318.3 0.0 reduce-scatter.5.cloned.1.call-update
  318.4 92.9 %reduce-scatter.5.cloned.1.call-done = f32[32,1024]{1,0:T(8,128)} async-done(((f32[512,1024]{1,0:T(8,128)}), f32[32,1024]{1,0:T(8,128)}) %reduce-scatter.5.cloned.1.call-update) | async-done | bytes 131088 | tf_op jit(solution)/shard_map/reduce_scatter | solution.py:22
  (3 shorter events, 0.0 us)
Async XLA Ops:
  6.5 309.1 %copy-start = (bf16[1024,1024]{1,0:T(8,128)(2,1)S(1)}, bf16[1024,1024]{1,0:T(8,128)(2,1)}, u32[]{:S(2)}) copy-start(bf16[1024,1024]{1,0:T(8,128)(2,1)} %param.5) | copy-start | bytes 6291460
  6.5 75.1 %all-gather.3.cloned.1.call-start = ((), (), s32[]{:S(2)}) async-start(), calls=%async_computation.4 | async-start | bytes 1081344 | tf_op jit(solution)/shard_map/all_gather | solution.py:8
  7.3 202.4 %reduce-scatter.3.cloned.1.call-start = ((), (), s32[]{:S(2)}) async-start(), calls=%async_computation.5 | async-start | bytes 1114112 | tf_op jit(solution)/shard_map/reduce_scatter | solution.py:11
  81.7 35.0 %copy-start.2 = (bf16[1024,512]{1,0:T(8,128)(2,1)S(1)}, bf16[1024,512]{1,0:T(8,128)(2,1)}, u32[]{:S(2)}) copy-start(bf16[1024,512]{1,0:T(8,128)(2,1)} %param.4) | copy-start | bytes 3145732
  118.4 160.3 %all-gather.5.cloned.1.call-start = ((), (), s32[]{:S(2)}) async-start(), calls=%async_computation.6 | async-start | bytes 2162688 | tf_op jit(solution)/shard_map/all_gather | solution.py:17
  209.7 201.6 %reduce-scatter.5.cloned.1.call-start = ((), (), s32[]{:S(2)}) async-start(), calls=%async_computation.7 | async-start | bytes 2228224 | tf_op jit(solution)/shard_map/reduce_scatter | solution.py:22
  278.6 2.2 copy-start.1
Sparse Core Ops, SparseCore 0:
  9.5 72.1 all-gather.2
  118.5 91.1 reduce-scatter.2
  211.8 66.7 all-gather.4
  318.5 92.7 reduce-scatter.4
where the time goes:
time: 419 us; the launch traced here: 418 us
  waiting for transfers between devices  328 us (78%)
  blocking collectives  68.1 us (16%)
  between operations  13.2 us (3%)
  matrix products  4.32 us (1%)
    reduce_scatter x1, waiting for transfers between devices, local(): lax.psum_scatter(lax.dot_general(picked, index_tiles, (((1,), (1,)), ((),...  92.9 us
    reduce_scatter x1, waiting for transfers between devices, local(): lax.psum_scatter(jnp.dot(picked, fisher_inverse, preferred_element_type=j...  91.2 us
    all_gather x1, waiting for transfers between devices, local(): query_wide = lax.all_gather(query_sketches, 'col', axis=1, tiled=True)  74.4 us
    all_gather x1, waiting for transfers between devices, local(): sketch_wide = lax.all_gather(partial_rows, 'col', axis=1, tiled=True)  68.9 us
    all_to_all x1, blocking collectives, local(): lax.all_to_all(unit_wide, 'row', split_axis=1, concat_axis=0, tiled=True)  34.5 us
    all_to_all x1, blocking collectives, local(): lax.all_to_all(query_wide, 'row', split_axis=1, concat_axis=0, tiled=True)  33.6 us
  transfers between devices with their start and end apart: 4, of which 4 were waited for; matrix products, arithmetic and copies ran while one was open for 0% of the time, Pallas kernels for 0%

commit v1 on v0

v1 whole, which is shorter than its diff:
```python
import functools

import jax
import jax.numpy as jnp
from jax import lax
from jax.experimental import pallas as pl
from jax.experimental.pallas import tpu as pltpu
from jax.sharding import Mesh, PartitionSpec as P

F32, F16, BF16 = jnp.float32, jnp.float16, jnp.bfloat16
AXES = ("zh", "x", "zl", "y", "k")
ROW = ("zh", "x")
PAIR = ("zl", "y")
LANES = 128
VMEM, SMEM = pltpu.VMEM, pltpu.SMEM


def exponent(rows):
    top = jnp.max(jnp.abs(rows), axis=-1, keepdims=True)
    return jnp.clip(jnp.ceil(jnp.log2(jnp.maximum(top, 1e-30))), -100.0, 100.0)


def columns(height, *values):
    lane = lax.broadcasted_iota(jnp.int32, (height, LANES), 1)
    out = jnp.zeros((height, LANES), F32)
    for place, value in enumerate(values):
        out = jnp.where(lane == place, value, out)
    return out


def pieces(value):
    out = []
    for _ in range(3):
        out.append(value.astype(BF16).astype(F32))
        value = value - out[-1]
    return out


def dot_t(a, b):
    return lax.dot_general(a, b, (((1,), (1,)), ((), ())), preferred_element_type=F32)


def first_kernel(order, me, held, fisher, other, out):
    core = me[0]
    groups, _, height, width = held.shape
    mine = held[:, core].reshape(groups * height, width)
    theirs = held[:, 1 - core].reshape(groups * height, width)
    part = dot_t(mine, fisher[...]) + dot_t(theirs, other[...])
    features = part.shape[1]
    e = exponent(part)
    part = part * jnp.exp2(12.0 - e)
    tail = columns(groups * height, e)
    for to, source in enumerate(order):
        out[to * height : (to + 1) * height, :features] = part[source * height : (source + 1) * height]
        out[to * height : (to + 1) * height, features:] = tail[source * height : (source + 1) * height]


def unit_kernel(got, out):
    copies, height, wide = out.shape
    features = wide - LANES
    full = jnp.zeros((height, features), F32)
    for source in range(got.shape[0]):
        full += got[source, :, :features] * jnp.exp2(got[source, :, features : features + 1] - 12.0)
    g = exponent(full)
    unit = full * jnp.exp2(-g)
    squares = jnp.sum(unit * unit, axis=-1, keepdims=True)
    unit = unit.astype(BF16)
    tail = columns(height, g, *pieces(squares)).astype(BF16)
    for copy in range(copies):
        out[copy, :, :features] = unit
        out[copy, :, features:] = tail


def score_kernel(got, index, other, out, held, sems):
    count, features = index.shape
    copies = [pltpu.make_async_copy(ref, held.at[i], sems.at[i]) for i, ref in enumerate((index, other))]
    for copy in copies:
        copy.start()
    out[:, 2 * count :] = got[:, features:].astype(F32)
    for i, copy in enumerate(copies):
        copy.wait()
        out[:, i * count : (i + 1) * count] = dot_t(got[:, :features], held[i]) * 8.0


def combine(got, wide, factor):
    sources = got.shape[0]
    tails = [got[i, :, wide:] for i in range(sources)]
    top = tails[0][:, :1]
    for tail in tails[1:]:
        top = jnp.maximum(top, tail[:, :1])
    total, squares = 0.0, 0.0
    for i, tail in enumerate(tails):
        scale = jnp.exp2(tail[:, :1] - top)
        total += got[i, :, :wide] * (scale * factor)
        squares += (tail[:, 1:2] + tail[:, 2:3] + tail[:, 3:4]) * (scale * scale)
    return total, squares, top


def middle_kernel(me, got, out):
    wide = got.shape[2] - LANES
    count = wide // 2
    total, squares, top = combine(got, wide, 0.25)
    tail = columns(total.shape[0], top, *pieces(squares))
    groups, _, height, _ = out.shape
    swapped = me[0] != 0
    own, other = total[:, :count], total[:, count:]
    halves = (jnp.where(swapped, other, own), jnp.where(swapped, own, other))
    for z in range(groups):
        for k, half in enumerate(halves):
            out[z, k, :, :count] = half[z * height : (z + 1) * height]
            out[z, k, :, count:] = tail[z * height : (z + 1) * height]


def last_kernel(got, out):
    wide = out.shape[1]
    total, squares, top = combine(got, wide, 0.5)
    out[...] = total / jnp.sqrt(squares + 1e-06 * jnp.exp2(-2.0 * jnp.maximum(top, -60.0)))


def call(kernel, spaces, shape, dtype, *args, **kwargs):
    return pl.pallas_call(
        kernel,
        out_shape=jax.ShapeDtypeStruct(shape, dtype),
        in_specs=[pl.BlockSpec(memory_space=space) for space in spaces],
        out_specs=pl.BlockSpec(memory_space=VMEM),
        compiler_params=pltpu.CompilerParams(vmem_limit_bytes=16 << 20),
        **kwargs,
    )(*args)


def swap(array):
    return lax.ppermute(array, "k", [(0, 1), (1, 0)])


def local(sizes, query, fisher, index):
    zh, x, zl, y, k = (sizes[a] for a in AXES)
    rows, pairs = zh * x, zl * y
    me = lax.axis_index("k").astype(jnp.int32).reshape(1)
    fisher_other = swap(fisher)
    index_other = swap(index)
    height, width = query.shape[0] // k, query.shape[1]
    features, count = fisher.shape[0], index.shape[0]
    batch = rows * height

    copies = jnp.broadcast_to(query[None], (rows,) + query.shape).reshape(-1, width)
    held = lax.all_to_all(copies, (*ROW, "k"), 0, 0, tiled=True).reshape(rows, k, height, width)

    order = tuple(z * x + i for i in range(x) for z in range(zh))
    sent = call(
        functools.partial(first_kernel, order), (SMEM, VMEM, VMEM, VMEM), (batch, features + LANES), F32,
        me, held, fisher, fisher_other,
    )
    got = lax.all_to_all(sent.astype(F16), PAIR, 0, 0, tiled=True).astype(F32)
    got = got.reshape(pairs, -1, features + LANES)

    sent = call(unit_kernel, (VMEM,), got.shape, BF16, got)
    got = lax.all_to_all(sent.reshape(batch, -1), PAIR, 0, 0, tiled=True)

    sent = call(
        score_kernel, (VMEM, pl.ANY, pl.ANY), (batch, 2 * count + LANES), F32, got, index, index_other,
        scratch_shapes=[VMEM((2, count, features), BF16), pltpu.SemaphoreType.DMA((2,))],
    )
    got = lax.all_to_all(sent.astype(F16), "x", 0, 0, tiled=True).astype(F32)
    got = got.reshape(x, zh * height, -1)

    sent = call(middle_kernel, (SMEM, VMEM), (zh, k, height, count + LANES), F32, me, got)
    sent = sent.reshape(zh * k * height, -1)
    got = lax.all_to_all(sent.astype(F16), ("zh", "k"), 0, 0, tiled=True).astype(F32)
    return call(last_kernel, (VMEM,), (k * height, count), F32, got.reshape(zh, k * height, -1))


def fine_mesh(mesh):
    rows, cols = mesh.devices.shape
    shape = (rows // 4, 4, 2, cols // 4, 2) if rows >= 16 else (2, rows // 2, 2, cols // 4, 2)
    return Mesh(mesh.devices.reshape(shape), AXES)


def solution(mesh):
    fine = fine_mesh(mesh)
    sizes = dict(fine.shape)
    row, col = ROW, (*PAIR, "k")
    placed = (P(row, col), P(row, col), P(col, row))
    return jax.shard_map(
        functools.partial(local, sizes), mesh=fine, in_specs=placed, out_specs=P(row, col), check_vma=False
    )
```

time: 419 us -> 124 us (0.30)
  waiting for transfers between devices: 328 us -> 45.5 us
  blocking collectives: 68.1 us -> 33.8 us
  starting transfers between devices: 0.12 us -> 34.4 us
  between operations: 13.2 us -> 0.13 us
  Pallas kernels: 0 us -> 5.77 us
  matrix products: 4.32 us -> 0 us
    reduce_scatter x2 -> x0, waiting for transfers between devices: 184 us -> none  [the longest x1 92.9 us: local(): lax.psum_scatter(lax.dot_general(picked, index_tiles, (((1,), (1,)), ((),...]
    all_gather x2 -> x0, waiting for transfers between devices: 143 us -> none  [the longest x1 74.4 us: local(): query_wide = lax.all_gather(query_sketches, 'col', axis=1, tiled=True)]
    all_to_all x0 -> x3, waiting for transfers between devices: none -> 45.5 us  [the longest x1 16.9 us: local(): lax.all_to_all(copies, (*ROW, 'k'), 0, 0, tiled=True)]
    all_to_all x2, blocking collectives: 68.1 us -> 33.8 us  [the longest x1 17.2 us: local(): lax.all_to_all(sent.astype(F16), ('zh', 'k'), 0, 0, tiled=True).astype(F32)]
    all_to_all x0 -> x3, starting transfers between devices: none -> 22.8 us  [the longest x1 9.17 us: local(): got = lax.all_to_all(sent.astype(F16), PAIR, 0, 0, tiled=True).astype(F32)]
    ppermute x0 -> x2, starting transfers between devices: none -> 11.6 us  [swap(): return lax.ppermute(array, 'k', [(0, 1), (1, 0)])]
    pallas_call x0 -> x5, Pallas kernels: none -> 5.77 us  [call(): pl.pallas_call(kernel, out_shape=jax.ShapeDtypeStruct(shape, dtype), in_s...]
    dot_general x2 -> x0, matrix products: 4.32 us -> none  [the longest x1 2.65 us: local(): lax.dot_general(picked, index_tiles, (((1,), (1,)), ((), ())), preferred_...]
  transfers between devices with their start and end apart: 4 -> 5, of which waited for: 4 -> 3; matrix products, arithmetic and copies ran while one was open for 0% -> 1% of each run, Pallas kernels for 0% -> 1%
where the time goes in v1:
time: 124 us; the launch traced here: 122 us
  waiting for transfers between devices  45.5 us (37%)
  starting transfers between devices  34.4 us (28%)
  blocking collectives  33.8 us (27%)
  Pallas kernels  5.77 us (5%)
  local copies, waits for them, and re-layouts  1.62 us (1%)
  other arithmetic  1.3 us (1%)
    all_to_all x1, blocking collectives, local(): lax.all_to_all(sent.astype(F16), ('zh', 'k'), 0, 0, tiled=True).astype(F32)  17.2 us
    all_to_all x1, waiting for transfers between devices, local(): lax.all_to_all(copies, (*ROW, 'k'), 0, 0, tiled=True)  16.9 us
    all_to_all x1, blocking collectives, local(): got = lax.all_to_all(sent.astype(F16), 'x', 0, 0, tiled=True).astype(F32)  16.5 us
    all_to_all x1, waiting for transfers between devices, local(): got = lax.all_to_all(sent.reshape(batch, -1), PAIR, 0, 0, tiled=True)  15.6 us
    all_to_all x1, waiting for transfers between devices, local(): got = lax.all_to_all(sent.astype(F16), PAIR, 0, 0, tiled=True).astype(F32)  13 us
    ppermute x2, starting transfers between devices, swap(): return lax.ppermute(array, 'k', [(0, 1), (1, 0)])  11.6 us
    all_to_all x1, starting transfers between devices, local(): got = lax.all_to_all(sent.astype(F16), PAIR, 0, 0, tiled=True).astype(F32)  9.17 us
    all_to_all x1, starting transfers between devices, local(): lax.all_to_all(copies, (*ROW, 'k'), 0, 0, tiled=True)  7.69 us
  transfers between devices with their start and end apart: 5, of which 3 were waited for; matrix products, arithmetic and copies ran while one was open for 1% of the time, Pallas kernels for 1%

profile of v1, /device:TPU:1, one launch (start us, length us, event | category | flops | bytes accessed | tf_op | source)
XLA Modules:
  0.0 122.4 jit_solution(6733344018182620229)
XLA Ops:
  0.0 8.9 %collective-permute-start = (bf16[1024,512]{1,0:T(8,128)(2,1)}, bf16[1024,512]{1,0:T(8,128)(2,1)S(1)}, u32[]{:S(2)}, u32[]{:S(2)}) collective-permute-start(bf16[1024,512]{1,0:T(8,128)(2,1)} %fisher.1), channel_id=1, source_target_pairs={{0,1},{1,0},{2,3},{3,2},{4,5},{5,4},{6,7},{7,6},{8,9},{9,8},{10,11... | collective-permute-start | bytes 3145736 | tf_op jit(solution)/shard_map/ppermute | solution.py:132
  8.9 1.6 %broadcast_in_dim.2 = bf16[16,32,512]{2,1,0:T(8,128)(2,1)} broadcast(bf16[32,512]{1,0:T(8,128)(2,1)} %param.3), dimensions={1,2} | broadcast | bytes 557056 | tf_op jit(solution)/shard_map/broadcast_in_dim | solution.py:145
  10.5 7.7 %all-to-all-start = ((bf16[32,16,512]{2,1,0:T(8,128)(2,1)}), bf16[32,16,512]{2,1,0:T(8,128)(2,1)S(1)}, u32[]{:S(2)}, u32[]{:S(2)}) async-start(bf16[32,16,512]{2,1,0:T(8,128)(2,1)} %bitcast.1), calls=%async_computation | async-start | bytes 1048576 | tf_op jit(solution)/shard_map/all_to_all | solution.py:146
  18.2 16.9 %all-to-all-done = bf16[32,16,512]{2,1,0:T(8,128)(2,1)S(1)} async-done(((bf16[32,16,512]{2,1,0:T(8,128)(2,1)}), bf16[32,16,512]{2,1,0:T(8,128)(2,1)S(1)}, u32[]{:S(2)}, u32[]{:S(2)}) %all-to-all-start) | async-done | bytes 524320 | tf_op jit(solution)/shard_map/all_to_all | solution.py:146
  35.0 0.0 collective-permute-done.other
  35.0 0.0 copy-done.1
  35.0 0.8 shard_map.37
  35.9 0.0 copy-start
  35.9 0.9 convert_element_type.28
  36.8 9.2 %all-to-all-start.1 = ((f16[16,16,1152]{2,1,0:T(8,128)(2,1)}), f16[16,16,1152]{2,1,0:T(8,128)(2,1)S(1)}, u32[]{:S(2)}, u32[]{:S(2)}) async-start(f16[16,16,1152]{2,1,0:T(8,128)(2,1)} %bitcast.3), calls=%async_computation.1 | async-start | bytes 1179648 | tf_op jit(solution)/shard_map/all_to_all | solution.py:153
  46.0 2.7 %collective-permute-start.1 = (bf16[1024,1024]{1,0:T(8,128)(2,1)S(1)}, bf16[1024,1024]{1,0:T(8,128)(2,1)}, u32[]{:S(2)}, u32[]{:S(2)}) collective-permute-start(bf16[1024,1024]{1,0:T(8,128)(2,1)S(1)} %copy-done), channel_id=1, source_target_pairs={{0,1},{1,0},{2,3},{3,2},{4,5},{5,4},{6,7},{7,6},{8,9},{9,8},{10,11... | collective-permute-start | bytes 6291464 | tf_op jit(solution)/shard_map/ppermute | solution.py:132
  48.7 13.0 %all-to-all-done.1 = f16[16,16,1152]{2,1,0:T(8,128)(2,1)S(1)} async-done(((f16[16,16,1152]{2,1,0:T(8,128)(2,1)}), f16[16,16,1152]{2,1,0:T(8,128)(2,1)S(1)}, u32[]{:S(2)}, u32[]{:S(2)}) %all-to-all-start.1) | async-done | bytes 589856 | tf_op jit(solution)/shard_map/all_to_all | solution.py:153
  61.7 0.1 convert_element_type.29.got
  61.8 1.2 shard_map.38
  62.9 5.9 %all-to-all-start.2 = ((bf16[16,16,1152]{2,1,0:T(8,128)(2,1)}), bf16[16,16,1152]{2,1,0:T(8,128)(2,1)S(1)}, u32[]{:S(2)}, u32[]{:S(2)}) async-start(bf16[16,16,1152]{2,1,0:T(8,128)(2,1)} %shard_map.38), calls=%async_computation.2 | async-start | bytes 1179648 | tf_op jit(solution)/shard_map/all_to_all | solution.py:157
  68.9 0.0 collective-permute-done.1.other
  68.9 15.6 %all-to-all-done.2 = bf16[16,16,1152]{2,1,0:T(8,128)(2,1)S(1)} async-done(((bf16[16,16,1152]{2,1,0:T(8,128)(2,1)}), bf16[16,16,1152]{2,1,0:T(8,128)(2,1)S(1)}, u32[]{:S(2)}, u32[]{:S(2)}) %all-to-all-start.2) | async-done | bytes 589856 | tf_op jit(solution)/shard_map/all_to_all | solution.py:157
  84.5 2.5 %shard_map.39 = f32[256,2176]{1,0:T(8,128)S(1)} custom-call(bf16[256,1152]{1,0:T(8,128)(2,1)S(1)} %bitcast.11, bf16[1024,1024]{1,0:T(8,128)(2,1)S(1)} %copy-done, bf16[1024,1024]{1,0:T(8,128)(2,1)} %collective-permute-done.1.other), custom_call_target="tpu_custom_call" | custom-call | tf_op jit(solution)/shard_map/pallas_call | solution.py:121
  87.0 0.1 convert_element_type.30
  87.1 16.5 %all_to_all.41 = f16[4,64,2176]{2,1,0:T(8,128)(2,1)S(1)} all-to-all(f16[4,64,2176]{2,1,0:T(8,128)(2,1)S(1)} %bitcast.13), channel_id=1, replica_groups=mesh['zh'=4,'x'=4,'zl'=2,'y'=8,'k'=2] {'x'}, dimensions={0} | all-to-all | bytes 2228224 | tf_op jit(solution)/shard_map/all_to_all | solution.py:163
  103.6 0.1 convert_element_type.31.got
  103.8 0.4 shard_map.40
  104.3 17.2 %all_to_all.42 = f16[8,16,1152]{2,1,0:T(8,128)(2,1)S(1)} all-to-all(f16[8,16,1152]{2,1,0:T(8,128)(2,1)S(1)} %bitcast.14), channel_id=1, replica_groups=mesh['zh'=4,'x'=4,'zl'=2,'y'=8,'k'=2] {'zh','k'}, dimensions={0} | all-to-all | bytes 589824 | tf_op jit(solution)/shard_map/all_to_all | solution.py:168
  121.5 0.9 shard_map.41
  (4 shorter events, 0.1 us)
Async XLA Ops:
  0.0 35.0 %copy-start.1 = (bf16[1024,512]{1,0:T(8,128)(2,1)S(1)}, bf16[1024,512]{1,0:T(8,128)(2,1)}, u32[]{:S(2)}) copy-start(bf16[1024,512]{1,0:T(8,128)(2,1)} %fisher.1) | copy-start | bytes 3145732
  0.0 35.0 %collective-permute-start = (bf16[1024,512]{1,0:T(8,128)(2,1)}, bf16[1024,512]{1,0:T(8,128)(2,1)S(1)}, u32[]{:S(2)}, u32[]{:S(2)}) collective-permute-start(bf16[1024,512]{1,0:T(8,128)(2,1)} %fisher.1), channel_id=1, source_target_pairs={{0,1},{1,0},{2,3},{3,2},{4,5},{5,4},{6,7},{7,6},{8,9},{9,8},{10,11... | collective-permute-start | bytes 3145736 | tf_op jit(solution)/shard_map/ppermute | solution.py:132
  10.5 24.6 %all-to-all-start = ((bf16[32,16,512]{2,1,0:T(8,128)(2,1)}), bf16[32,16,512]{2,1,0:T(8,128)(2,1)S(1)}, u32[]{:S(2)}, u32[]{:S(2)}) async-start(bf16[32,16,512]{2,1,0:T(8,128)(2,1)} %bitcast.1), calls=%async_computation | async-start | bytes 1048576 | tf_op jit(solution)/shard_map/all_to_all | solution.py:146
  35.9 10.1 %copy-start = (bf16[1024,1024]{1,0:T(8,128)(2,1)S(1)}, bf16[1024,1024]{1,0:T(8,128)(2,1)}, u32[]{:S(2)}) copy-start(bf16[1024,1024]{1,0:T(8,128)(2,1)} %index.1) | copy-start | bytes 6291460
  36.8 24.9 %all-to-all-start.1 = ((f16[16,16,1152]{2,1,0:T(8,128)(2,1)}), f16[16,16,1152]{2,1,0:T(8,128)(2,1)S(1)}, u32[]{:S(2)}, u32[]{:S(2)}) async-start(f16[16,16,1152]{2,1,0:T(8,128)(2,1)} %bitcast.3), calls=%async_computation.1 | async-start | bytes 1179648 | tf_op jit(solution)/shard_map/all_to_all | solution.py:153
  46.0 22.9 %collective-permute-start.1 = (bf16[1024,1024]{1,0:T(8,128)(2,1)S(1)}, bf16[1024,1024]{1,0:T(8,128)(2,1)}, u32[]{:S(2)}, u32[]{:S(2)}) collective-permute-start(bf16[1024,1024]{1,0:T(8,128)(2,1)S(1)} %copy-done), channel_id=1, source_target_pairs={{0,1},{1,0},{2,3},{3,2},{4,5},{5,4},{6,7},{7,6},{8,9},{9,8},{10,11... | collective-permute-start | bytes 6291464 | tf_op jit(solution)/shard_map/ppermute | solution.py:132
  62.9 21.6 %all-to-all-start.2 = ((bf16[16,16,1152]{2,1,0:T(8,128)(2,1)}), bf16[16,16,1152]{2,1,0:T(8,128)(2,1)S(1)}, u32[]{:S(2)}, u32[]{:S(2)}) async-start(bf16[16,16,1152]{2,1,0:T(8,128)(2,1)} %shard_map.38), calls=%async_computation.2 | async-start | bytes 1179648 | tf_op jit(solution)/shard_map/all_to_all | solution.py:157

commit v2 on v1

v2 whole, which is shorter than its diff:
```python
import functools

import jax
import jax.numpy as jnp
from jax import lax
from jax.experimental import pallas as pl
from jax.experimental.pallas import tpu as pltpu
from jax.sharding import Mesh, PartitionSpec as P

F32, F16, BF16 = jnp.float32, jnp.float16, jnp.bfloat16
AXES = ("zh", "xh", "xl", "zl", "y", "k")
LANES = 128
VMEM, SMEM = pltpu.VMEM, pltpu.SMEM


def exponent(rows):
    top = jnp.max(jnp.abs(rows), axis=-1, keepdims=True)
    return jnp.clip(jnp.ceil(jnp.log2(jnp.maximum(top, 1e-30))), -100.0, 100.0)


def columns(height, *values):
    lane = lax.broadcasted_iota(jnp.int32, (height, LANES), 1)
    out = jnp.zeros((height, LANES), F32)
    for place, value in enumerate(values):
        out = jnp.where(lane == place, value, out)
    return out


def pieces(value):
    out = []
    for _ in range(3):
        out.append(value.astype(BF16).astype(F32))
        value = value - out[-1]
    return out


def dot_t(a, b):
    return lax.dot_general(a, b, (((1,), (1,)), ((), ())), preferred_element_type=F32)


def first_kernel(order, height, me, held, fisher, other, out):
    core = me[0]
    groups, _, rows, width = held.shape
    mine = held[:, core].reshape(groups * rows, width)
    theirs = held[:, 1 - core].reshape(groups * rows, width)
    part = dot_t(mine, fisher[...]) + dot_t(theirs, other[...])
    features = part.shape[1]
    e = exponent(part)
    part = part * jnp.exp2(12.0 - e)
    tail = columns(part.shape[0], e)
    for to, source in enumerate(order):
        out[to * height : (to + 1) * height, :features] = part[source * height : (source + 1) * height]
        out[to * height : (to + 1) * height, features:] = tail[source * height : (source + 1) * height]


def unit_kernel(got, out):
    blocks, sources, height, wide = got.shape
    features = wide - LANES
    full = []
    for block in range(blocks):
        total = jnp.zeros((height, features), F32)
        for i in range(sources):
            total += got[block, i, :, :features] * jnp.exp2(got[block, i, :, features : features + 1] - 12.0)
        full.append(total)
    full = jnp.concatenate(full, axis=1)
    g = exponent(full)
    unit = full * jnp.exp2(-g)
    squares = jnp.sum(unit * unit, axis=-1, keepdims=True)
    unit = unit.astype(BF16)
    tail = columns(height, g, *pieces(squares)).astype(BF16)
    for copy in range(out.shape[0]):
        out[copy, :, : blocks * features] = unit
        out[copy, :, blocks * features :] = tail


def score_kernel(me, got, own, across, core, core_across, out):
    count, features = own.shape
    mine = got[:, pl.ds(pl.multiple_of(me[1] * features, features), features)]
    theirs = got[:, pl.ds(pl.multiple_of((1 - me[1]) * features, features), features)]
    tail = got[:, 2 * features :].astype(F32)
    groups, _, height, _ = out.shape
    for k, here, there in ((me[0], own, across), (1 - me[0], core, core_across)):
        scores = (dot_t(mine, here[...]) + dot_t(theirs, there[...])) * 4.0
        for i in range(groups):
            out[i, k, :, :count] = scores[i * height : (i + 1) * height]
            out[i, k, :, count:] = tail[i * height : (i + 1) * height]


def last_kernel(got, out):
    wide = out.shape[1]
    tails = [got[i, :, wide:] for i in range(got.shape[0])]
    top = tails[0][:, :1]
    for tail in tails[1:]:
        top = jnp.maximum(top, tail[:, :1])
    total, squares = 0.0, 0.0
    for i, tail in enumerate(tails):
        scale = jnp.exp2(tail[:, :1] - top)
        total += got[i, :, :wide] * (scale * 0.25)
        squares += (tail[:, 1:2] + tail[:, 2:3] + tail[:, 3:4]) * (scale * scale)
    out[...] = total / jnp.sqrt(squares + 1e-06 * jnp.exp2(-2.0 * jnp.maximum(top, -60.0)))


def call(kernel, shape, dtype, *args):
    spaces = [SMEM if arg.dtype == jnp.int32 else VMEM for arg in args]
    return pl.pallas_call(
        kernel,
        out_shape=jax.ShapeDtypeStruct(shape, dtype),
        in_specs=[pl.BlockSpec(memory_space=space) for space in spaces],
        out_specs=pl.BlockSpec(memory_space=VMEM),
        compiler_params=pltpu.CompilerParams(vmem_limit_bytes=24 << 20),
    )(*args)


def swap(array, axis):
    return lax.ppermute(array, axis, [(0, 1), (1, 0)])


def local(sizes, query, fisher, index):
    zh, xh, xl, zl, y, k = (sizes[a] for a in AXES)
    x, pairs = xh * xl, zl * y
    me = jnp.stack([lax.axis_index("k"), lax.axis_index("xl")]).astype(jnp.int32)
    height, width = query.shape[0] // k, query.shape[1]
    features, count = fisher.shape[0], index.shape[0]
    batch = zh * x * height

    copies = jnp.broadcast_to(query[None], (zh,) + query.shape).reshape(-1, width)
    held = lax.all_to_all(copies, "zh", 0, 0, tiled=True).reshape(zh, k, height, width)
    fisher_core = swap(fisher, "k")
    copies = jnp.broadcast_to(held.transpose(1, 0, 2, 3)[None], (x, k, zh, height, width)).reshape(-1, width)
    held = lax.all_to_all(copies, ("xh", "xl", "k"), 0, 0, tiled=True).reshape(x, k, zh * height, width)

    index_across = swap(index, "xl")
    index_core = swap(index, "k")
    index_core_across = swap(index_across, "k")

    order = tuple((h * xl + i) * zh + z for i in range(xl) for z in range(zh) for h in range(xh))
    sent = call(
        functools.partial(first_kernel, order, height), (batch, features + LANES), F32, me, held, fisher, fisher_core
    )
    got = lax.all_to_all(sent.astype(F16), ("xl", "zl", "y"), 0, 0, tiled=True).astype(F32)
    got = got.reshape(xl, pairs, -1, features + LANES)

    sent = call(unit_kernel, (pairs, got.shape[2], xl * features + LANES), BF16, got)
    got = lax.all_to_all(sent.reshape(batch // xl, -1), ("zl", "y"), 0, 0, tiled=True)

    sent = call(
        score_kernel, (zh * xh, k, height, count + LANES), F32,
        me, got, index, index_across, index_core, index_core_across,
    )
    sent = sent.reshape(batch, -1)
    got = lax.all_to_all(sent.astype(F16), ("zh", "xh", "k"), 0, 0, tiled=True).astype(F32)
    return call(last_kernel, (k * height, count), F32, got.reshape(zh * xh, k * height, -1))


def fine_mesh(mesh):
    rows, cols = mesh.devices.shape
    return Mesh(mesh.devices.reshape(rows // 4, 2, 2, 2, cols // 4, 2), AXES)


def solution(mesh):
    fine = fine_mesh(mesh)
    sizes = dict(fine.shape)
    row, col = AXES[:3], AXES[3:]
    placed = (P(row, col), P(row, col), P(col, row))
    return jax.shard_map(
        functools.partial(local, sizes), mesh=fine, in_specs=placed, out_specs=P(row, col), check_vma=False
    )
```

time: 124 us -> 146 us (1.18)
  blocking collectives: 33.8 us -> 47.2 us
  starting transfers between devices: 34.4 us -> 38.1 us
  Pallas kernels: 5.77 us -> 9.23 us
  waiting for transfers between devices: 45.5 us -> 48.1 us
    all_to_all x2, blocking collectives: 33.8 us -> 47.2 us  [the longest x1 33.8 us: local(): lax.all_to_all(sent.astype(F16), ('zh', 'xh', 'k'), 0, 0, tiled=True)]
    ppermute x2 -> x4, starting transfers between devices: 11.6 us -> 16.3 us  [swap(): return lax.ppermute(array, axis, [(0, 1), (1, 0)])]
    pallas_call x5 -> x4, Pallas kernels: 5.77 us -> 9.23 us  [call(): pl.pallas_call(kernel, out_shape=jax.ShapeDtypeStruct(shape, dtype), in_s...]
    all_to_all x3, waiting for transfers between devices: 45.5 us -> 48.1 us  [the longest x1 25.4 us: local(): lax.all_to_all(copies, ('xh', 'xl', 'k'), 0, 0, tiled=True)]
  transfers between devices with their start and end apart: 5 -> 7, of which waited for: 3 -> 3; matrix products, arithmetic and copies ran while one was open for 1% -> 2% of each run, Pallas kernels for 1% -> 2%
where the time goes in v2:
time: 146 us
  waiting for transfers between devices  48.1 us (33%)
  blocking collectives  47.2 us (32%)
  starting transfers between devices  38.1 us (26%)
  Pallas kernels  9.23 us (6%)
  local copies, waits for them, and re-layouts  1.64 us (1%)
    all_to_all x1, blocking collectives, local(): lax.all_to_all(sent.astype(F16), ('zh', 'xh', 'k'), 0, 0, tiled=True)  33.8 us
    all_to_all x1, waiting for transfers between devices, local(): lax.all_to_all(copies, ('xh', 'xl', 'k'), 0, 0, tiled=True)  25.4 us
    ppermute x4, starting transfers between devices, swap(): return lax.ppermute(array, axis, [(0, 1), (1, 0)])  16.3 us
    all_to_all x1, waiting for transfers between devices, local(): lax.all_to_all(sent.reshape(batch // xl, -1), ('zl', 'y'), 0, 0, tiled=True)  13.5 us
    all_to_all x1, blocking collectives, local(): lax.all_to_all(copies, 'zh', 0, 0, tiled=True).reshape(zh, k, height, width)  13.4 us
    pallas_call x4, Pallas kernels, call(): pl.pallas_call(kernel, out_shape=jax.ShapeDtypeStruct(shape, dtype), in_s...  9.23 us
    all_to_all x1, waiting for transfers between devices, local(): lax.all_to_all(sent.astype(F16), ('xl', 'zl', 'y'), 0, 0, tiled=True)  9.21 us
    all_to_all x1, starting transfers between devices, local(): lax.all_to_all(sent.astype(F16), ('xl', 'zl', 'y'), 0, 0, tiled=True)  9.02 us
  transfers between devices with their start and end apart: 7, of which 3 were waited for; matrix products, arithmetic and copies ran while one was open for 2% of the time, Pallas kernels for 2%

profile of v2, /device:TPU:1, one launch (start us, length us, event | category | flops | bytes accessed | tf_op | source)
XLA Modules:
  0.0 145.6 jit_solution(702450995585818085)
XLA Ops:
  0.0 4.1 %collective-permute-start.1 = (bf16[1024,1024]{1,0:T(8,128)(2,1)}, bf16[1024,1024]{1,0:T(8,128)(2,1)}, u32[]{:S(2)}, u32[]{:S(2)}) collective-permute-start(bf16[1024,1024]{1,0:T(8,128)(2,1)} %own.1), channel_id=1, source_target_pairs={{0,32},{32,0},{1,33},{33,1},{2,34},{34,2},{3,35},{35,3},{4,36},{36... | collective-permute-start | bytes 6291464 | tf_op jit(solution)/shard_map/ppermute | solution.py:115
  4.1 6.7 %collective-permute-start = (bf16[1024,512]{1,0:T(8,128)(2,1)}, bf16[1024,512]{1,0:T(8,128)(2,1)S(1)}, u32[]{:S(2)}, u32[]{:S(2)}) collective-permute-start(bf16[1024,512]{1,0:T(8,128)(2,1)} %fisher.1), channel_id=1, source_target_pairs={{0,1},{1,0},{2,3},{3,2},{4,5},{5,4},{6,7},{7,6},{8,9},{9,8},{10,11... | collective-permute-start | bytes 3145736 | tf_op jit(solution)/shard_map/ppermute | solution.py:115
  10.8 0.8 broadcast_in_dim.4
  11.6 13.4 %all_to_all.38 = bf16[4,32,512]{2,1,0:T(8,128)(2,1)S(1)} all-to-all(bf16[4,32,512]{2,1,0:T(8,128)(2,1)S(1)} %broadcast_in_dim.4), channel_id=1, replica_groups=mesh['zh'=4,'xh'=2,'xl'=2,'zl'=2,'y'=8,'k'=2] {'zh'}, dimensions={0} | all-to-all | bytes 262144 | tf_op jit(solution)/shard_map/all_to_all | solution.py:127
  24.9 0.9 broadcast_in_dim.5
  25.8 6.2 %all-to-all-start.1 = ((bf16[8,64,512]{2,1,0:T(8,128)(2,1)}), bf16[8,64,512]{2,1,0:T(8,128)(2,1)S(1)}, u32[]{:S(2)}, u32[]{:S(2)}) async-start(bf16[8,64,512]{2,1,0:T(8,128)(2,1)} %bitcast.4), calls=%async_computation.1 | async-start | bytes 1048576 | tf_op jit(solution)/shard_map/all_to_all | solution.py:130
  32.0 0.1 pad_add_fusion.me
  32.1 25.4 %all-to-all-done.1 = bf16[8,64,512]{2,1,0:T(8,128)(2,1)S(1)} async-done(((bf16[8,64,512]{2,1,0:T(8,128)(2,1)}), bf16[8,64,512]{2,1,0:T(8,128)(2,1)S(1)}, u32[]{:S(2)}, u32[]{:S(2)}) %all-to-all-start.1) | async-done | bytes 524320 | tf_op jit(solution)/shard_map/all_to_all | solution.py:130
  57.5 1.4 shard_map.37
  58.9 0.0 copy-start
  58.9 0.9 convert_bitcast_fusion
  59.8 9.0 %all-to-all-start.2 = ((f16[32,8,1152]{2,1,0:T(8,128)(2,1)}), f16[32,8,1152]{2,1,0:T(8,128)(2,1)S(1)}, u32[]{:S(2)}, u32[]{:S(2)}) async-start(f16[32,8,1152]{2,1,0:T(8,128)(2,1)} %convert_bitcast_fusion), calls=%async_computation.2 | async-start | bytes 1179648 | tf_op jit(solution)/shard_map/all_to_all | solution.py:140
  68.9 3.6 %collective-permute-start.2 = (bf16[1024,1024]{1,0:T(8,128)(2,1)S(1)}, bf16[1024,1024]{1,0:T(8,128)(2,1)}, u32[]{:S(2)}, u32[]{:S(2)}) collective-permute-start(bf16[1024,1024]{1,0:T(8,128)(2,1)S(1)} %copy-done), channel_id=1, source_target_pairs={{0,1},{1,0},{2,3},{3,2},{4,5},{5,4},{6,7},{7,6},{8,9},{9,8},{10,11... | collective-permute-start | bytes 6291464 | tf_op jit(solution)/shard_map/ppermute | solution.py:115
  72.5 1.9 %collective-permute-start.3 = (bf16[1024,1024]{1,0:T(8,128)(2,1)}, bf16[1024,1024]{1,0:T(8,128)(2,1)}, u32[]{:S(2)}, u32[]{:S(2)}) collective-permute-start(bf16[1024,1024]{1,0:T(8,128)(2,1)} %collective-permute-done.1.across), channel_id=1, source_target_pairs={{0,1},{1,0},{2,3},{3,2},{4,5},{5,4},{6,7},{7,6},{8,9},{9,8},{10,11... | collective-permute-start | bytes 6291464 | tf_op jit(solution)/shard_map/ppermute | solution.py:115
  74.4 9.2 %all-to-all-done.2 = f16[32,8,1152]{2,1,0:T(8,128)(2,1)S(1)} async-done(((f16[32,8,1152]{2,1,0:T(8,128)(2,1)}), f16[32,8,1152]{2,1,0:T(8,128)(2,1)S(1)}, u32[]{:S(2)}, u32[]{:S(2)}) %all-to-all-start.2) | async-done | bytes 589856 | tf_op jit(solution)/shard_map/all_to_all | solution.py:140
  83.6 0.1 convert.2.got
  83.7 1.2 shard_map.38
  84.8 6.6 %all-to-all-start.3 = ((bf16[16,8,2176]{2,1,0:T(8,128)(2,1)}), bf16[16,8,2176]{2,1,0:T(8,128)(2,1)S(1)}, u32[]{:S(2)}, u32[]{:S(2)}) async-start(bf16[16,8,2176]{2,1,0:T(8,128)(2,1)} %shard_map.38), calls=%async_computation.3 | async-start | bytes 1114112 | tf_op jit(solution)/shard_map/all_to_all | solution.py:144
  91.4 13.5 %all-to-all-done.3 = bf16[16,8,2176]{2,1,0:T(8,128)(2,1)S(1)} async-done(((bf16[16,8,2176]{2,1,0:T(8,128)(2,1)}), bf16[16,8,2176]{2,1,0:T(8,128)(2,1)S(1)}, u32[]{:S(2)}, u32[]{:S(2)}) %all-to-all-start.3) | async-done | bytes 557088 | tf_op jit(solution)/shard_map/all_to_all | solution.py:144
  105.0 5.7 %shard_map.39 = f32[8,2,16,1152]{3,2,1,0:T(8,128)S(1)} custom-call(s32[2]{0:T(128)S(1)} %pad_add_fusion.me, bf16[128,2176]{1,0:T(8,128)(2,1)S(1)} %bitcast.17, bf16[1024,1024]{1,0:T(8,128)(2,1)S(1)} %copy-done, bf16[1024,1024]{1,0:T(8,128)(2,1)} %collective-permute-done.1.across, bf16[1024,1024]{1,0:T(8,128)(2,1)} %collective-permute-done.2.core, ...), custom_call_target="tpu_custom_call" | custom-call | tf_op jit(solution)/shard_map/pallas_call | solution.py:105
  110.7 0.1 convert_element_type.27
  110.8 33.8 %all_to_all.39 = f16[16,16,1152]{2,1,0:T(8,128)(2,1)S(1)} all-to-all(f16[16,16,1152]{2,1,0:T(8,128)(2,1)S(1)} %bitcast.20), channel_id=1, replica_groups=mesh['zh'=4,'xh'=2,'xl'=2,'zl'=2,'y'=8,'k'=2] {'zh','xh','k'}, dimensions={0} | all-to-all | bytes 1179648 | tf_op jit(solution)/shard_map/all_to_all | solution.py:151
  144.6 0.1 bitcast_convert_fusion.got
  144.7 1.0 shard_map.40
  (8 shorter events, 0.0 us)
Async XLA Ops:
  0.0 57.5 %copy-start.1 = (bf16[1024,512]{1,0:T(8,128)(2,1)S(1)}, bf16[1024,512]{1,0:T(8,128)(2,1)}, u32[]{:S(2)}) copy-start(bf16[1024,512]{1,0:T(8,128)(2,1)} %fisher.1) | copy-start | bytes 3145732
  0.0 72.5 %collective-permute-start.1 = (bf16[1024,1024]{1,0:T(8,128)(2,1)}, bf16[1024,1024]{1,0:T(8,128)(2,1)}, u32[]{:S(2)}, u32[]{:S(2)}) collective-permute-start(bf16[1024,1024]{1,0:T(8,128)(2,1)} %own.1), channel_id=1, source_target_pairs={{0,32},{32,0},{1,33},{33,1},{2,34},{34,2},{3,35},{35,3},{4,36},{36... | collective-permute-start | bytes 6291464 | tf_op jit(solution)/shard_map/ppermute | solution.py:115
  4.1 53.4 %collective-permute-start = (bf16[1024,512]{1,0:T(8,128)(2,1)}, bf16[1024,512]{1,0:T(8,128)(2,1)S(1)}, u32[]{:S(2)}, u32[]{:S(2)}) collective-permute-start(bf16[1024,512]{1,0:T(8,128)(2,1)} %fisher.1), channel_id=1, source_target_pairs={{0,1},{1,0},{2,3},{3,2},{4,5},{5,4},{6,7},{7,6},{8,9},{9,8},{10,11... | collective-permute-start | bytes 3145736 | tf_op jit(solution)/shard_map/ppermute | solution.py:115
  25.8 31.7 %all-to-all-start.1 = ((bf16[8,64,512]{2,1,0:T(8,128)(2,1)}), bf16[8,64,512]{2,1,0:T(8,128)(2,1)S(1)}, u32[]{:S(2)}, u32[]{:S(2)}) async-start(bf16[8,64,512]{2,1,0:T(8,128)(2,1)} %bitcast.4), calls=%async_computation.1 | async-start | bytes 1048576 | tf_op jit(solution)/shard_map/all_to_all | solution.py:130
  58.9 9.9 %copy-start = (bf16[1024,1024]{1,0:T(8,128)(2,1)S(1)}, bf16[1024,1024]{1,0:T(8,128)(2,1)}, u32[]{:S(2)}) copy-start(bf16[1024,1024]{1,0:T(8,128)(2,1)} %own.1) | copy-start | bytes 6291460
  59.8 23.8 %all-to-all-start.2 = ((f16[32,8,1152]{2,1,0:T(8,128)(2,1)}), f16[32,8,1152]{2,1,0:T(8,128)(2,1)S(1)}, u32[]{:S(2)}, u32[]{:S(2)}) async-start(f16[32,8,1152]{2,1,0:T(8,128)(2,1)} %convert_bitcast_fusion), calls=%async_computation.2 | async-start | bytes 1179648 | tf_op jit(solution)/shard_map/all_to_all | solution.py:140
  68.9 22.6 %collective-permute-start.2 = (bf16[1024,1024]{1,0:T(8,128)(2,1)S(1)}, bf16[1024,1024]{1,0:T(8,128)(2,1)}, u32[]{:S(2)}, u32[]{:S(2)}) collective-permute-start(bf16[1024,1024]{1,0:T(8,128)(2,1)S(1)} %copy-done), channel_id=1, source_target_pairs={{0,1},{1,0},{2,3},{3,2},{4,5},{5,4},{6,7},{7,6},{8,9},{9,8},{10,11... | collective-permute-start | bytes 6291464 | tf_op jit(solution)/shard_map/ppermute | solution.py:115
  72.5 32.5 %collective-permute-start.3 = (bf16[1024,1024]{1,0:T(8,128)(2,1)}, bf16[1024,1024]{1,0:T(8,128)(2,1)}, u32[]{:S(2)}, u32[]{:S(2)}) collective-permute-start(bf16[1024,1024]{1,0:T(8,128)(2,1)} %collective-permute-done.1.across), channel_id=1, source_target_pairs={{0,1},{1,0},{2,3},{3,2},{4,5},{5,4},{6,7},{7,6},{8,9},{9,8},{10,11... | collective-permute-start | bytes 6291464 | tf_op jit(solution)/shard_map/ppermute | solution.py:115
  84.8 20.1 %all-to-all-start.3 = ((bf16[16,8,2176]{2,1,0:T(8,128)(2,1)}), bf16[16,8,2176]{2,1,0:T(8,128)(2,1)S(1)}, u32[]{:S(2)}, u32[]{:S(2)}) async-start(bf16[16,8,2176]{2,1,0:T(8,128)(2,1)} %shard_map.38), calls=%async_computation.3 | async-start | bytes 1114112 | tf_op jit(solution)/shard_map/all_to_all | solution.py:144

commit v3 on v2

--- a/solution.py
+++ b/solution.py
@@ -73,21 +73,30 @@
         out[copy, :, blocks * features :] = tail
 
 
-def score_kernel(me, got, own, across, core, core_across, out):
+def score_kernel(me, got, own, across, out, held, sems):
     count, features = own.shape
+    copies = [pltpu.make_async_copy(ref, held.at[i], sems.at[i]) for i, ref in enumerate((own, across))]
+    for copy in copies:
+        copy.start()
     mine = got[:, pl.ds(pl.multiple_of(me[1] * features, features), features)]
     theirs = got[:, pl.ds(pl.multiple_of((1 - me[1]) * features, features), features)]
+    copies[0].wait()
+    scores = dot_t(mine, held[0])
+    copies[1].wait()
+    scores = (scores + dot_t(theirs, held[1])) * 4.0
     tail = got[:, 2 * features :].astype(F32)
     groups, _, height, _ = out.shape
-    for k, here, there in ((me[0], own, across), (1 - me[0], core, core_across)):
-        scores = (dot_t(mine, here[...]) + dot_t(theirs, there[...])) * 4.0
-        for i in range(groups):
-            out[i, k, :, :count] = scores[i * height : (i + 1) * height]
-            out[i, k, :, count:] = tail[i * height : (i + 1) * height]
-
-
-def last_kernel(got, out):
-    wide = out.shape[1]
+    for i in range(groups):
+        out[i, 0, :, :count] = scores[i * height : (i + 1) * height]
+        out[i, 0, :, count:] = tail[i * height : (i + 1) * height]
+
+
+def rest_kernel(me, got, own, across, done, out, held, sems):
+    out[:, 1:] = done[...]
+    score_kernel(me, got, own, across, out.at[:, 0:1], held, sems)
+
+
+def combine(got, wide, factor):
     tails = [got[i, :, wide:] for i in range(got.shape[0])]
     top = tails[0][:, :1]
     for tail in tails[1:]:
@@ -95,19 +104,35 @@
     total, squares = 0.0, 0.0
     for i, tail in enumerate(tails):
         scale = jnp.exp2(tail[:, :1] - top)
-        total += got[i, :, :wide] * (scale * 0.25)
+        total += got[i, :, :wide] * (scale * factor)
         squares += (tail[:, 1:2] + tail[:, 2:3] + tail[:, 3:4]) * (scale * scale)
-    out[...] = total / jnp.sqrt(squares + 1e-06 * jnp.exp2(-2.0 * jnp.maximum(top, -60.0)))
-
-
-def call(kernel, shape, dtype, *args):
-    spaces = [SMEM if arg.dtype == jnp.int32 else VMEM for arg in args]
+    return total, squares, top
+
+
+def middle_kernel(got, out):
+    wide = got.shape[2] - LANES
+    total, squares, top = combine(got, wide, 0.5)
+    out[:, :wide] = total
+    out[:, wide:] = columns(total.shape[0], top, *pieces(squares))
+
+
+def last_kernel(me, got, out):
+    total, squares, top = combine(got, out.shape[2], 0.5)
+    total = total / jnp.sqrt(squares + 1e-06 * jnp.exp2(-2.0 * jnp.maximum(top, -60.0)))
+    height = out.shape[1]
+    out[1 - me[0]] = total[:height]
+    out[me[0]] = total[height:]
+
+
+def call(kernel, shape, dtype, *args, spaces=None, **kwargs):
+    spaces = spaces or [SMEM if arg.dtype == jnp.int32 else VMEM for arg in args]
     return pl.pallas_call(
         kernel,
         out_shape=jax.ShapeDtypeStruct(shape, dtype),
         in_specs=[pl.BlockSpec(memory_space=space) for space in spaces],
         out_specs=pl.BlockSpec(memory_space=VMEM),
         compiler_params=pltpu.CompilerParams(vmem_limit_bytes=24 << 20),
+        **kwargs,
     )(*args)
 
 
@@ -129,27 +154,35 @@
     copies = jnp.broadcast_to(held.transpose(1, 0, 2, 3)[None], (x, k, zh, height, width)).reshape(-1, width)
     held = lax.all_to_all(copies, ("xh", "xl", "k"), 0, 0, tiled=True).reshape(x, k, zh * height, width)
 
-    index_across = swap(index, "xl")
-    index_core = swap(index, "k")
-    index_core_across = swap(index_across, "k")
-
-    order = tuple((h * xl + i) * zh + z for i in range(xl) for z in range(zh) for h in range(xh))
+    order = tuple((h * xl + i) * zh + z for i in range(xl) for h in range(xh) for z in range(zh))
     sent = call(
         functools.partial(first_kernel, order, height), (batch, features + LANES), F32, me, held, fisher, fisher_core
     )
+    index_across = swap(index, "xl")
     got = lax.all_to_all(sent.astype(F16), ("xl", "zl", "y"), 0, 0, tiled=True).astype(F32)
     got = got.reshape(xl, pairs, -1, features + LANES)
 
     sent = call(unit_kernel, (pairs, got.shape[2], xl * features + LANES), BF16, got)
     got = lax.all_to_all(sent.reshape(batch // xl, -1), ("zl", "y"), 0, 0, tiled=True)
 
-    sent = call(
-        score_kernel, (zh * xh, k, height, count + LANES), F32,
-        me, got, index, index_across, index_core, index_core_across,
+    blocks = zh * xh
+    spaces = (SMEM, VMEM) + (pl.ANY,) * 2
+    scratch = [VMEM((2, count, features), BF16), pltpu.SemaphoreType.DMA((2,))]
+    cost = pl.CostEstimate(
+        flops=4 * blocks * height * count * features, bytes_accessed=4 * count * features, transcendentals=0
     )
+    more = dict(scratch_shapes=scratch, cost_estimate=cost)
+    others = swap(got, "k")
+    shape = (blocks, 1, height, count + LANES)
+    done = call(score_kernel, shape, F32, me, got, index, index_across, spaces=spaces, **more)
+    shape = (blocks, k, height, count + LANES)
+    sent = call(rest_kernel, shape, F32, me, others, index, index_across, done, spaces=spaces + (VMEM,), **more)
     sent = sent.reshape(batch, -1)
-    got = lax.all_to_all(sent.astype(F16), ("zh", "xh", "k"), 0, 0, tiled=True).astype(F32)
-    return call(last_kernel, (k * height, count), F32, got.reshape(zh * xh, k * height, -1))
+    got = lax.all_to_all(sent.astype(F16), "xh", 0, 0, tiled=True).astype(F32).reshape(xh, zh * k * height, -1)
+
+    sent = call(middle_kernel, got.shape[1:], F32, got)
+    got = lax.all_to_all(sent.astype(F16), "zh", 0, 0, tiled=True).astype(F32).reshape(zh, k * height, -1)
+    return call(last_kernel, (k, height, count), F32, me, got).reshape(k * height, count)
 
 
 def fine_mesh(mesh):

time: 146 us -> 138 us (0.945)
  the two profiles are of different devices: /device:TPU:1 before, /device:TPU:56 now
where the time goes in v3:
time: 138 us
  blocking collectives  68 us (49%)
  waiting for transfers between devices  36.6 us (27%)
  starting transfers between devices  19 us (14%)
  Pallas kernels  11.1 us (8%)
  local copies, waits for them, and re-layouts  1.65 us (1%)
    all_to_all x1, blocking collectives, local(): lax.all_to_all(sent.reshape(batch // xl, -1), ('zl', 'y'), 0, 0, tiled=True)  22 us
    all_to_all x1, blocking collectives, local(): lax.all_to_all(copies, 'zh', 0, 0, tiled=True).reshape(zh, k, height, width)  19.4 us
    ppermute x3, waiting for transfers between devices, swap(): return lax.ppermute(array, axis, [(0, 1), (1, 0)])  14.3 us
    all_to_all x1, blocking collectives, local(): lax.all_to_all(sent.astype(F16), 'zh', 0, 0, tiled=True).astype(F32)  13.7 us
    all_to_all x1, blocking collectives, local(): lax.all_to_all(sent.astype(F16), 'xh', 0, 0, tiled=True).astype(F32)  12.9 us
    all_to_all x1, waiting for transfers between devices, local(): lax.all_to_all(sent.astype(F16), ('xl', 'zl', 'y'), 0, 0, tiled=True)  12 us
    pallas_call x6, Pallas kernels, call(): pl.pallas_call(kernel, out_shape=jax.ShapeDtypeStruct(shape, dtype), in_s...  11.1 us
    all_to_all x1, waiting for transfers between devices, local(): lax.all_to_all(copies, ('xh', 'xl', 'k'), 0, 0, tiled=True)  10.2 us
  transfers between devices with their start and end apart: 5, of which 3 were waited for; matrix products, arithmetic and copies ran while one was open for 1% of the time, Pallas kernels for 3%

profile of v3, /device:TPU:56, one launch (start us, length us, event | category | flops | bytes accessed | tf_op | source)
XLA Modules:
  0.0 137.8 jit_solution(6176349828832097150)
XLA Ops:
  0.0 2.0 %collective-permute-start = (bf16[1024,512]{1,0:T(8,128)(2,1)}, bf16[1024,512]{1,0:T(8,128)(2,1)S(1)}, u32[]{:S(2)}, u32[]{:S(2)}) collective-permute-start(bf16[1024,512]{1,0:T(8,128)(2,1)} %fisher.1), channel_id=1, source_target_pairs={{0,1},{1,0},{2,3},{3,2},{4,5},{5,4},{6,7},{7,6},{8,9},{9,8},{10,11... | collective-permute-start | bytes 3145736 | tf_op jit(solution)/shard_map/ppermute | solution.py:140
  2.0 0.8 broadcast_in_dim.4
  2.8 19.4 %all_to_all.47 = bf16[4,32,512]{2,1,0:T(8,128)(2,1)S(1)} all-to-all(bf16[4,32,512]{2,1,0:T(8,128)(2,1)S(1)} %broadcast_in_dim.4), channel_id=1, replica_groups=mesh['zh'=4,'xh'=2,'xl'=2,'zl'=2,'y'=8,'k'=2] {'zh'}, dimensions={0} | all-to-all | bytes 262144 | tf_op jit(solution)/shard_map/all_to_all | solution.py:152
  22.3 0.9 broadcast_in_dim.5
  23.1 4.3 %all-to-all-start.1 = ((bf16[8,64,512]{2,1,0:T(8,128)(2,1)}), bf16[8,64,512]{2,1,0:T(8,128)(2,1)S(1)}, u32[]{:S(2)}, u32[]{:S(2)}) async-start(bf16[8,64,512]{2,1,0:T(8,128)(2,1)} %bitcast.4), calls=%async_computation.1 | async-start | bytes 1048576 | tf_op jit(solution)/shard_map/all_to_all | solution.py:155
  27.5 0.1 pad_add_fusion.me
  27.5 10.2 %all-to-all-done.1 = bf16[8,64,512]{2,1,0:T(8,128)(2,1)S(1)} async-done(((bf16[8,64,512]{2,1,0:T(8,128)(2,1)}), bf16[8,64,512]{2,1,0:T(8,128)(2,1)S(1)}, u32[]{:S(2)}, u32[]{:S(2)}) %all-to-all-start.1) | async-done | bytes 524320 | tf_op jit(solution)/shard_map/all_to_all | solution.py:155
  37.8 1.4 %shard_map.37 = f32[256,1152]{1,0:T(8,128)S(1)} custom-call(s32[2]{0:T(128)S(1)} %pad_add_fusion.me, bf16[4,2,64,512]{3,2,1,0:T(8,128)(2,1)S(1)} %bitcast.17, bf16[1024,512]{1,0:T(8,128)(2,1)S(1)} %copy-done.1, bf16[1024,512]{1,0:T(8,128)(2,1)S(1)} %collective-permute-done.other), custom_call_target="tpu_custom_call" | custom-call | tf_op jit(solution)/shard_map/pallas_call | solution.py:129
  39.2 0.9 convert_bitcast_fusion
  40.1 7.4 %all-to-all-start.2 = ((f16[32,8,1152]{2,1,0:T(8,128)(2,1)}), f16[32,8,1152]{2,1,0:T(8,128)(2,1)S(1)}, u32[]{:S(2)}, u32[]{:S(2)}) async-start(f16[32,8,1152]{2,1,0:T(8,128)(2,1)} %convert_bitcast_fusion), calls=%async_computation.2 | async-start | bytes 1179648 | tf_op jit(solution)/shard_map/all_to_all | solution.py:162
  47.5 3.4 %collective-permute-start.2 = (bf16[1024,1024]{1,0:T(8,128)(2,1)S(1)}, bf16[1024,1024]{1,0:T(8,128)(2,1)}, u32[]{:S(2)}, u32[]{:S(2)}) collective-permute-start(bf16[1024,1024]{1,0:T(8,128)(2,1)S(1)} %copy-done), channel_id=1, source_target_pairs={{0,32},{32,0},{1,33},{33,1},{2,34},{34,2},{3,35},{35,3},{4,36},{36... | collective-permute-start | bytes 6291464 | tf_op jit(solution)/shard_map/ppermute | solution.py:140
  50.9 12.0 %all-to-all-done.2 = f16[32,8,1152]{2,1,0:T(8,128)(2,1)S(1)} async-done(((f16[32,8,1152]{2,1,0:T(8,128)(2,1)}), f16[32,8,1152]{2,1,0:T(8,128)(2,1)S(1)}, u32[]{:S(2)}, u32[]{:S(2)}) %all-to-all-start.2) | async-done | bytes 589856 | tf_op jit(solution)/shard_map/all_to_all | solution.py:162
  62.9 0.1 convert.1.got
  63.0 0.3 shard_map.38
  63.3 22.0 %all_to_all.48 = bf16[16,8,2176]{2,1,0:T(8,128)(2,1)S(1)} all-to-all(bf16[16,8,2176]{2,1,0:T(8,128)(2,1)S(1)} %shard_map.38), channel_id=1, replica_groups=mesh['zh'=4,'xh'=2,'xl'=2,'zl'=2,'y'=8,'k'=2] {'zl','y'}, dimensions={0} | all-to-all | bytes 1114112 | tf_op jit(solution)/shard_map/all_to_all | solution.py:166
  85.3 1.9 %collective-permute-start.1 = (bf16[128,2176]{1,0:T(8,128)(2,1)S(1)}, bf16[128,2176]{1,0:T(8,128)(2,1)S(1)}, u32[]{:S(2)}, u32[]{:S(2)}) collective-permute-start(bf16[128,2176]{1,0:T(8,128)(2,1)S(1)} %bitcast.15), channel_id=1, source_target_pairs={{0,1},{1,0},{2,3},{3,2},{4,5},{5,4},{6,7},{7,6},{8,9},{9,8},{10,11... | collective-permute-start | bytes 1671176 | tf_op jit(solution)/shard_map/ppermute | solution.py:140
  87.2 14.3 %collective-permute-done.2.across = bf16[1024,1024]{1,0:T(8,128)(2,1)} collective-permute-done((bf16[1024,1024]{1,0:T(8,128)(2,1)S(1)}, bf16[1024,1024]{1,0:T(8,128)(2,1)}, u32[]{:S(2)}, u32[]{:S(2)}) %collective-permute-start.2) | collective-permute-done | bytes 2097184 | tf_op jit(solution)/shard_map/ppermute | solution.py:140
  101.5 3.8 %shard_map.39.done = f32[8,1,16,1152]{3,2,1,0:T(8,128)S(1)} custom-call(s32[2]{0:T(128)S(1)} %pad_add_fusion.me, bf16[128,2176]{1,0:T(8,128)(2,1)S(1)} %bitcast.16, bf16[1024,1024]{1,0:T(8,128)(2,1)S(1)} %copy-done, bf16[1024,1024]{1,0:T(8,128)(2,1)} %collective-permute-done.2.across), custom_call_target="tpu_custom_call" | custom-call | flops 536870912 | bytes 4194304 | tf_op jit(solution)/shard_map/pallas_call | solution.py:129
  105.3 3.8 %shard_map.40 = f32[8,2,16,1152]{3,2,1,0:T(8,128)S(1)} custom-call(s32[2]{0:T(128)S(1)} %pad_add_fusion.me, bf16[128,2176]{1,0:T(8,128)(2,1)S(1)} %collective-permute-done.1.got, bf16[1024,1024]{1,0:T(8,128)(2,1)S(1)} %copy-done, bf16[1024,1024]{1,0:T(8,128)(2,1)} %collective-permute-done.2.across, f32[8,1,16,1152]{3,2,1,0:T(8,128)S(1)} %shard_map.39.done), custom_call_target="tpu_custom_call" | custom-call | flops 536870912 | bytes 4194304 | tf_op jit(solution)/shard_map/pallas_call | solution.py:129
  109.2 12.9 %all_to_all.49 = f16[2,128,1152]{2,1,0:T(8,128)(2,1)S(1)} all-to-all(f16[2,128,1152]{2,1,0:T(8,128)(2,1)S(1)} %bitcast.19), channel_id=1, replica_groups=mesh['zh'=4,'xh'=2,'xl'=2,'zl'=2,'y'=8,'k'=2] {'xh'}, dimensions={0} | all-to-all | bytes 1179648 | tf_op jit(solution)/shard_map/all_to_all | solution.py:181
  122.1 0.1 convert_element_type.33.got
  122.2 0.3 shard_map.41
  122.6 13.7 %all_to_all.50 = f16[4,32,1152]{2,1,0:T(8,128)(2,1)S(1)} all-to-all(f16[4,32,1152]{2,1,0:T(8,128)(2,1)S(1)} %bitcast.20), channel_id=1, replica_groups=mesh['zh'=4,'xh'=2,'xl'=2,'zl'=2,'y'=8,'k'=2] {'zh'}, dimensions={0} | all-to-all | bytes 589824 | tf_op jit(solution)/shard_map/all_to_all | solution.py:184
  136.3 1.4 %shard_map.42 = f32[2,16,1024]{2,1,0:T(8,128)} custom-call(s32[2]{0:T(128)S(1)} %pad_add_fusion.me, f32[4,32,1152]{2,1,0:T(8,128)S(1)} %convert_element_type.35.got), custom_call_target="tpu_custom_call" | custom-call | tf_op jit(solution)/shard_map/pallas_call | solution.py:129
  (10 shorter events, 0.2 us)
Async XLA Ops:
  0.0 37.8 %copy-start.1 = (bf16[1024,512]{1,0:T(8,128)(2,1)S(1)}, bf16[1024,512]{1,0:T(8,128)(2,1)}, u32[]{:S(2)}) copy-start(bf16[1024,512]{1,0:T(8,128)(2,1)} %fisher.1) | copy-start | bytes 3145732
  0.0 37.8 %collective-permute-start = (bf16[1024,512]{1,0:T(8,128)(2,1)}, bf16[1024,512]{1,0:T(8,128)(2,1)S(1)}, u32[]{:S(2)}, u32[]{:S(2)}) collective-permute-start(bf16[1024,512]{1,0:T(8,128)(2,1)} %fisher.1), channel_id=1, source_target_pairs={{0,1},{1,0},{2,3},{3,2},{4,5},{5,4},{6,7},{7,6},{8,9},{9,8},{10,11... | collective-permute-start | bytes 3145736 | tf_op jit(solution)/shard_map/ppermute | solution.py:140
  23.1 14.6 %all-to-all-start.1 = ((bf16[8,64,512]{2,1,0:T(8,128)(2,1)}), bf16[8,64,512]{2,1,0:T(8,128)(2,1)S(1)}, u32[]{:S(2)}, u32[]{:S(2)}) async-start(bf16[8,64,512]{2,1,0:T(8,128)(2,1)} %bitcast.4), calls=%async_computation.1 | async-start | bytes 1048576 | tf_op jit(solution)/shard_map/all_to_all | solution.py:155
  39.2 8.3 %copy-start = (bf16[1024,1024]{1,0:T(8,128)(2,1)S(1)}, bf16[1024,1024]{1,0:T(8,128)(2,1)}, u32[]{:S(2)}) copy-start(bf16[1024,1024]{1,0:T(8,128)(2,1)} %own.3) | copy-start | bytes 6291460
  40.1 22.8 %all-to-all-start.2 = ((f16[32,8,1152]{2,1,0:T(8,128)(2,1)}), f16[32,8,1152]{2,1,0:T(8,128)(2,1)S(1)}, u32[]{:S(2)}, u32[]{:S(2)}) async-start(f16[32,8,1152]{2,1,0:T(8,128)(2,1)} %convert_bitcast_fusion), calls=%async_computation.2 | async-start | bytes 1179648 | tf_op jit(solution)/shard_map/all_to_all | solution.py:162
  47.5 54.0 %collective-permute-start.2 = (bf16[1024,1024]{1,0:T(8,128)(2,1)S(1)}, bf16[1024,1024]{1,0:T(8,128)(2,1)}, u32[]{:S(2)}, u32[]{:S(2)}) collective-permute-start(bf16[1024,1024]{1,0:T(8,128)(2,1)S(1)} %copy-done), channel_id=1, source_target_pairs={{0,32},{32,0},{1,33},{33,1},{2,34},{34,2},{3,35},{35,3},{4,36},{36... | collective-permute-start | bytes 6291464 | tf_op jit(solution)/shard_map/ppermute | solution.py:140
  85.3 20.0 %collective-permute-start.1 = (bf16[128,2176]{1,0:T(8,128)(2,1)S(1)}, bf16[128,2176]{1,0:T(8,128)(2,1)S(1)}, u32[]{:S(2)}, u32[]{:S(2)}) collective-permute-start(bf16[128,2176]{1,0:T(8,128)(2,1)S(1)} %bitcast.15), channel_id=1, source_target_pairs={{0,1},{1,0},{2,3},{3,2},{4,5},{5,4},{6,7},{7,6},{8,9},{9,8},{10,11... | collective-permute-start | bytes 1671176 | tf_op jit(solution)/shard_map/ppermute | solution.py:140

commit v4 on v1

--- a/solution.py
+++ b/solution.py
@@ -71,15 +71,14 @@
         out[copy, :, features:] = tail
 
 
-def score_kernel(got, index, other, out, held, sems):
+def score_kernel(got, index, other, out, held, sem):
     count, features = index.shape
-    copies = [pltpu.make_async_copy(ref, held.at[i], sems.at[i]) for i, ref in enumerate((index, other))]
-    for copy in copies:
-        copy.start()
+    copy = pltpu.make_async_copy(other, held, sem)
+    copy.start()
     out[:, 2 * count :] = got[:, features:].astype(F32)
-    for i, copy in enumerate(copies):
-        copy.wait()
-        out[:, i * count : (i + 1) * count] = dot_t(got[:, :features], held[i]) * 8.0
+    out[:, :count] = dot_t(got[:, :features], index[...]) * 8.0
+    copy.wait()
+    out[:, count : 2 * count] = dot_t(got[:, :features], held[...]) * 8.0
 
 
 def combine(got, wide, factor):
@@ -143,22 +142,24 @@
     batch = rows * height
 
     copies = jnp.broadcast_to(query[None], (rows,) + query.shape).reshape(-1, width)
-    held = lax.all_to_all(copies, (*ROW, "k"), 0, 0, tiled=True).reshape(rows, k, height, width)
+    held = lax.all_to_all(copies, (*ROW, "k"), 0, 0, tiled=True)
+    held = held.reshape(rows, k, height, width)
 
     order = tuple(z * x + i for i in range(x) for z in range(zh))
     sent = call(
         functools.partial(first_kernel, order), (SMEM, VMEM, VMEM, VMEM), (batch, features + LANES), F32,
         me, held, fisher, fisher_other,
     )
-    got = lax.all_to_all(sent.astype(F16), PAIR, 0, 0, tiled=True).astype(F32)
-    got = got.reshape(pairs, -1, features + LANES)
+    sent = sent.astype(F16)
+    got = lax.all_to_all(sent, PAIR, 0, 0, tiled=True)
+    got = got.astype(F32).reshape(pairs, -1, features + LANES)
 
     sent = call(unit_kernel, (VMEM,), got.shape, BF16, got)
     got = lax.all_to_all(sent.reshape(batch, -1), PAIR, 0, 0, tiled=True)
 
     sent = call(
-        score_kernel, (VMEM, pl.ANY, pl.ANY), (batch, 2 * count + LANES), F32, got, index, index_other,
-        scratch_shapes=[VMEM((2, count, features), BF16), pltpu.SemaphoreType.DMA((2,))],
+        score_kernel, (VMEM, VMEM, pl.ANY), (batch, 2 * count + LANES), F32, got, index, index_other,
+        scratch_shapes=[VMEM((count, features), BF16), pltpu.SemaphoreType.DMA],
     )
     got = lax.all_to_all(sent.astype(F16), "x", 0, 0, tiled=True).astype(F32)
     got = got.reshape(x, zh * height, -1)

time: 124 us -> 123 us (level)
  no operation moved by 1% of the time
where the time goes in v4:
time: 123 us; the launch traced here: 122 us
  waiting for transfers between devices  45.5 us (37%)
  starting transfers between devices  34.4 us (28%)
  blocking collectives  33.8 us (27%)
  Pallas kernels  5.62 us (5%)
  local copies, waits for them, and re-layouts  1.62 us (1%)
  other arithmetic  1.3 us (1%)
    all_to_all x1, blocking collectives, local(): lax.all_to_all(sent.astype(F16), ('zh', 'k'), 0, 0, tiled=True).astype(F32)  17.2 us
    all_to_all x1, waiting for transfers between devices, local(): held = lax.all_to_all(copies, (*ROW, 'k'), 0, 0, tiled=True)  16.9 us
    all_to_all x1, blocking collectives, local(): got = lax.all_to_all(sent.astype(F16), 'x', 0, 0, tiled=True).astype(F32)  16.5 us
    all_to_all x1, waiting for transfers between devices, local(): got = lax.all_to_all(sent.reshape(batch, -1), PAIR, 0, 0, tiled=True)  15.6 us
    all_to_all x1, waiting for transfers between devices, local(): got = lax.all_to_all(sent, PAIR, 0, 0, tiled=True)  13 us
    ppermute x2, starting transfers between devices, swap(): return lax.ppermute(array, 'k', [(0, 1), (1, 0)])  11.6 us
    all_to_all x1, starting transfers between devices, local(): got = lax.all_to_all(sent, PAIR, 0, 0, tiled=True)  9.17 us
    all_to_all x1, starting transfers between devices, local(): held = lax.all_to_all(copies, (*ROW, 'k'), 0, 0, tiled=True)  7.69 us
  transfers between devices with their start and end apart: 5, of which 3 were waited for; matrix products, arithmetic and copies ran while one was open for 1% of the time, Pallas kernels for 1%

profile of v4, /device:TPU:1, one launch (start us, length us, event | category | flops | bytes accessed | tf_op | source)
XLA Modules:
  0.0 122.3 jit_solution(5644379901499523816)
XLA Ops:
  0.0 8.9 %collective-permute-start = (bf16[1024,512]{1,0:T(8,128)(2,1)}, bf16[1024,512]{1,0:T(8,128)(2,1)S(1)}, u32[]{:S(2)}, u32[]{:S(2)}) collective-permute-start(bf16[1024,512]{1,0:T(8,128)(2,1)} %fisher.1), channel_id=1, source_target_pairs={{0,1},{1,0},{2,3},{3,2},{4,5},{5,4},{6,7},{7,6},{8,9},{9,8},{10,11... | collective-permute-start | bytes 3145736 | tf_op jit(solution)/shard_map/ppermute | solution.py:131
  8.9 1.6 %broadcast_in_dim.2 = bf16[16,32,512]{2,1,0:T(8,128)(2,1)} broadcast(bf16[32,512]{1,0:T(8,128)(2,1)} %param.3), dimensions={1,2} | broadcast | bytes 557056 | tf_op jit(solution)/shard_map/broadcast_in_dim | solution.py:144
  10.5 7.7 %all-to-all-start = ((bf16[32,16,512]{2,1,0:T(8,128)(2,1)}), bf16[32,16,512]{2,1,0:T(8,128)(2,1)S(1)}, u32[]{:S(2)}, u32[]{:S(2)}) async-start(bf16[32,16,512]{2,1,0:T(8,128)(2,1)} %bitcast.1), calls=%async_computation | async-start | bytes 1048576 | tf_op jit(solution)/shard_map/all_to_all | solution.py:145
  18.2 16.9 %all-to-all-done = bf16[32,16,512]{2,1,0:T(8,128)(2,1)S(1)} async-done(((bf16[32,16,512]{2,1,0:T(8,128)(2,1)}), bf16[32,16,512]{2,1,0:T(8,128)(2,1)S(1)}, u32[]{:S(2)}, u32[]{:S(2)}) %all-to-all-start) | async-done | bytes 524320 | tf_op jit(solution)/shard_map/all_to_all | solution.py:145
  35.0 0.0 collective-permute-done.other
  35.0 0.8 shard_map.37
  35.9 0.0 copy-start
  35.9 0.9 convert_element_type.28
  36.8 9.2 %all-to-all-start.1 = ((f16[16,16,1152]{2,1,0:T(8,128)(2,1)}), f16[16,16,1152]{2,1,0:T(8,128)(2,1)S(1)}, u32[]{:S(2)}, u32[]{:S(2)}) async-start(f16[16,16,1152]{2,1,0:T(8,128)(2,1)} %bitcast.3), calls=%async_computation.1 | async-start | bytes 1179648 | tf_op jit(solution)/shard_map/all_to_all | solution.py:154
  46.0 0.0 copy-done
  46.0 2.7 %collective-permute-start.1 = (bf16[1024,1024]{1,0:T(8,128)(2,1)S(1)}, bf16[1024,1024]{1,0:T(8,128)(2,1)}, u32[]{:S(2)}, u32[]{:S(2)}) collective-permute-start(bf16[1024,1024]{1,0:T(8,128)(2,1)S(1)} %copy-done), channel_id=1, source_target_pairs={{0,1},{1,0},{2,3},{3,2},{4,5},{5,4},{6,7},{7,6},{8,9},{9,8},{10,11... | collective-permute-start | bytes 6291464 | tf_op jit(solution)/shard_map/ppermute | solution.py:131
  48.7 13.0 %all-to-all-done.1 = f16[16,16,1152]{2,1,0:T(8,128)(2,1)S(1)} async-done(((f16[16,16,1152]{2,1,0:T(8,128)(2,1)}), f16[16,16,1152]{2,1,0:T(8,128)(2,1)S(1)}, u32[]{:S(2)}, u32[]{:S(2)}) %all-to-all-start.1) | async-done | bytes 589856 | tf_op jit(solution)/shard_map/all_to_all | solution.py:154
  61.7 0.1 convert_element_type.29.got
  61.8 1.2 shard_map.38
  62.9 5.9 %all-to-all-start.2 = ((bf16[16,16,1152]{2,1,0:T(8,128)(2,1)}), bf16[16,16,1152]{2,1,0:T(8,128)(2,1)S(1)}, u32[]{:S(2)}, u32[]{:S(2)}) async-start(bf16[16,16,1152]{2,1,0:T(8,128)(2,1)} %shard_map.38), calls=%async_computation.2 | async-start | bytes 1179648 | tf_op jit(solution)/shard_map/all_to_all | solution.py:158
  68.9 0.0 collective-permute-done.1.other
  68.9 15.6 %all-to-all-done.2 = bf16[16,16,1152]{2,1,0:T(8,128)(2,1)S(1)} async-done(((bf16[16,16,1152]{2,1,0:T(8,128)(2,1)}), bf16[16,16,1152]{2,1,0:T(8,128)(2,1)S(1)}, u32[]{:S(2)}, u32[]{:S(2)}) %all-to-all-start.2) | async-done | bytes 589856 | tf_op jit(solution)/shard_map/all_to_all | solution.py:158
  84.5 2.3 %shard_map.39 = f32[256,2176]{1,0:T(8,128)S(1)} custom-call(bf16[256,1152]{1,0:T(8,128)(2,1)S(1)} %bitcast.11, bf16[1024,1024]{1,0:T(8,128)(2,1)S(1)} %copy-done, bf16[1024,1024]{1,0:T(8,128)(2,1)} %collective-permute-done.1.other), custom_call_target="tpu_custom_call" | custom-call | tf_op jit(solution)/shard_map/pallas_call | solution.py:120
  86.9 0.1 convert_element_type.30
  87.0 16.5 %all_to_all.41 = f16[4,64,2176]{2,1,0:T(8,128)(2,1)S(1)} all-to-all(f16[4,64,2176]{2,1,0:T(8,128)(2,1)S(1)} %bitcast.13), channel_id=1, replica_groups=mesh['zh'=4,'x'=4,'zl'=2,'y'=8,'k'=2] {'x'}, dimensions={0} | all-to-all | bytes 2228224 | tf_op jit(solution)/shard_map/all_to_all | solution.py:164
  103.5 0.1 convert_element_type.31.got
  103.6 0.4 shard_map.40
  104.1 17.2 %all_to_all.42 = f16[8,16,1152]{2,1,0:T(8,128)(2,1)S(1)} all-to-all(f16[8,16,1152]{2,1,0:T(8,128)(2,1)S(1)} %bitcast.14), channel_id=1, replica_groups=mesh['zh'=4,'x'=4,'zl'=2,'y'=8,'k'=2] {'zh','k'}, dimensions={0} | all-to-all | bytes 589824 | tf_op jit(solution)/shard_map/all_to_all | solution.py:169
  121.4 0.9 shard_map.41
  (4 shorter events, 0.1 us)
Async XLA Ops:
  0.0 35.0 %copy-start.1 = (bf16[1024,512]{1,0:T(8,128)(2,1)S(1)}, bf16[1024,512]{1,0:T(8,128)(2,1)}, u32[]{:S(2)}) copy-start(bf16[1024,512]{1,0:T(8,128)(2,1)} %fisher.1) | copy-start | bytes 3145732
  0.0 35.0 %collective-permute-start = (bf16[1024,512]{1,0:T(8,128)(2,1)}, bf16[1024,512]{1,0:T(8,128)(2,1)S(1)}, u32[]{:S(2)}, u32[]{:S(2)}) collective-permute-start(bf16[1024,512]{1,0:T(8,128)(2,1)} %fisher.1), channel_id=1, source_target_pairs={{0,1},{1,0},{2,3},{3,2},{4,5},{5,4},{6,7},{7,6},{8,9},{9,8},{10,11... | collective-permute-start | bytes 3145736 | tf_op jit(solution)/shard_map/ppermute | solution.py:131
  10.5 24.6 %all-to-all-start = ((bf16[32,16,512]{2,1,0:T(8,128)(2,1)}), bf16[32,16,512]{2,1,0:T(8,128)(2,1)S(1)}, u32[]{:S(2)}, u32[]{:S(2)}) async-start(bf16[32,16,512]{2,1,0:T(8,128)(2,1)} %bitcast.1), calls=%async_computation | async-start | bytes 1048576 | tf_op jit(solution)/shard_map/all_to_all | solution.py:145
  35.9 10.1 %copy-start = (bf16[1024,1024]{1,0:T(8,128)(2,1)S(1)}, bf16[1024,1024]{1,0:T(8,128)(2,1)}, u32[]{:S(2)}) copy-start(bf16[1024,1024]{1,0:T(8,128)(2,1)} %index.1) | copy-start | bytes 6291460
  36.8 24.9 %all-to-all-start.1 = ((f16[16,16,1152]{2,1,0:T(8,128)(2,1)}), f16[16,16,1152]{2,1,0:T(8,128)(2,1)S(1)}, u32[]{:S(2)}, u32[]{:S(2)}) async-start(f16[16,16,1152]{2,1,0:T(8,128)(2,1)} %bitcast.3), calls=%async_computation.1 | async-start | bytes 1179648 | tf_op jit(solution)/shard_map/all_to_all | solution.py:154
  46.0 22.9 %collective-permute-start.1 = (bf16[1024,1024]{1,0:T(8,128)(2,1)S(1)}, bf16[1024,1024]{1,0:T(8,128)(2,1)}, u32[]{:S(2)}, u32[]{:S(2)}) collective-permute-start(bf16[1024,1024]{1,0:T(8,128)(2,1)S(1)} %copy-done), channel_id=1, source_target_pairs={{0,1},{1,0},{2,3},{3,2},{4,5},{5,4},{6,7},{7,6},{8,9},{9,8},{10,11... | collective-permute-start | bytes 6291464 | tf_op jit(solution)/shard_map/ppermute | solution.py:131
  62.9 21.6 %all-to-all-start.2 = ((bf16[16,16,1152]{2,1,0:T(8,128)(2,1)}), bf16[16,16,1152]{2,1,0:T(8,128)(2,1)S(1)}, u32[]{:S(2)}, u32[]{:S(2)}) async-start(bf16[16,16,1152]{2,1,0:T(8,128)(2,1)} %shard_map.38), calls=%async_computation.2 | async-start | bytes 1179648 | tf_op jit(solution)/shard_map/all_to_all | solution.py:158

commit v5 on v4

v5 whole, which is shorter than its diff:
```python
import functools

import jax
import jax.numpy as jnp
from jax import lax
from jax.experimental import pallas as pl
from jax.experimental.pallas import tpu as pltpu
from jax.sharding import Mesh, PartitionSpec as P

F32, F16, BF16 = jnp.float32, jnp.float16, jnp.bfloat16
AXES = ("zh", "x", "zl", "y", "k")
ROW = ("zh", "x")
PAIR = ("zl", "y")
LANES = 128
TAIL = 8
VMEM, SMEM = pltpu.VMEM, pltpu.SMEM


def exponent(rows):
    top = jnp.max(jnp.abs(rows), axis=-1, keepdims=True)
    return jnp.clip(jnp.ceil(jnp.log2(jnp.maximum(top, 1e-30))), -100.0, 100.0)


def diagonal(height):
    return lax.broadcasted_iota(jnp.int32, (height, LANES), 0) == lax.broadcasted_iota(jnp.int32, (height, LANES), 1)


def across(*columns):
    here = diagonal(columns[0].shape[0])
    row = lax.broadcasted_iota(jnp.int32, (TAIL, LANES), 0)
    out = jnp.zeros((TAIL, LANES), F32)
    for place, column in enumerate(columns):
        out = jnp.where(row == place, jnp.sum(jnp.where(here, column, 0.0), axis=0, keepdims=True), out)
    return out


def down(row, height):
    return jnp.sum(jnp.where(diagonal(height), row, 0.0), axis=1, keepdims=True)


def pieces(value):
    out = []
    for _ in range(3):
        out.append(value.astype(BF16).astype(F32))
        value = value - out[-1]
    return out


def dot_t(a, b):
    return lax.dot_general(a, b, (((1,), (1,)), ((), ())), preferred_element_type=F32)


def copy_kernel(query, out):
    for i in range(out.shape[0]):
        out[i] = query[...]


def first_kernel(order, me, held, fisher, other, out):
    core = me[0]
    groups, _, height, width = held.shape
    mine = held[:, core].reshape(groups * height, width)
    theirs = held[:, 1 - core].reshape(groups * height, width)
    part = dot_t(mine, fisher[...]) + dot_t(theirs, other[...])
    tiles = part.shape[1] // LANES
    e = exponent(part)
    part = part * jnp.exp2(12.0 - e)
    for to, source in enumerate(order):
        rows = slice(source * height, (source + 1) * height)
        for c in range(tiles):
            out[to, c * height : (c + 1) * height] = part[rows, c * LANES : (c + 1) * LANES]
        out[to, tiles * height :] = across(e[rows])


def unit_kernel(height, got, out):
    tiles = (out.shape[1] - TAIL) // height
    full = [jnp.zeros((height, LANES), F32)] * tiles
    for i in range(got.shape[0]):
        scale = jnp.exp2(down(got[i, tiles * height : tiles * height + 1], height) - 12.0)
        full = [full[c] + got[i, c * height : (c + 1) * height] * scale for c in range(tiles)]
    full = jnp.concatenate(full, axis=1)
    g = exponent(full)
    unit = full * jnp.exp2(-g)
    squares = jnp.sum(unit * unit, axis=-1, keepdims=True)
    unit = unit.astype(BF16)
    tail = across(g, *pieces(squares)).astype(BF16)
    for copy in range(out.shape[0]):
        for c in range(tiles):
            out[copy, c * height : (c + 1) * height] = unit[:, c * LANES : (c + 1) * LANES]
        out[copy, tiles * height :] = tail


def score_kernel(height, got, index, other, out, held, sem):
    count, features = index.shape
    copy = pltpu.make_async_copy(other, held, sem)
    copy.start()
    sources, tiles = got.shape[0], features // LANES
    unit = jnp.concatenate(
        [got[:, c * height : (c + 1) * height].reshape(sources * height, LANES) for c in range(tiles)], axis=1
    )
    tails = got[:, tiles * height :].astype(F32)
    chunks = out.shape[0]
    per = sources // chunks
    rows = per * height
    tiles = count // LANES
    for i in range(chunks):
        tail = tails[i * per]
        for z in range(1, per):
            tail += pltpu.roll(tails[i * per + z], z * height, 1)
        out[i, 2 * tiles * rows :] = tail

    def put(block, scores):
        for i in range(chunks):
            for c in range(tiles):
                at = (block * tiles + c) * rows
                out[i, at : at + rows] = scores[i * rows : (i + 1) * rows, c * LANES : (c + 1) * LANES]

    put(0, dot_t(unit, index[...]) * 8.0)
    copy.wait()
    put(1, dot_t(unit, held[...]) * 8.0)


def combine(tiles, height, factor, got):
    tails = [[down(block[tiles * height + t : tiles * height + t + 1], height) for t in range(4)] for block in got]
    top = tails[0][0]
    for tail in tails[1:]:
        top = jnp.maximum(top, tail[0])
    total, squares = [0.0] * tiles, 0.0
    for block, (g, *parts) in zip(got, tails):
        scale = jnp.exp2(g - top)
        squares += sum(parts) * (scale * scale)
        scale = scale * factor
        total = [total[c] + block[c * height : (c + 1) * height] * scale for c in range(tiles)]
    return total, squares, top


def middle_kernel(height, me, got, out):
    groups = out.shape[0]
    rows = groups * height
    tiles = (out.shape[2] - TAIL) // height
    total, squares, top = combine(2 * tiles, rows, 0.25, [got.at[i] for i in range(got.shape[0])])
    values = (top, *pieces(squares))
    for z in range(groups):
        here = slice(z * height, (z + 1) * height)
        tail = across(*(value[here] for value in values))
        for block, k in enumerate((me[0], 1 - me[0])):
            for c in range(tiles):
                out[z, k, c * height : (c + 1) * height] = total[block * tiles + c][here]
            out[z, k, tiles * height :] = tail


def last_kernel(height, got, out):
    tiles = out.shape[1] // LANES
    for k in range(got.shape[1]):
        total, squares, top = combine(tiles, height, 0.5, [got.at[i, k] for i in range(got.shape[0])])
        norm = jnp.sqrt(squares + 1e-06 * jnp.exp2(-2.0 * jnp.maximum(top, -60.0)))
        for c in range(tiles):
            out[k * height : (k + 1) * height, c * LANES : (c + 1) * LANES] = total[c] / norm


def call(kernel, spaces, shape, dtype, *args, **kwargs):
    return pl.pallas_call(
        kernel,
        out_shape=jax.ShapeDtypeStruct(shape, dtype),
        in_specs=[pl.BlockSpec(memory_space=space) for space in spaces],
        out_specs=pl.BlockSpec(memory_space=VMEM),
        compiler_params=pltpu.CompilerParams(vmem_limit_bytes=16 << 20),
        **kwargs,
    )(*args)


def swap(array):
    return lax.ppermute(array, "k", [(0, 1), (1, 0)])


def local(sizes, query, fisher, index):
    zh, x, zl, y, k = (sizes[a] for a in AXES)
    rows, pairs = zh * x, zl * y
    me = lax.axis_index("k").astype(jnp.int32).reshape(1)
    fisher_other = swap(fisher)
    index_other = swap(index)
    height, width = query.shape[0] // k, query.shape[1]
    features, count = fisher.shape[0], index.shape[0]
    deep = features // LANES * height + TAIL
    wide = 2 * (count // LANES) * zh * height + TAIL
    short = count // LANES * height + TAIL

    def exchange(sent, axes, shape):
        return lax.all_to_all(sent.reshape(-1, LANES), axes, 0, 0, tiled=True).reshape(shape)

    copies = call(copy_kernel, (VMEM,), (rows,) + query.shape, BF16, query).reshape(-1, width)
    held = lax.all_to_all(copies, (*ROW, "k"), 0, 0, tiled=True)
    held = held.reshape(rows, k, height, width)

    order = tuple(z * x + i for i in range(x) for z in range(zh))
    sent = call(
        functools.partial(first_kernel, order), (SMEM, VMEM, VMEM, VMEM), (pairs, deep, LANES), F32,
        me, held, fisher, fisher_other,
    )
    got = exchange(sent.astype(F16), PAIR, (pairs, deep, LANES)).astype(F32)

    sent = call(functools.partial(unit_kernel, height), (VMEM,), got.shape, BF16, got)
    got = exchange(sent, PAIR, got.shape)

    sent = call(
        functools.partial(score_kernel, height), (VMEM, VMEM, pl.ANY), (x, wide, LANES), F32, got, index, index_other,
        scratch_shapes=[VMEM((count, features), BF16), pltpu.SemaphoreType.DMA],
    )
    got = exchange(sent.astype(F16), "x", sent.shape).astype(F32)

    sent = call(functools.partial(middle_kernel, height), (SMEM, VMEM), (zh, k, short, LANES), F32, me, got)
    got = exchange(sent.astype(F16), ("zh", "k"), sent.shape).astype(F32)
    return call(functools.partial(last_kernel, height), (VMEM,), (k * height, count), F32, got)


def fine_mesh(mesh):
    rows, cols = mesh.devices.shape
    shape = (rows // 4, 4, 2, cols // 4, 2) if rows >= 16 else (2, rows // 2, 2, cols // 4, 2)
    return Mesh(mesh.devices.reshape(shape), AXES)


def solution(mesh):
    fine = fine_mesh(mesh)
    sizes = dict(fine.shape)
    row, col = ROW, (*PAIR, "k")
    placed = (P(row, col), P(row, col), P(col, row))
    return jax.shard_map(
        functools.partial(local, sizes), mesh=fine, in_specs=placed, out_specs=P(row, col), check_vma=False
    )
```

time: 123 us -> 119 us (0.967)
  blocking collectives: 33.8 us -> 60.1 us
  waiting for transfers between devices: 45.5 us -> 28 us
  starting transfers between devices: 34.4 us -> 22.4 us
    all_to_all x2 -> x3, blocking collectives: 33.8 us -> 60.1 us  [exchange(): lax.all_to_all(sent.reshape(-1, LANES), axes, 0, 0, tiled=True)]
    all_to_all x2 -> x1, waiting for transfers between devices: 28.6 us -> 13.3 us  [exchange(): lax.all_to_all(sent.reshape(-1, LANES), axes, 0, 0, tiled=True)]
    all_to_all x2 -> x1, starting transfers between devices: 15.1 us -> 3.66 us  [exchange(): lax.all_to_all(sent.reshape(-1, LANES), axes, 0, 0, tiled=True)]
    all_to_all x1, waiting for transfers between devices: 16.9 us -> 14.7 us  [local(): held = lax.all_to_all(copies, (*ROW, 'k'), 0, 0, tiled=True)]
    broadcast_in_dim x1 -> x0, local copies, waits for them, and re-layouts: 1.61 us -> none  [local(): jnp.broadcast_to(query[None], (rows,) + query.shape).reshape(-1, width)]
    pallas_call x5 -> x6, Pallas kernels: 5.62 us -> 6.47 us  [call(): pl.pallas_call(kernel, out_shape=jax.ShapeDtypeStruct(shape, dtype), in_s...]
  transfers between devices with their start and end apart: 5 -> 4, of which waited for: 3 -> 2; matrix products, arithmetic and copies ran while one was open for 1% -> 0% of each run, Pallas kernels for 1% -> 2%
where the time goes in v5:
time: 119 us; the launch traced here: 118 us
  blocking collectives  60.1 us (51%)
  waiting for transfers between devices  28 us (24%)
  starting transfers between devices  22.4 us (19%)
  Pallas kernels  6.47 us (5%)
    all_to_all x3, blocking collectives, exchange(): lax.all_to_all(sent.reshape(-1, LANES), axes, 0, 0, tiled=True)  60.1 us
    all_to_all x1, waiting for transfers between devices, local(): held = lax.all_to_all(copies, (*ROW, 'k'), 0, 0, tiled=True)  14.7 us
    all_to_all x1, waiting for transfers between devices, exchange(): lax.all_to_all(sent.reshape(-1, LANES), axes, 0, 0, tiled=True)  13.3 us
    ppermute x2, starting transfers between devices, swap(): return lax.ppermute(array, 'k', [(0, 1), (1, 0)])  11 us
    all_to_all x1, starting transfers between devices, local(): held = lax.all_to_all(copies, (*ROW, 'k'), 0, 0, tiled=True)  7.69 us
    pallas_call x6, Pallas kernels, call(): pl.pallas_call(kernel, out_shape=jax.ShapeDtypeStruct(shape, dtype), in_s...  6.47 us
    all_to_all x1, starting transfers between devices, exchange(): lax.all_to_all(sent.reshape(-1, LANES), axes, 0, 0, tiled=True)  3.66 us
  transfers between devices with their start and end apart: 4, of which 2 were waited for; matrix products, arithmetic and copies ran while one was open for 0% of the time, Pallas kernels for 2%

profile of v5, /device:TPU:1, one launch (start us, length us, event | category | flops | bytes accessed | tf_op | source)
XLA Modules:
  0.0 118.3 jit_solution(6834102550555007132)
XLA Ops:
  0.0 8.9 %collective-permute-start = (bf16[1024,512]{1,0:T(8,128)(2,1)}, bf16[1024,512]{1,0:T(8,128)(2,1)S(1)}, u32[]{:S(2)}, u32[]{:S(2)}) collective-permute-start(bf16[1024,512]{1,0:T(8,128)(2,1)} %fisher.1), channel_id=1, source_target_pairs={{0,1},{1,0},{2,3},{3,2},{4,5},{5,4},{6,7},{7,6},{8,9},{9,8},{10,11... | collective-permute-start | bytes 3145736 | tf_op jit(solution)/shard_map/ppermute | solution.py:172
  8.9 0.0 copy-start.2
  8.9 0.7 copy-done.2
  9.6 0.8 shard_map.37
  10.5 7.7 %all-to-all-start = ((bf16[32,16,512]{2,1,0:T(8,128)(2,1)}), bf16[32,16,512]{2,1,0:T(8,128)(2,1)S(1)}, u32[]{:S(2)}, u32[]{:S(2)}) async-start(bf16[32,16,512]{2,1,0:T(8,128)(2,1)} %bitcast.1), calls=%async_computation | async-start | bytes 1048576 | tf_op jit(solution)/shard_map/all_to_all | solution.py:191
  18.2 2.1 %collective-permute-start.1 = (bf16[1024,1024]{1,0:T(8,128)(2,1)}, bf16[1024,1024]{1,0:T(8,128)(2,1)}, u32[]{:S(2)}, u32[]{:S(2)}) collective-permute-start(bf16[1024,1024]{1,0:T(8,128)(2,1)} %index.1), channel_id=1, source_target_pairs={{0,1},{1,0},{2,3},{3,2},{4,5},{5,4},{6,7},{7,6},{8,9},{9,8},{10,11... | collective-permute-start | bytes 6291464 | tf_op jit(solution)/shard_map/ppermute | solution.py:172
  20.3 14.7 %all-to-all-done = bf16[32,16,512]{2,1,0:T(8,128)(2,1)S(1)} async-done(((bf16[32,16,512]{2,1,0:T(8,128)(2,1)}), bf16[32,16,512]{2,1,0:T(8,128)(2,1)S(1)}, u32[]{:S(2)}, u32[]{:S(2)}) %all-to-all-start) | async-done | bytes 524320 | tf_op jit(solution)/shard_map/all_to_all | solution.py:191
  35.0 0.0 collective-permute-done.other
  35.0 0.0 copy-done.1
  35.0 0.9 shard_map.38
  35.9 0.1 convert_element_type.20
  36.0 26.2 %all_to_all.36 = f16[16,136,128]{2,1,0:T(8,128)(2,1)S(1)} all-to-all(f16[16,136,128]{2,1,0:T(8,128)(2,1)S(1)} %convert_element_type.20), channel_id=1, replica_groups=mesh['zh'=4,'x'=4,'zl'=2,'y'=8,'k'=2] {'zl','y'}, dimensions={0} | all-to-all | bytes 1114112 | tf_op jit(solution)/shard_map/all_to_all | solution.py:188
  62.2 0.1 convert_element_type.21.got
  62.2 1.2 shard_map.39
  63.4 3.7 %all-to-all-start.2 = ((bf16[16,136,128]{2,1,0:T(8,128)(2,1)}), bf16[16,136,128]{2,1,0:T(8,128)(2,1)S(1)}, u32[]{:S(2)}, u32[]{:S(2)}) async-start(bf16[16,136,128]{2,1,0:T(8,128)(2,1)} %shard_map.39), calls=%async_computation.2 | async-start | bytes 1114112 | tf_op jit(solution)/shard_map/all_to_all | solution.py:188
  67.1 0.0 collective-permute-done.1.other
  67.1 13.3 %all-to-all-done.2.got = bf16[16,136,128]{2,1,0:T(8,128)(2,1)S(1)} async-done(((bf16[16,136,128]{2,1,0:T(8,128)(2,1)}), bf16[16,136,128]{2,1,0:T(8,128)(2,1)S(1)}, u32[]{:S(2)}, u32[]{:S(2)}) %all-to-all-start.2) | async-done | bytes 557088 | tf_op jit(solution)/shard_map/all_to_all | solution.py:188
  80.4 2.3 %shard_map.40 = f32[4,1032,128]{2,1,0:T(8,128)S(1)} custom-call(bf16[16,136,128]{2,1,0:T(8,128)(2,1)S(1)} %all-to-all-done.2.got, bf16[1024,1024]{1,0:T(8,128)(2,1)S(1)} %copy-done, bf16[1024,1024]{1,0:T(8,128)(2,1)} %collective-permute-done.1.other), custom_call_target="tpu_custom_call" | custom-call | tf_op jit(solution)/shard_map/pallas_call | solution.py:161
  82.7 0.1 convert_element_type.22
  82.9 15.1 %all_to_all.37 = f16[4,1032,128]{2,1,0:T(8,128)(2,1)S(1)} all-to-all(f16[4,1032,128]{2,1,0:T(8,128)(2,1)S(1)} %convert_element_type.22), channel_id=1, replica_groups=mesh['zh'=4,'x'=4,'zl'=2,'y'=8,'k'=2] {'x'}, dimensions={0} | all-to-all | bytes 2113536 | tf_op jit(solution)/shard_map/all_to_all | solution.py:188
  98.0 0.1 convert_element_type.23.got
  98.1 0.4 shard_map.41
  98.6 18.8 %all_to_all.38 = f16[8,136,128]{2,1,0:T(8,128)(2,1)S(1)} all-to-all(f16[8,136,128]{2,1,0:T(8,128)(2,1)S(1)} %bitcast.7), channel_id=1, replica_groups=mesh['zh'=4,'x'=4,'zl'=2,'y'=8,'k'=2] {'zh','k'}, dimensions={0} | all-to-all | bytes 557056 | tf_op jit(solution)/shard_map/all_to_all | solution.py:188
  117.4 0.8 shard_map.42
  (5 shorter events, 0.1 us)
Async XLA Ops:
  0.0 35.0 %copy-start.1 = (bf16[1024,512]{1,0:T(8,128)(2,1)S(1)}, bf16[1024,512]{1,0:T(8,128)(2,1)}, u32[]{:S(2)}) copy-start(bf16[1024,512]{1,0:T(8,128)(2,1)} %fisher.1) | copy-start | bytes 3145732
  0.0 35.0 %collective-permute-start = (bf16[1024,512]{1,0:T(8,128)(2,1)}, bf16[1024,512]{1,0:T(8,128)(2,1)S(1)}, u32[]{:S(2)}, u32[]{:S(2)}) collective-permute-start(bf16[1024,512]{1,0:T(8,128)(2,1)} %fisher.1), channel_id=1, source_target_pairs={{0,1},{1,0},{2,3},{3,2},{4,5},{5,4},{6,7},{7,6},{8,9},{9,8},{10,11... | collective-permute-start | bytes 3145736 | tf_op jit(solution)/shard_map/ppermute | solution.py:172
  8.9 0.8 copy-start.2
  10.5 24.6 %all-to-all-start = ((bf16[32,16,512]{2,1,0:T(8,128)(2,1)}), bf16[32,16,512]{2,1,0:T(8,128)(2,1)S(1)}, u32[]{:S(2)}, u32[]{:S(2)}) async-start(bf16[32,16,512]{2,1,0:T(8,128)(2,1)} %bitcast.1), calls=%async_computation | async-start | bytes 1048576 | tf_op jit(solution)/shard_map/all_to_all | solution.py:191
  18.2 48.9 %collective-permute-start.1 = (bf16[1024,1024]{1,0:T(8,128)(2,1)}, bf16[1024,1024]{1,0:T(8,128)(2,1)}, u32[]{:S(2)}, u32[]{:S(2)}) collective-permute-start(bf16[1024,1024]{1,0:T(8,128)(2,1)} %index.1), channel_id=1, source_target_pairs={{0,1},{1,0},{2,3},{3,2},{4,5},{5,4},{6,7},{7,6},{8,9},{9,8},{10,11... | collective-permute-start | bytes 6291464 | tf_op jit(solution)/shard_map/ppermute | solution.py:172
  62.2 18.2 %copy-start = (bf16[1024,1024]{1,0:T(8,128)(2,1)S(1)}, bf16[1024,1024]{1,0:T(8,128)(2,1)}, u32[]{:S(2)}) copy-start(bf16[1024,1024]{1,0:T(8,128)(2,1)} %index.1) | copy-start | bytes 6291460
  63.4 17.0 %all-to-all-start.2 = ((bf16[16,136,128]{2,1,0:T(8,128)(2,1)}), bf16[16,136,128]{2,1,0:T(8,128)(2,1)S(1)}, u32[]{:S(2)}, u32[]{:S(2)}) async-start(bf16[16,136,128]{2,1,0:T(8,128)(2,1)} %shard_map.39), calls=%async_computation.2 | async-start | bytes 1114112 | tf_op jit(solution)/shard_map/all_to_all | solution.py:188

commit v6 on v5

--- a/solution.py
+++ b/solution.py
@@ -50,25 +50,28 @@
     return lax.dot_general(a, b, (((1,), (1,)), ((), ())), preferred_element_type=F32)
 
 
-def copy_kernel(query, out):
+def copy_kernel(me, mine, theirs, out):
+    height = out.shape[2]
+    rows = pl.ds(pl.multiple_of(me[0] * height, height), height)
+    blocks = mine[rows], theirs[rows]
     for i in range(out.shape[0]):
-        out[i] = query[...]
-
-
-def first_kernel(order, me, held, fisher, other, out):
-    core = me[0]
+        for k, block in enumerate(blocks):
+            out[i, k] = block
+
+
+def first_kernel(held, fisher, other, out):
     groups, _, height, width = held.shape
-    mine = held[:, core].reshape(groups * height, width)
-    theirs = held[:, 1 - core].reshape(groups * height, width)
+    mine = held[:, 0].reshape(groups * height, width)
+    theirs = held[:, 1].reshape(groups * height, width)
     part = dot_t(mine, fisher[...]) + dot_t(theirs, other[...])
     tiles = part.shape[1] // LANES
     e = exponent(part)
     part = part * jnp.exp2(12.0 - e)
-    for to, source in enumerate(order):
-        rows = slice(source * height, (source + 1) * height)
+    for i in range(groups):
+        rows = slice(i * height, (i + 1) * height)
         for c in range(tiles):
-            out[to, c * height : (c + 1) * height] = part[rows, c * LANES : (c + 1) * LANES]
-        out[to, tiles * height :] = across(e[rows])
+            out[i, c * height : (c + 1) * height] = part[rows, c * LANES : (c + 1) * LANES]
+        out[i, tiles * height :] = across(e[rows])
 
 
 def unit_kernel(height, got, out):
@@ -187,15 +190,11 @@
     def exchange(sent, axes, shape):
         return lax.all_to_all(sent.reshape(-1, LANES), axes, 0, 0, tiled=True).reshape(shape)
 
-    copies = call(copy_kernel, (VMEM,), (rows,) + query.shape, BF16, query).reshape(-1, width)
-    held = lax.all_to_all(copies, (*ROW, "k"), 0, 0, tiled=True)
+    copies = call(copy_kernel, (SMEM, VMEM, VMEM), (rows, k, height, width), BF16, me, query, swap(query))
+    held = lax.all_to_all(copies.reshape(-1, width), ("x", "zh"), 0, 0, tiled=True)
     held = held.reshape(rows, k, height, width)
 
-    order = tuple(z * x + i for i in range(x) for z in range(zh))
-    sent = call(
-        functools.partial(first_kernel, order), (SMEM, VMEM, VMEM, VMEM), (pairs, deep, LANES), F32,
-        me, held, fisher, fisher_other,
-    )
+    sent = call(first_kernel, (VMEM, VMEM, VMEM), (pairs, deep, LANES), F32, held, fisher, fisher_other)
     got = exchange(sent.astype(F16), PAIR, (pairs, deep, LANES)).astype(F32)
 
     sent = call(functools.partial(unit_kernel, height), (VMEM,), got.shape, BF16, got)

time: 119 us -> 122 us (1.025)
  starting transfers between devices: 22.4 us -> 25.4 us
    ppermute x2 -> x3, starting transfers between devices: 11 us -> 13.1 us  [swap(): return lax.ppermute(array, 'k', [(0, 1), (1, 0)])]
    ppermute x2 -> x3, waiting for transfers between devices: 0.01 us -> 1.38 us  [swap(): return lax.ppermute(array, 'k', [(0, 1), (1, 0)])]
    all_to_all x1, waiting for transfers between devices: 14.7 us -> 13.4 us  [local(): lax.all_to_all(copies.reshape(-1, width), ('x', 'zh'), 0, 0, tiled=True)]
    all_to_all x1, starting transfers between devices: 3.66 us -> 4.97 us  [exchange(): lax.all_to_all(sent.reshape(-1, LANES), axes, 0, 0, tiled=True)]
  transfers between devices with their start and end apart: 4 -> 5, of which waited for: 2 -> 3; matrix products, arithmetic and copies ran while one was open for 0% -> 0% of each run, Pallas kernels for 2% -> 2%
where the time goes in v6:
time: 122 us; the launch traced here: 121 us
  blocking collectives  60.3 us (49%)
  waiting for transfers between devices  27.5 us (23%)
  starting transfers between devices  25.4 us (21%)
  Pallas kernels  6.47 us (5%)
    all_to_all x3, blocking collectives, exchange(): lax.all_to_all(sent.reshape(-1, LANES), axes, 0, 0, tiled=True)  60.3 us
    all_to_all x1, waiting for transfers between devices, local(): lax.all_to_all(copies.reshape(-1, width), ('x', 'zh'), 0, 0, tiled=True)  13.4 us
    ppermute x3, starting transfers between devices, swap(): return lax.ppermute(array, 'k', [(0, 1), (1, 0)])  13.1 us
    all_to_all x1, waiting for transfers between devices, exchange(): lax.all_to_all(sent.reshape(-1, LANES), axes, 0, 0, tiled=True)  12.8 us
    all_to_all x1, starting transfers between devices, local(): lax.all_to_all(copies.reshape(-1, width), ('x', 'zh'), 0, 0, tiled=True)  7.24 us
    pallas_call x6, Pallas kernels, call(): pl.pallas_call(kernel, out_shape=jax.ShapeDtypeStruct(shape, dtype), in_s...  6.47 us
    all_to_all x1, starting transfers between devices, exchange(): lax.all_to_all(sent.reshape(-1, LANES), axes, 0, 0, tiled=True)  4.97 us
  transfers between devices with their start and end apart: 5, of which 3 were waited for; matrix products, arithmetic and copies ran while one was open for 0% of the time, Pallas kernels for 2%

profile of v6, /device:TPU:1, one launch (start us, length us, event | category | flops | bytes accessed | tf_op | source)
XLA Modules:
  0.0 121.1 jit_solution(9889951823333414627)
XLA Ops:
  0.0 8.9 %collective-permute-start.1 = (bf16[1024,512]{1,0:T(8,128)(2,1)}, bf16[1024,512]{1,0:T(8,128)(2,1)S(1)}, u32[]{:S(2)}, u32[]{:S(2)}) collective-permute-start(bf16[1024,512]{1,0:T(8,128)(2,1)} %fisher.1), channel_id=1, source_target_pairs={{0,1},{1,0},{2,3},{3,2},{4,5},{5,4},{6,7},{7,6},{8,9},{9,8},{10,11... | collective-permute-start | bytes 3145736 | tf_op jit(solution)/shard_map/ppermute | solution.py:175
  8.9 1.9 %collective-permute-start = (bf16[32,512]{1,0:T(8,128)(2,1)}, bf16[32,512]{1,0:T(8,128)(2,1)S(1)}, u32[]{:S(2)}, u32[]{:S(2)}) collective-permute-start(bf16[32,512]{1,0:T(8,128)(2,1)} %mine.1), channel_id=1, source_target_pairs={{0,1},{1,0},{2,3},{3,2},{4,5},{5,4},{6,7},{7,6},{8,9},{9,8},{10,11... | collective-permute-start | bytes 98312 | tf_op jit(solution)/shard_map/ppermute | solution.py:175
  10.8 1.4 %collective-permute-done.theirs = bf16[32,512]{1,0:T(8,128)(2,1)S(1)} collective-permute-done((bf16[32,512]{1,0:T(8,128)(2,1)}, bf16[32,512]{1,0:T(8,128)(2,1)S(1)}, u32[]{:S(2)}, u32[]{:S(2)}) %collective-permute-start) | collective-permute-done | bytes 32800 | tf_op jit(solution)/shard_map/ppermute | solution.py:175
  12.2 0.8 copy-done.2
  12.9 0.9 shard_map.37
  13.8 7.2 %all-to-all-start = ((bf16[16,32,512]{2,1,0:T(8,128)(2,1)}), bf16[16,32,512]{2,1,0:T(8,128)(2,1)S(1)}, u32[]{:S(2)}, u32[]{:S(2)}) async-start(bf16[16,32,512]{2,1,0:T(8,128)(2,1)} %bitcast.1), calls=%async_computation | async-start | bytes 1048576 | tf_op jit(solution)/shard_map/all_to_all | solution.py:194
  21.1 2.4 %collective-permute-start.2 = (bf16[1024,1024]{1,0:T(8,128)(2,1)}, bf16[1024,1024]{1,0:T(8,128)(2,1)}, u32[]{:S(2)}, u32[]{:S(2)}) collective-permute-start(bf16[1024,1024]{1,0:T(8,128)(2,1)} %index.1), channel_id=1, source_target_pairs={{0,1},{1,0},{2,3},{3,2},{4,5},{5,4},{6,7},{7,6},{8,9},{9,8},{10,11... | collective-permute-start | bytes 6291464 | tf_op jit(solution)/shard_map/ppermute | solution.py:175
  23.4 13.4 %all-to-all-done = bf16[16,32,512]{2,1,0:T(8,128)(2,1)S(1)} async-done(((bf16[16,32,512]{2,1,0:T(8,128)(2,1)}), bf16[16,32,512]{2,1,0:T(8,128)(2,1)S(1)}, u32[]{:S(2)}, u32[]{:S(2)}) %all-to-all-start) | async-done | bytes 524320 | tf_op jit(solution)/shard_map/all_to_all | solution.py:194
  36.8 0.0 collective-permute-done.1.other
  36.8 0.9 shard_map.38
  37.6 0.1 convert_element_type.20
  37.7 24.7 %all_to_all.36 = f16[16,136,128]{2,1,0:T(8,128)(2,1)S(1)} all-to-all(f16[16,136,128]{2,1,0:T(8,128)(2,1)S(1)} %convert_element_type.20), channel_id=1, replica_groups=mesh['zh'=4,'x'=4,'zl'=2,'y'=8,'k'=2] {'zl','y'}, dimensions={0} | all-to-all | bytes 1114112 | tf_op jit(solution)/shard_map/all_to_all | solution.py:191
  62.4 0.1 convert_element_type.21.got
  62.5 1.2 shard_map.39
  63.7 5.0 %all-to-all-start.2 = ((bf16[16,136,128]{2,1,0:T(8,128)(2,1)}), bf16[16,136,128]{2,1,0:T(8,128)(2,1)S(1)}, u32[]{:S(2)}, u32[]{:S(2)}) async-start(bf16[16,136,128]{2,1,0:T(8,128)(2,1)} %shard_map.39), calls=%async_computation.2 | async-start | bytes 1114112 | tf_op jit(solution)/shard_map/all_to_all | solution.py:191
  68.7 0.0 collective-permute-done.2.other
  68.7 12.8 %all-to-all-done.2.got = bf16[16,136,128]{2,1,0:T(8,128)(2,1)S(1)} async-done(((bf16[16,136,128]{2,1,0:T(8,128)(2,1)}), bf16[16,136,128]{2,1,0:T(8,128)(2,1)S(1)}, u32[]{:S(2)}, u32[]{:S(2)}) %all-to-all-start.2) | async-done | bytes 557088 | tf_op jit(solution)/shard_map/all_to_all | solution.py:191
  81.5 2.3 %shard_map.40 = f32[4,1032,128]{2,1,0:T(8,128)S(1)} custom-call(bf16[16,136,128]{2,1,0:T(8,128)(2,1)S(1)} %all-to-all-done.2.got, bf16[1024,1024]{1,0:T(8,128)(2,1)S(1)} %copy-done, bf16[1024,1024]{1,0:T(8,128)(2,1)} %collective-permute-done.2.other), custom_call_target="tpu_custom_call" | custom-call | tf_op jit(solution)/shard_map/pallas_call | solution.py:164
  83.8 0.1 convert_element_type.22
  84.0 14.3 %all_to_all.37 = f16[4,1032,128]{2,1,0:T(8,128)(2,1)S(1)} all-to-all(f16[4,1032,128]{2,1,0:T(8,128)(2,1)S(1)} %convert_element_type.22), channel_id=1, replica_groups=mesh['zh'=4,'x'=4,'zl'=2,'y'=8,'k'=2] {'x'}, dimensions={0} | all-to-all | bytes 2113536 | tf_op jit(solution)/shard_map/all_to_all | solution.py:191
  98.3 0.1 convert_element_type.23.got
  98.4 0.4 shard_map.41
  98.9 21.3 %all_to_all.38 = f16[8,136,128]{2,1,0:T(8,128)(2,1)S(1)} all-to-all(f16[8,136,128]{2,1,0:T(8,128)(2,1)S(1)} %bitcast.7), channel_id=1, replica_groups=mesh['zh'=4,'x'=4,'zl'=2,'y'=8,'k'=2] {'zh','k'}, dimensions={0} | all-to-all | bytes 557056 | tf_op jit(solution)/shard_map/all_to_all | solution.py:191
  120.2 0.8 shard_map.42
  (7 shorter events, 0.1 us)
Async XLA Ops:
  0.0 36.8 %copy-start.1 = (bf16[1024,512]{1,0:T(8,128)(2,1)S(1)}, bf16[1024,512]{1,0:T(8,128)(2,1)}, u32[]{:S(2)}) copy-start(bf16[1024,512]{1,0:T(8,128)(2,1)} %fisher.1) | copy-start | bytes 3145732
  0.0 36.8 %collective-permute-start.1 = (bf16[1024,512]{1,0:T(8,128)(2,1)}, bf16[1024,512]{1,0:T(8,128)(2,1)S(1)}, u32[]{:S(2)}, u32[]{:S(2)}) collective-permute-start(bf16[1024,512]{1,0:T(8,128)(2,1)} %fisher.1), channel_id=1, source_target_pairs={{0,1},{1,0},{2,3},{3,2},{4,5},{5,4},{6,7},{7,6},{8,9},{9,8},{10,11... | collective-permute-start | bytes 3145736 | tf_op jit(solution)/shard_map/ppermute | solution.py:175
  8.9 3.3 %collective-permute-start = (bf16[32,512]{1,0:T(8,128)(2,1)}, bf16[32,512]{1,0:T(8,128)(2,1)S(1)}, u32[]{:S(2)}, u32[]{:S(2)}) collective-permute-start(bf16[32,512]{1,0:T(8,128)(2,1)} %mine.1), channel_id=1, source_target_pairs={{0,1},{1,0},{2,3},{3,2},{4,5},{5,4},{6,7},{7,6},{8,9},{9,8},{10,11... | collective-permute-start | bytes 98312 | tf_op jit(solution)/shard_map/ppermute | solution.py:175
  12.2 0.8 copy-start.2
  13.8 23.0 %all-to-all-start = ((bf16[16,32,512]{2,1,0:T(8,128)(2,1)}), bf16[16,32,512]{2,1,0:T(8,128)(2,1)S(1)}, u32[]{:S(2)}, u32[]{:S(2)}) async-start(bf16[16,32,512]{2,1,0:T(8,128)(2,1)} %bitcast.1), calls=%async_computation | async-start | bytes 1048576 | tf_op jit(solution)/shard_map/all_to_all | solution.py:194
  21.1 47.6 %collective-permute-start.2 = (bf16[1024,1024]{1,0:T(8,128)(2,1)}, bf16[1024,1024]{1,0:T(8,128)(2,1)}, u32[]{:S(2)}, u32[]{:S(2)}) collective-permute-start(bf16[1024,1024]{1,0:T(8,128)(2,1)} %index.1), channel_id=1, source_target_pairs={{0,1},{1,0},{2,3},{3,2},{4,5},{5,4},{6,7},{7,6},{8,9},{9,8},{10,11... | collective-permute-start | bytes 6291464 | tf_op jit(solution)/shard_map/ppermute | solution.py:175
  62.4 19.0 %copy-start = (bf16[1024,1024]{1,0:T(8,128)(2,1)S(1)}, bf16[1024,1024]{1,0:T(8,128)(2,1)}, u32[]{:S(2)}) copy-start(bf16[1024,1024]{1,0:T(8,128)(2,1)} %index.1) | copy-start | bytes 6291460
  63.7 17.8 %all-to-all-start.2 = ((bf16[16,136,128]{2,1,0:T(8,128)(2,1)}), bf16[16,136,128]{2,1,0:T(8,128)(2,1)S(1)}, u32[]{:S(2)}, u32[]{:S(2)}) async-start(bf16[16,136,128]{2,1,0:T(8,128)(2,1)} %shard_map.39), calls=%async_computation.2 | async-start | bytes 1114112 | tf_op jit(solution)/shard_map/all_to_all | solution.py:191

commit v7 on v5

--- a/solution.py
+++ b/solution.py
@@ -55,7 +55,7 @@
         out[i] = query[...]
 
 
-def first_kernel(order, me, held, fisher, other, out):
+def first_kernel(me, held, fisher, other, out):
     core = me[0]
     groups, _, height, width = held.shape
     mine = held[:, core].reshape(groups * height, width)
@@ -64,11 +64,11 @@
     tiles = part.shape[1] // LANES
     e = exponent(part)
     part = part * jnp.exp2(12.0 - e)
-    for to, source in enumerate(order):
-        rows = slice(source * height, (source + 1) * height)
-        for c in range(tiles):
-            out[to, c * height : (c + 1) * height] = part[rows, c * LANES : (c + 1) * LANES]
-        out[to, tiles * height :] = across(e[rows])
+    for i in range(groups):
+        rows = slice(i * height, (i + 1) * height)
+        for c in range(tiles):
+            out[i, c * height : (c + 1) * height] = part[rows, c * LANES : (c + 1) * LANES]
+        out[i, tiles * height :] = across(e[rows])
 
 
 def unit_kernel(height, got, out):
@@ -89,34 +89,34 @@
         out[copy, tiles * height :] = tail
 
 
-def score_kernel(height, got, index, other, out, held, sem):
-    count, features = index.shape
-    copy = pltpu.make_async_copy(other, held, sem)
-    copy.start()
-    sources, tiles = got.shape[0], features // LANES
+def unit_scores(height, got, index):
+    sources, tiles = got.shape[0], index.shape[1] // LANES
     unit = jnp.concatenate(
         [got[:, c * height : (c + 1) * height].reshape(sources * height, LANES) for c in range(tiles)], axis=1
     )
-    tails = got[:, tiles * height :].astype(F32)
-    chunks = out.shape[0]
-    per = sources // chunks
-    rows = per * height
-    tiles = count // LANES
-    for i in range(chunks):
-        tail = tails[i * per]
-        for z in range(1, per):
-            tail += pltpu.roll(tails[i * per + z], z * height, 1)
-        out[i, 2 * tiles * rows :] = tail
-
-    def put(block, scores):
-        for i in range(chunks):
-            for c in range(tiles):
-                at = (block * tiles + c) * rows
-                out[i, at : at + rows] = scores[i * rows : (i + 1) * rows, c * LANES : (c + 1) * LANES]
-
-    put(0, dot_t(unit, index[...]) * 8.0)
-    copy.wait()
-    put(1, dot_t(unit, held[...]) * 8.0)
+    return dot_t(unit, index[...]) * 8.0, got[:, tiles * height :].astype(F32)
+
+
+def score_kernel(height, got, index, out):
+    scores, tails = unit_scores(height, got, index)
+    tiles = index.shape[0] // LANES
+    for i in range(out.shape[0]):
+        for c in range(tiles):
+            rows = scores[i * height : (i + 1) * height, c * LANES : (c + 1) * LANES]
+            out[i, c * height : (c + 1) * height] = rows
+        out[i, tiles * height :] = tails[i]
+
+
+def rest_kernel(height, got, index, done, out):
+    scores, tails = unit_scores(height, got, index)
+    tiles = index.shape[0] // LANES
+    for i in range(out.shape[0]):
+        for c in range(tiles):
+            at = 2 * c * height
+            out[i, at : at + height] = done[i, c * height : (c + 1) * height]
+            rows = scores[i * height : (i + 1) * height, c * LANES : (c + 1) * LANES]
+            out[i, at + height : at + 2 * height] = rows
+        out[i, 2 * tiles * height :] = done[i, tiles * height :] + pltpu.roll(tails[i], height, 1)
 
 
 def combine(tiles, height, factor, got):
@@ -133,28 +133,14 @@
     return total, squares, top
 
 
-def middle_kernel(height, me, got, out):
-    groups = out.shape[0]
-    rows = groups * height
-    tiles = (out.shape[2] - TAIL) // height
-    total, squares, top = combine(2 * tiles, rows, 0.25, [got.at[i] for i in range(got.shape[0])])
-    values = (top, *pieces(squares))
-    for z in range(groups):
-        here = slice(z * height, (z + 1) * height)
-        tail = across(*(value[here] for value in values))
-        for block, k in enumerate((me[0], 1 - me[0])):
-            for c in range(tiles):
-                out[z, k, c * height : (c + 1) * height] = total[block * tiles + c][here]
-            out[z, k, tiles * height :] = tail
-
-
-def last_kernel(height, got, out):
-    tiles = out.shape[1] // LANES
-    for k in range(got.shape[1]):
-        total, squares, top = combine(tiles, height, 0.5, [got.at[i, k] for i in range(got.shape[0])])
-        norm = jnp.sqrt(squares + 1e-06 * jnp.exp2(-2.0 * jnp.maximum(top, -60.0)))
-        for c in range(tiles):
-            out[k * height : (k + 1) * height, c * LANES : (c + 1) * LANES] = total[c] / norm
+def last_kernel(me, got, out):
+    height, tiles = out.shape[1], out.shape[2] // LANES
+    total, squares, top = combine(tiles, 2 * height, 0.125, [got.at[i] for i in range(got.shape[0])])
+    norm = jnp.sqrt(squares + 1e-06 * jnp.exp2(-2.0 * jnp.maximum(top, -60.0)))
+    for c in range(tiles):
+        block = total[c] / norm
+        out[me[0], :, c * LANES : (c + 1) * LANES] = block[:height]
+        out[1 - me[0], :, c * LANES : (c + 1) * LANES] = block[height:]
 
 
 def call(kernel, spaces, shape, dtype, *args, **kwargs):
@@ -177,23 +163,21 @@
     rows, pairs = zh * x, zl * y
     me = lax.axis_index("k").astype(jnp.int32).reshape(1)
     fisher_other = swap(fisher)
-    index_other = swap(index)
     height, width = query.shape[0] // k, query.shape[1]
     features, count = fisher.shape[0], index.shape[0]
     deep = features // LANES * height + TAIL
-    wide = 2 * (count // LANES) * zh * height + TAIL
     short = count // LANES * height + TAIL
+    wide = short * 2 - TAIL
 
     def exchange(sent, axes, shape):
         return lax.all_to_all(sent.reshape(-1, LANES), axes, 0, 0, tiled=True).reshape(shape)
 
     copies = call(copy_kernel, (VMEM,), (rows,) + query.shape, BF16, query).reshape(-1, width)
-    held = lax.all_to_all(copies, (*ROW, "k"), 0, 0, tiled=True)
+    held = lax.all_to_all(copies, ("x", "zh", "k"), 0, 0, tiled=True)
     held = held.reshape(rows, k, height, width)
 
-    order = tuple(z * x + i for i in range(x) for z in range(zh))
     sent = call(
-        functools.partial(first_kernel, order), (SMEM, VMEM, VMEM, VMEM), (pairs, deep, LANES), F32,
+        first_kernel, (SMEM, VMEM, VMEM, VMEM), (pairs, deep, LANES), F32,
         me, held, fisher, fisher_other,
     )
     got = exchange(sent.astype(F16), PAIR, (pairs, deep, LANES)).astype(F32)
@@ -201,15 +185,15 @@
     sent = call(functools.partial(unit_kernel, height), (VMEM,), got.shape, BF16, got)
     got = exchange(sent, PAIR, got.shape)
 
-    sent = call(
-        functools.partial(score_kernel, height), (VMEM, VMEM, pl.ANY), (x, wide, LANES), F32, got, index, index_other,
-        scratch_shapes=[VMEM((count, features), BF16), pltpu.SemaphoreType.DMA],
-    )
-    got = exchange(sent.astype(F16), "x", sent.shape).astype(F32)
-
-    sent = call(functools.partial(middle_kernel, height), (SMEM, VMEM), (zh, k, short, LANES), F32, me, got)
-    got = exchange(sent.astype(F16), ("zh", "k"), sent.shape).astype(F32)
-    return call(functools.partial(last_kernel, height), (VMEM,), (k * height, count), F32, got)
+    others = swap(got)
+    cost = pl.CostEstimate(flops=2 * rows * height * count * features, bytes_accessed=8 << 20, transcendentals=0)
+    kernel = functools.partial(score_kernel, height)
+    done = call(kernel, (VMEM, VMEM), (rows, short, LANES), F32, got, index, cost_estimate=cost)
+    kernel = functools.partial(rest_kernel, height)
+    sent = call(kernel, (VMEM,) * 3, (rows, wide, LANES), F32, others, index, done, cost_estimate=cost)
+
+    got = exchange(sent.astype(F16), ("x", "zh"), sent.shape).astype(F32)
+    return call(last_kernel, (SMEM, VMEM), (k, height, count), F32, me, got).reshape(k * height, count)
 
 
 def fine_mesh(mesh):

time: 119 us -> 125 us (1.050)
  blocking collectives: 60.1 us -> 78.9 us
  waiting for transfers between devices: 28 us -> 18 us
  Pallas kernels: 6.47 us -> 4.74 us
    all_to_all x3, blocking collectives: 60.1 us -> 78.9 us  [exchange(): lax.all_to_all(sent.reshape(-1, LANES), axes, 0, 0, tiled=True)]
    all_to_all x2 -> x1, waiting for transfers between devices: 28 us -> 17.2 us  [local(): held = lax.all_to_all(copies, ('x', 'zh', 'k'), 0, 0, tiled=True)]
    all_to_all x2 -> x1, starting transfers between devices: 11.4 us -> 7.69 us  [local(): held = lax.all_to_all(copies, ('x', 'zh', 'k'), 0, 0, tiled=True)]
    ppermute x2, starting transfers between devices: 11 us -> 14.1 us  [swap(): return lax.ppermute(array, 'k', [(0, 1), (1, 0)])]
    pallas_call x6, Pallas kernels: 6.47 us -> 4.74 us  [call(): pl.pallas_call(kernel, out_shape=jax.ShapeDtypeStruct(shape, dtype), in_s...]
  transfers between devices with their start and end apart: 4 -> 3, of which waited for: 2 -> 2; matrix products, arithmetic and copies ran while one was open for 0% -> 0% of each run, Pallas kernels for 2% -> 1%
where the time goes in v7:
time: 125 us
  blocking collectives  78.9 us (63%)
  starting transfers between devices  21.8 us (17%)
  waiting for transfers between devices  18 us (14%)
  Pallas kernels  4.74 us (4%)
    all_to_all x3, blocking collectives, exchange(): lax.all_to_all(sent.reshape(-1, LANES), axes, 0, 0, tiled=True)  78.9 us
    all_to_all x1, waiting for transfers between devices, local(): held = lax.all_to_all(copies, ('x', 'zh', 'k'), 0, 0, tiled=True)  17.2 us
    ppermute x2, starting transfers between devices, swap(): return lax.ppermute(array, 'k', [(0, 1), (1, 0)])  14.1 us
    all_to_all x1, starting transfers between devices, local(): held = lax.all_to_all(copies, ('x', 'zh', 'k'), 0, 0, tiled=True)  7.69 us
    pallas_call x6, Pallas kernels, call(): pl.pallas_call(kernel, out_shape=jax.ShapeDtypeStruct(shape, dtype), in_s...  4.74 us
  transfers between devices with their start and end apart: 3, of which 2 were waited for; matrix products, arithmetic and copies ran while one was open for 0% of the time, Pallas kernels for 1%

profile of v7, /device:TPU:1, one launch (start us, length us, event | category | flops | bytes accessed | tf_op | source)
XLA Modules:
  0.0 124.8 jit_solution(13813870690140921431)
XLA Ops:
  0.0 8.9 %collective-permute-start = (bf16[1024,512]{1,0:T(8,128)(2,1)}, bf16[1024,512]{1,0:T(8,128)(2,1)S(1)}, u32[]{:S(2)}, u32[]{:S(2)}) collective-permute-start(bf16[1024,512]{1,0:T(8,128)(2,1)} %fisher.1), channel_id=1, source_target_pairs={{0,1},{1,0},{2,3},{3,2},{4,5},{5,4},{6,7},{7,6},{8,9},{9,8},{10,11... | collective-permute-start | bytes 3145736 | tf_op jit(solution)/shard_map/ppermute | solution.py:158
  8.9 0.0 copy-start.2
  8.9 0.7 copy-done.2
  9.6 0.8 shard_map.37
  10.5 7.7 %all-to-all-start = ((bf16[32,16,512]{2,1,0:T(8,128)(2,1)}), bf16[32,16,512]{2,1,0:T(8,128)(2,1)S(1)}, u32[]{:S(2)}, u32[]{:S(2)}) async-start(bf16[32,16,512]{2,1,0:T(8,128)(2,1)} %bitcast.1), calls=%async_computation | async-start | bytes 1048576 | tf_op jit(solution)/shard_map/all_to_all | solution.py:176
  18.2 17.2 %all-to-all-done = bf16[32,16,512]{2,1,0:T(8,128)(2,1)S(1)} async-done(((bf16[32,16,512]{2,1,0:T(8,128)(2,1)}), bf16[32,16,512]{2,1,0:T(8,128)(2,1)S(1)}, u32[]{:S(2)}, u32[]{:S(2)}) %all-to-all-start) | async-done | bytes 524320 | tf_op jit(solution)/shard_map/all_to_all | solution.py:176
  35.3 0.0 collective-permute-done.other
  35.3 0.0 copy-done.1
  35.3 0.9 shard_map.38
  36.2 0.1 convert_element_type.12
  36.3 26.9 %all_to_all.27 = f16[16,136,128]{2,1,0:T(8,128)(2,1)S(1)} all-to-all(f16[16,136,128]{2,1,0:T(8,128)(2,1)S(1)} %convert_element_type.12), channel_id=1, replica_groups=mesh['zh'=4,'x'=4,'zl'=2,'y'=8,'k'=2] {'zl','y'}, dimensions={0} | all-to-all | bytes 1114112 | tf_op jit(solution)/shard_map/all_to_all | solution.py:173
  63.2 0.1 convert_element_type.13.got
  63.2 0.0 copy-start
  63.3 0.4 shard_map.39
  63.6 19.7 %all_to_all.28.got = bf16[16,136,128]{2,1,0:T(8,128)(2,1)S(1)} all-to-all(bf16[16,136,128]{2,1,0:T(8,128)(2,1)S(1)} %shard_map.39), channel_id=1, replica_groups=mesh['zh'=4,'x'=4,'zl'=2,'y'=8,'k'=2] {'zl','y'}, dimensions={0} | all-to-all | bytes 1114112 | tf_op jit(solution)/shard_map/all_to_all | solution.py:173
  83.3 5.3 %collective-permute-start.1 = (bf16[16,136,128]{2,1,0:T(8,128)(2,1)S(1)}, bf16[16,136,128]{2,1,0:T(8,128)(2,1)S(1)}, u32[]{:S(2)}, u32[]{:S(2)}) collective-permute-start(bf16[16,136,128]{2,1,0:T(8,128)(2,1)S(1)} %all_to_all.28.got), channel_id=1, source_target_pairs={{0,1},{1,0},{2,3},{3,2},{4,5},{5,4},{6,7},{7,6},{8,9},{9,8},{10,11... | collective-permute-start | bytes 1671176 | tf_op jit(solution)/shard_map/ppermute | solution.py:158
  88.6 0.0 copy-done
  88.6 0.7 shard_map.40.done
  89.4 0.8 collective-permute-done.1.got
  90.2 0.8 shard_map.41
  91.0 0.1 convert_element_type.14
  91.1 32.3 %all_to_all.29 = f16[16,264,128]{2,1,0:T(8,128)(2,1)S(1)} all-to-all(f16[16,264,128]{2,1,0:T(8,128)(2,1)S(1)} %convert_element_type.14), channel_id=1, replica_groups=mesh['zh'=4,'x'=4,'zl'=2,'y'=8,'k'=2] {'x','zh'}, dimensions={0} | all-to-all | bytes 2162688 | tf_op jit(solution)/shard_map/all_to_all | solution.py:173
  123.4 0.1 convert_element_type.15.got
  123.6 1.2 shard_map.42
  (1 shorter events, 0.0 us)
Async XLA Ops:
  0.0 35.3 %copy-start.1 = (bf16[1024,512]{1,0:T(8,128)(2,1)S(1)}, bf16[1024,512]{1,0:T(8,128)(2,1)}, u32[]{:S(2)}) copy-start(bf16[1024,512]{1,0:T(8,128)(2,1)} %fisher.1) | copy-start | bytes 3145732
  0.0 35.3 %collective-permute-start = (bf16[1024,512]{1,0:T(8,128)(2,1)}, bf16[1024,512]{1,0:T(8,128)(2,1)S(1)}, u32[]{:S(2)}, u32[]{:S(2)}) collective-permute-start(bf16[1024,512]{1,0:T(8,128)(2,1)} %fisher.1), channel_id=1, source_target_pairs={{0,1},{1,0},{2,3},{3,2},{4,5},{5,4},{6,7},{7,6},{8,9},{9,8},{10,11... | collective-permute-start | bytes 3145736 | tf_op jit(solution)/shard_map/ppermute | solution.py:158
  8.9 0.8 copy-start.2
  10.5 24.9 %all-to-all-start = ((bf16[32,16,512]{2,1,0:T(8,128)(2,1)}), bf16[32,16,512]{2,1,0:T(8,128)(2,1)S(1)}, u32[]{:S(2)}, u32[]{:S(2)}) async-start(bf16[32,16,512]{2,1,0:T(8,128)(2,1)} %bitcast.1), calls=%async_computation | async-start | bytes 1048576 | tf_op jit(solution)/shard_map/all_to_all | solution.py:176
  63.2 25.4 %copy-start = (bf16[1024,1024]{1,0:T(8,128)(2,1)S(1)}, bf16[1024,1024]{1,0:T(8,128)(2,1)}, u32[]{:S(2)}) copy-start(bf16[1024,1024]{1,0:T(8,128)(2,1)} %index.3) | copy-start | bytes 6291460
  83.3 6.8 %collective-permute-start.1 = (bf16[16,136,128]{2,1,0:T(8,128)(2,1)S(1)}, bf16[16,136,128]{2,1,0:T(8,128)(2,1)S(1)}, u32[]{:S(2)}, u32[]{:S(2)}) collective-permute-start(bf16[16,136,128]{2,1,0:T(8,128)(2,1)S(1)} %all_to_all.28.got), channel_id=1, source_target_pairs={{0,1},{1,0},{2,3},{3,2},{4,5},{5,4},{6,7},{7,6},{8,9},{9,8},{10,11... | collective-permute-start | bytes 1671176 | tf_op jit(solution)/shard_map/ppermute | solution.py:158

commit v8 on v5

--- a/solution.py
+++ b/solution.py
@@ -13,6 +13,7 @@
 PAIR = ("zl", "y")
 LANES = 128
 TAIL = 8
+MARKS = {"parts": 3, "over_x": 5, "over_zh": 7}
 VMEM, SMEM = pltpu.VMEM, pltpu.SMEM
 
 
@@ -71,7 +72,7 @@
         out[to, tiles * height :] = across(e[rows])
 
 
-def unit_kernel(height, got, out):
+def unit_kernel(height, mark, got, out):
     tiles = (out.shape[1] - TAIL) // height
     full = [jnp.zeros((height, LANES), F32)] * tiles
     for i in range(got.shape[0]):
@@ -133,7 +134,8 @@
     return total, squares, top
 
 
-def middle_kernel(height, me, got, out):
+def middle_kernel(height, mark, got, out):
+    core = mark[0] - MARKS["over_x"]
     groups = out.shape[0]
     rows = groups * height
     tiles = (out.shape[2] - TAIL) // height
@@ -142,13 +144,13 @@
     for z in range(groups):
         here = slice(z * height, (z + 1) * height)
         tail = across(*(value[here] for value in values))
-        for block, k in enumerate((me[0], 1 - me[0])):
+        for block, k in enumerate((core, 1 - core)):
             for c in range(tiles):
                 out[z, k, c * height : (c + 1) * height] = total[block * tiles + c][here]
             out[z, k, tiles * height :] = tail
 
 
-def last_kernel(height, got, out):
+def last_kernel(height, mark, got, out):
     tiles = out.shape[1] // LANES
     for k in range(got.shape[1]):
         total, squares, top = combine(tiles, height, 0.5, [got.at[i, k] for i in range(got.shape[0])])
@@ -166,6 +168,19 @@
         compiler_params=pltpu.CompilerParams(vmem_limit_bytes=16 << 20),
         **kwargs,
     )(*args)
+
+
+def mark(name, me):
+    def kernel(me, out):
+        out[0] = me[0] + MARKS[name]
+
+    return pl.pallas_call(
+        kernel,
+        out_shape=jax.ShapeDtypeStruct((1,), jnp.int32),
+        in_specs=[pl.BlockSpec(memory_space=SMEM)],
+        out_specs=pl.BlockSpec(memory_space=SMEM),
+        cost_estimate=pl.CostEstimate(flops=1, bytes_accessed=8, transcendentals=0),
+    )(me)
 
 
 def swap(array):
@@ -196,20 +211,29 @@
         functools.partial(first_kernel, order), (SMEM, VMEM, VMEM, VMEM), (pairs, deep, LANES), F32,
         me, held, fisher, fisher_other,
     )
-    got = exchange(sent.astype(F16), PAIR, (pairs, deep, LANES)).astype(F32)
-
-    sent = call(functools.partial(unit_kernel, height), (VMEM,), got.shape, BF16, got)
+    sent = sent.astype(F16)
+    got = exchange(sent, PAIR, (pairs, deep, LANES))
+    got = got.astype(F32)
+
+    kernel = functools.partial(unit_kernel, height)
+    sent = call(kernel, (SMEM, VMEM), got.shape, BF16, mark("parts", me), got)
     got = exchange(sent, PAIR, got.shape)
 
     sent = call(
         functools.partial(score_kernel, height), (VMEM, VMEM, pl.ANY), (x, wide, LANES), F32, got, index, index_other,
         scratch_shapes=[VMEM((count, features), BF16), pltpu.SemaphoreType.DMA],
     )
-    got = exchange(sent.astype(F16), "x", sent.shape).astype(F32)
-
-    sent = call(functools.partial(middle_kernel, height), (SMEM, VMEM), (zh, k, short, LANES), F32, me, got)
-    got = exchange(sent.astype(F16), ("zh", "k"), sent.shape).astype(F32)
-    return call(functools.partial(last_kernel, height), (VMEM,), (k * height, count), F32, got)
+    sent = sent.astype(F16)
+    got = exchange(sent, "x", sent.shape)
+    got = got.astype(F32)
+
+    kernel = functools.partial(middle_kernel, height)
+    sent = call(kernel, (SMEM, VMEM), (zh, k, short, LANES), F32, mark("over_x", me), got)
+    sent = sent.astype(F16)
+    got = exchange(sent, ("zh", "k"), sent.shape)
+    got = got.astype(F32)
+    kernel = functools.partial(last_kernel, height)
+    return call(kernel, (SMEM, VMEM), (k * height, count), F32, mark("over_zh", me), got)
 
 
 def fine_mesh(mesh):

time: 119 us -> 126 us (1.059)
  blocking collectives: 60.1 us -> 0 us
  waiting for transfers between devices: 28 us -> 65.1 us
  starting transfers between devices: 22.4 us -> 45.1 us
  Pallas kernels: 6.47 us -> 9.89 us
  other arithmetic: 0.51 us -> 3.03 us
    all_to_all x3 -> x0, blocking collectives: 60.1 us -> none  [exchange(): lax.all_to_all(sent.reshape(-1, LANES), axes, 0, 0, tiled=True)]
    all_to_all x1 -> x4, waiting for transfers between devices: 13.3 us -> 50.3 us  [exchange(): lax.all_to_all(sent.reshape(-1, LANES), axes, 0, 0, tiled=True)]
    all_to_all x1 -> x4, starting transfers between devices: 3.66 us -> 26.4 us  [exchange(): lax.all_to_all(sent.reshape(-1, LANES), axes, 0, 0, tiled=True)]
    convert_element_type x6, other arithmetic: 0.51 us -> 3.03 us  [the longest x3 2.78 us: local(): sent = sent.astype(F16)]
    pallas_call x6, Pallas kernels: 6.47 us -> 8.34 us  [call(): pl.pallas_call(kernel, out_shape=jax.ShapeDtypeStruct(shape, dtype), in_s...]
    pallas_call x0 -> x3, Pallas kernels: none -> 1.56 us  [mark(): pl.pallas_call(kernel, out_shape=jax.ShapeDtypeStruct((1,), jnp.int32), i...]
  transfers between devices with their start and end apart: 4 -> 7, of which waited for: 2 -> 5; matrix products, arithmetic and copies ran while one was open for 0% -> 1% of each run, Pallas kernels for 2% -> 4%
where the time goes in v8:
time: 126 us; the launch traced here: 124 us
  waiting for transfers between devices  65.1 us (52%)
  starting transfers between devices  45.1 us (36%)
  Pallas kernels  9.89 us (8%)
  other arithmetic  3.03 us (2%)
    all_to_all x4, waiting for transfers between devices, exchange(): lax.all_to_all(sent.reshape(-1, LANES), axes, 0, 0, tiled=True)  50.3 us
    all_to_all x4, starting transfers between devices, exchange(): lax.all_to_all(sent.reshape(-1, LANES), axes, 0, 0, tiled=True)  26.4 us
    all_to_all x1, waiting for transfers between devices, local(): held = lax.all_to_all(copies, (*ROW, 'k'), 0, 0, tiled=True)  14.7 us
    ppermute x2, starting transfers between devices, swap(): return lax.ppermute(array, 'k', [(0, 1), (1, 0)])  11 us
    pallas_call x6, Pallas kernels, call(): pl.pallas_call(kernel, out_shape=jax.ShapeDtypeStruct(shape, dtype), in_s...  8.34 us
    all_to_all x1, starting transfers between devices, local(): held = lax.all_to_all(copies, (*ROW, 'k'), 0, 0, tiled=True)  7.69 us
    convert_element_type x3, other arithmetic, local(): sent = sent.astype(F16)  2.78 us
  transfers between devices with their start and end apart: 7, of which 5 were waited for; matrix products, arithmetic and copies ran while one was open for 1% of the time, Pallas kernels for 4%

profile of v8, /device:TPU:1, one launch (start us, length us, event | category | flops | bytes accessed | tf_op | source)
XLA Modules:
  0.0 124.0 jit_solution(17640807593213017358)
XLA Ops:
  0.0 8.9 %collective-permute-start = (bf16[1024,512]{1,0:T(8,128)(2,1)}, bf16[1024,512]{1,0:T(8,128)(2,1)S(1)}, u32[]{:S(2)}, u32[]{:S(2)}) collective-permute-start(bf16[1024,512]{1,0:T(8,128)(2,1)} %fisher.1), channel_id=1, source_target_pairs={{0,1},{1,0},{2,3},{3,2},{4,5},{5,4},{6,7},{7,6},{8,9},{9,8},{10,11... | collective-permute-start | bytes 3145736 | tf_op jit(solution)/shard_map/ppermute | solution.py:187
  8.9 0.7 copy-done.2
  9.6 0.8 shard_map.40
  10.5 7.7 %all-to-all-start = ((bf16[32,16,512]{2,1,0:T(8,128)(2,1)}), bf16[32,16,512]{2,1,0:T(8,128)(2,1)S(1)}, u32[]{:S(2)}, u32[]{:S(2)}) async-start(bf16[32,16,512]{2,1,0:T(8,128)(2,1)} %bitcast.1), calls=%async_computation | async-start | bytes 1048576 | tf_op jit(solution)/shard_map/all_to_all | solution.py:206
  18.2 2.1 %collective-permute-start.1 = (bf16[1024,1024]{1,0:T(8,128)(2,1)}, bf16[1024,1024]{1,0:T(8,128)(2,1)}, u32[]{:S(2)}, u32[]{:S(2)}) collective-permute-start(bf16[1024,1024]{1,0:T(8,128)(2,1)} %index.1), channel_id=1, source_target_pairs={{0,1},{1,0},{2,3},{3,2},{4,5},{5,4},{6,7},{7,6},{8,9},{9,8},{10,11... | collective-permute-start | bytes 6291464 | tf_op jit(solution)/shard_map/ppermute | solution.py:187
  20.3 14.7 %all-to-all-done = bf16[32,16,512]{2,1,0:T(8,128)(2,1)S(1)} async-done(((bf16[32,16,512]{2,1,0:T(8,128)(2,1)}), bf16[32,16,512]{2,1,0:T(8,128)(2,1)S(1)}, u32[]{:S(2)}, u32[]{:S(2)}) %all-to-all-start) | async-done | bytes 524320 | tf_op jit(solution)/shard_map/all_to_all | solution.py:206
  35.0 0.9 shard_map.41
  35.9 0.9 convert_element_type.20
  36.8 9.2 %all-to-all-start.1 = ((f16[16,136,128]{2,1,0:T(8,128)(2,1)}), f16[16,136,128]{2,1,0:T(8,128)(2,1)S(1)}, u32[]{:S(2)}, u32[]{:S(2)}) async-start(f16[16,136,128]{2,1,0:T(8,128)(2,1)} %convert_element_type.20), calls=%async_computation.1 | async-start | bytes 1114112 | tf_op jit(solution)/shard_map/all_to_all | solution.py:203
  46.0 0.5 shard_map.39.mark
  46.5 13.9 %all-to-all-done.1 = f16[16,136,128]{2,1,0:T(8,128)(2,1)S(1)} async-done(((f16[16,136,128]{2,1,0:T(8,128)(2,1)}), f16[16,136,128]{2,1,0:T(8,128)(2,1)S(1)}, u32[]{:S(2)}, u32[]{:S(2)}) %all-to-all-start.1) | async-done | bytes 557088 | tf_op jit(solution)/shard_map/all_to_all | solution.py:203
  60.5 1.8 %shard_map.42 = bf16[16,136,128]{2,1,0:T(8,128)(2,1)} custom-call(s32[1]{0:T(128)} %shard_map.39.mark, f32[16,136,128]{2,1,0:T(8,128)S(1)} %convert_element_type.21.got), custom_call_target="tpu_custom_call" | custom-call | tf_op jit(solution)/shard_map/pallas_call | solution.py:163
  62.2 6.5 %all-to-all-start.2 = ((bf16[16,136,128]{2,1,0:T(8,128)(2,1)}), bf16[16,136,128]{2,1,0:T(8,128)(2,1)S(1)}, u32[]{:S(2)}, u32[]{:S(2)}) async-start(bf16[16,136,128]{2,1,0:T(8,128)(2,1)} %shard_map.42), calls=%async_computation.2 | async-start | bytes 1114112 | tf_op jit(solution)/shard_map/all_to_all | solution.py:203
  68.7 14.5 %all-to-all-done.2.got = bf16[16,136,128]{2,1,0:T(8,128)(2,1)S(1)} async-done(((bf16[16,136,128]{2,1,0:T(8,128)(2,1)}), bf16[16,136,128]{2,1,0:T(8,128)(2,1)S(1)}, u32[]{:S(2)}, u32[]{:S(2)}) %all-to-all-start.2) | async-done | bytes 557088 | tf_op jit(solution)/shard_map/all_to_all | solution.py:203
  83.2 2.3 %shard_map.43 = f32[4,1032,128]{2,1,0:T(8,128)S(1)} custom-call(bf16[16,136,128]{2,1,0:T(8,128)(2,1)S(1)} %all-to-all-done.2.got, bf16[1024,1024]{1,0:T(8,128)(2,1)S(1)} %copy-done, bf16[1024,1024]{1,0:T(8,128)(2,1)} %collective-permute-done.1.other), custom_call_target="tpu_custom_call" | custom-call | tf_op jit(solution)/shard_map/pallas_call | solution.py:163
  85.6 1.1 convert_element_type.22
  86.7 3.5 %all-to-all-start.3 = ((f16[4,1032,128]{2,1,0:T(8,128)(2,1)}), f16[4,1032,128]{2,1,0:T(8,128)(2,1)S(1)}, u32[]{:S(2)}, u32[]{:S(2)}) async-start(f16[4,1032,128]{2,1,0:T(8,128)(2,1)} %convert_element_type.22), calls=%async_computation.3 | async-start | bytes 2113536 | tf_op jit(solution)/shard_map/all_to_all | solution.py:203
  90.2 0.5 shard_map.38.mark
  90.7 11.6 %all-to-all-done.3 = f16[4,1032,128]{2,1,0:T(8,128)(2,1)S(1)} async-done(((f16[4,1032,128]{2,1,0:T(8,128)(2,1)}), f16[4,1032,128]{2,1,0:T(8,128)(2,1)S(1)}, u32[]{:S(2)}, u32[]{:S(2)}) %all-to-all-start.3) | async-done | bytes 1056800 | tf_op jit(solution)/shard_map/all_to_all | solution.py:203
  102.5 1.0 shard_map.44
  103.5 0.7 convert_element_type.24
  104.3 7.3 %all-to-all-start.4 = ((f16[8,136,128]{2,1,0:T(8,128)(2,1)}), f16[8,136,128]{2,1,0:T(8,128)(2,1)S(1)}, u32[]{:S(2)}, u32[]{:S(2)}) async-start(f16[8,136,128]{2,1,0:T(8,128)(2,1)} %bitcast.3), calls=%async_computation.4 | async-start | bytes 557056 | tf_op jit(solution)/shard_map/all_to_all | solution.py:203
  112.1 10.4 %all-to-all-done.4 = f16[8,136,128]{2,1,0:T(8,128)(2,1)S(1)} async-done(((f16[8,136,128]{2,1,0:T(8,128)(2,1)}), f16[8,136,128]{2,1,0:T(8,128)(2,1)S(1)}, u32[]{:S(2)}, u32[]{:S(2)}) %all-to-all-start.4) | async-done | bytes 278560 | tf_op jit(solution)/shard_map/all_to_all | solution.py:203
  122.5 1.5 %shard_map.45 = f32[32,1024]{1,0:T(8,128)} custom-call(s32[1]{0:T(128)} %shard_map.37.mark, f32[4,2,136,128]{3,2,1,0:T(8,128)S(1)} %convert.1.got), custom_call_target="tpu_custom_call" | custom-call | tf_op jit(solution)/shard_map/pallas_call | solution.py:163
  (11 shorter events, 0.8 us)
Async XLA Ops:
  0.0 35.0 %copy-start.1 = (bf16[1024,512]{1,0:T(8,128)(2,1)S(1)}, bf16[1024,512]{1,0:T(8,128)(2,1)}, u32[]{:S(2)}) copy-start(bf16[1024,512]{1,0:T(8,128)(2,1)} %fisher.1) | copy-start | bytes 3145732
  0.0 35.0 %collective-permute-start = (bf16[1024,512]{1,0:T(8,128)(2,1)}, bf16[1024,512]{1,0:T(8,128)(2,1)S(1)}, u32[]{:S(2)}, u32[]{:S(2)}) collective-permute-start(bf16[1024,512]{1,0:T(8,128)(2,1)} %fisher.1), channel_id=1, source_target_pairs={{0,1},{1,0},{2,3},{3,2},{4,5},{5,4},{6,7},{7,6},{8,9},{9,8},{10,11... | collective-permute-start | bytes 3145736 | tf_op jit(solution)/shard_map/ppermute | solution.py:187
  8.9 0.8 copy-start.2
  10.5 24.6 %all-to-all-start = ((bf16[32,16,512]{2,1,0:T(8,128)(2,1)}), bf16[32,16,512]{2,1,0:T(8,128)(2,1)S(1)}, u32[]{:S(2)}, u32[]{:S(2)}) async-start(bf16[32,16,512]{2,1,0:T(8,128)(2,1)} %bitcast.1), calls=%async_computation | async-start | bytes 1048576 | tf_op jit(solution)/shard_map/all_to_all | solution.py:206
  18.2 50.5 %collective-permute-start.1 = (bf16[1024,1024]{1,0:T(8,128)(2,1)}, bf16[1024,1024]{1,0:T(8,128)(2,1)}, u32[]{:S(2)}, u32[]{:S(2)}) collective-permute-start(bf16[1024,1024]{1,0:T(8,128)(2,1)} %index.1), channel_id=1, source_target_pairs={{0,1},{1,0},{2,3},{3,2},{4,5},{5,4},{6,7},{7,6},{8,9},{9,8},{10,11... | collective-permute-start | bytes 6291464 | tf_op jit(solution)/shard_map/ppermute | solution.py:187
  36.8 23.6 %all-to-all-start.1 = ((f16[16,136,128]{2,1,0:T(8,128)(2,1)}), f16[16,136,128]{2,1,0:T(8,128)(2,1)S(1)}, u32[]{:S(2)}, u32[]{:S(2)}) async-start(f16[16,136,128]{2,1,0:T(8,128)(2,1)} %convert_element_type.20), calls=%async_computation.1 | async-start | bytes 1114112 | tf_op jit(solution)/shard_map/all_to_all | solution.py:203
  46.5 36.7 %copy-start = (bf16[1024,1024]{1,0:T(8,128)(2,1)S(1)}, bf16[1024,1024]{1,0:T(8,128)(2,1)}, u32[]{:S(2)}) copy-start(bf16[1024,1024]{1,0:T(8,128)(2,1)} %index.1) | copy-start | bytes 6291460
  62.2 21.0 %all-to-all-start.2 = ((bf16[16,136,128]{2,1,0:T(8,128)(2,1)}), bf16[16,136,128]{2,1,0:T(8,128)(2,1)S(1)}, u32[]{:S(2)}, u32[]{:S(2)}) async-start(bf16[16,136,128]{2,1,0:T(8,128)(2,1)} %shard_map.42), calls=%async_computation.2 | async-start | bytes 1114112 | tf_op jit(solution)/shard_map/all_to_all | solution.py:203
  86.7 15.7 %all-to-all-start.3 = ((f16[4,1032,128]{2,1,0:T(8,128)(2,1)}), f16[4,1032,128]{2,1,0:T(8,128)(2,1)S(1)}, u32[]{:S(2)}, u32[]{:S(2)}) async-start(f16[4,1032,128]{2,1,0:T(8,128)(2,1)} %convert_element_type.22), calls=%async_computation.3 | async-start | bytes 2113536 | tf_op jit(solution)/shard_map/all_to_all | solution.py:203
  104.3 18.2 %all-to-all-start.4 = ((f16[8,136,128]{2,1,0:T(8,128)(2,1)}), f16[8,136,128]{2,1,0:T(8,128)(2,1)S(1)}, u32[]{:S(2)}, u32[]{:S(2)}) async-start(f16[8,136,128]{2,1,0:T(8,128)(2,1)} %bitcast.3), calls=%async_computation.4 | async-start | bytes 557056 | tf_op jit(solution)/shard_map/all_to_all | solution.py:203

commit v9 on v5

--- a/solution.py
+++ b/solution.py
@@ -168,6 +168,19 @@
     )(*args)
 
 
+def beside(me):
+    def kernel(me, out):
+        out[0] = me[0] + 1
+
+    pl.pallas_call(
+        kernel,
+        out_shape=jax.ShapeDtypeStruct((1,), jnp.int32),
+        in_specs=[pl.BlockSpec(memory_space=SMEM)],
+        out_specs=pl.BlockSpec(memory_space=SMEM),
+        compiler_params=pltpu.CompilerParams(has_side_effects=True),
+    )(me)
+
+
 def swap(array):
     return lax.ppermute(array, "k", [(0, 1), (1, 0)])
 
@@ -208,7 +221,10 @@
     got = exchange(sent.astype(F16), "x", sent.shape).astype(F32)
 
     sent = call(functools.partial(middle_kernel, height), (SMEM, VMEM), (zh, k, short, LANES), F32, me, got)
-    got = exchange(sent.astype(F16), ("zh", "k"), sent.shape).astype(F32)
+    sent = sent.astype(F16)
+    got = exchange(sent, ("zh", "k"), sent.shape)
+    beside(me)
+    got = got.astype(F32)
     return call(functools.partial(last_kernel, height), (VMEM,), (k * height, count), F32, got)
 
 

time: 119 us -> 121 us (1.017)
  the two profiles are of different devices: /device:TPU:1 before, /device:TPU:8 now
where the time goes in v9:
time: 121 us; the launch traced here: 120 us
  blocking collectives  43.8 us (36%)
  waiting for transfers between devices  41.7 us (34%)
  starting transfers between devices  25.6 us (21%)
  Pallas kernels  6.98 us (6%)
  other arithmetic  1.22 us (1%)
    all_to_all x2, blocking collectives, exchange(): lax.all_to_all(sent.reshape(-1, LANES), axes, 0, 0, tiled=True)  43.8 us
    all_to_all x2, waiting for transfers between devices, exchange(): lax.all_to_all(sent.reshape(-1, LANES), axes, 0, 0, tiled=True)  26.8 us
    all_to_all x1, waiting for transfers between devices, local(): held = lax.all_to_all(copies, (*ROW, 'k'), 0, 0, tiled=True)  14.9 us
    all_to_all x1, starting transfers between devices, local(): held = lax.all_to_all(copies, (*ROW, 'k'), 0, 0, tiled=True)  13.3 us
    all_to_all x2, starting transfers between devices, exchange(): lax.all_to_all(sent.reshape(-1, LANES), axes, 0, 0, tiled=True)  8.11 us
    pallas_call x6, Pallas kernels, call(): pl.pallas_call(kernel, out_shape=jax.ShapeDtypeStruct(shape, dtype), in_s...  6.46 us
    ppermute x2, starting transfers between devices, swap(): return lax.ppermute(array, 'k', [(0, 1), (1, 0)])  4.22 us
  transfers between devices with their start and end apart: 5, of which 3 were waited for; matrix products, arithmetic and copies ran while one was open for 0% of the time, Pallas kernels for 3%

profile of v9, /device:TPU:8, one launch (start us, length us, event | category | flops | bytes accessed | tf_op | source)
XLA Modules:
  0.0 120.2 jit_solution(18446194079027368120)
XLA Ops:
  0.0 2.0 %collective-permute-start = (bf16[1024,512]{1,0:T(8,128)(2,1)}, bf16[1024,512]{1,0:T(8,128)(2,1)S(1)}, u32[]{:S(2)}, u32[]{:S(2)}) collective-permute-start(bf16[1024,512]{1,0:T(8,128)(2,1)} %fisher.1), channel_id=1, source_target_pairs={{0,1},{1,0},{2,3},{3,2},{4,5},{5,4},{6,7},{7,6},{8,9},{9,8},{10,11... | collective-permute-start | bytes 3145736 | tf_op jit(solution)/shard_map/ppermute | solution.py:185
  2.1 0.7 copy-done.2
  2.8 0.8 shard_map.38
  3.6 13.3 %all-to-all-start = ((bf16[32,16,512]{2,1,0:T(8,128)(2,1)}), bf16[32,16,512]{2,1,0:T(8,128)(2,1)S(1)}, u32[]{:S(2)}, u32[]{:S(2)}) async-start(bf16[32,16,512]{2,1,0:T(8,128)(2,1)} %bitcast.1), calls=%async_computation | async-start | bytes 1048576 | tf_op jit(solution)/shard_map/all_to_all | solution.py:204
  16.9 2.2 %collective-permute-start.1 = (bf16[1024,1024]{1,0:T(8,128)(2,1)}, bf16[1024,1024]{1,0:T(8,128)(2,1)}, u32[]{:S(2)}, u32[]{:S(2)}) collective-permute-start(bf16[1024,1024]{1,0:T(8,128)(2,1)} %index.1), channel_id=1, source_target_pairs={{0,1},{1,0},{2,3},{3,2},{4,5},{5,4},{6,7},{7,6},{8,9},{9,8},{10,11... | collective-permute-start | bytes 6291464 | tf_op jit(solution)/shard_map/ppermute | solution.py:185
  19.1 14.9 %all-to-all-done = bf16[32,16,512]{2,1,0:T(8,128)(2,1)S(1)} async-done(((bf16[32,16,512]{2,1,0:T(8,128)(2,1)}), bf16[32,16,512]{2,1,0:T(8,128)(2,1)S(1)}, u32[]{:S(2)}, u32[]{:S(2)}) %all-to-all-start) | async-done | bytes 524320 | tf_op jit(solution)/shard_map/all_to_all | solution.py:204
  34.0 0.9 shard_map.39
  34.9 0.1 convert_element_type.20
  35.0 27.3 %all_to_all.36 = f16[16,136,128]{2,1,0:T(8,128)(2,1)S(1)} all-to-all(f16[16,136,128]{2,1,0:T(8,128)(2,1)S(1)} %convert_element_type.20), channel_id=1, replica_groups=mesh['zh'=4,'x'=4,'zl'=2,'y'=8,'k'=2] {'zl','y'}, dimensions={0} | all-to-all | bytes 1114112 | tf_op jit(solution)/shard_map/all_to_all | solution.py:201
  62.3 0.1 convert_element_type.21.got
  62.3 1.2 shard_map.40
  63.5 4.7 %all-to-all-start.2 = ((bf16[16,136,128]{2,1,0:T(8,128)(2,1)}), bf16[16,136,128]{2,1,0:T(8,128)(2,1)S(1)}, u32[]{:S(2)}, u32[]{:S(2)}) async-start(bf16[16,136,128]{2,1,0:T(8,128)(2,1)} %shard_map.40), calls=%async_computation.2 | async-start | bytes 1114112 | tf_op jit(solution)/shard_map/all_to_all | solution.py:201
  68.2 0.0 collective-permute-done.1.other
  68.2 14.3 %all-to-all-done.2.got = bf16[16,136,128]{2,1,0:T(8,128)(2,1)S(1)} async-done(((bf16[16,136,128]{2,1,0:T(8,128)(2,1)}), bf16[16,136,128]{2,1,0:T(8,128)(2,1)S(1)}, u32[]{:S(2)}, u32[]{:S(2)}) %all-to-all-start.2) | async-done | bytes 557088 | tf_op jit(solution)/shard_map/all_to_all | solution.py:201
  82.6 2.3 %shard_map.41 = f32[4,1032,128]{2,1,0:T(8,128)S(1)} custom-call(bf16[16,136,128]{2,1,0:T(8,128)(2,1)S(1)} %all-to-all-done.2.got, bf16[1024,1024]{1,0:T(8,128)(2,1)S(1)} %copy-done, bf16[1024,1024]{1,0:T(8,128)(2,1)} %collective-permute-done.1.other), custom_call_target="tpu_custom_call" | custom-call | tf_op jit(solution)/shard_map/pallas_call | solution.py:161
  84.9 0.1 convert_element_type.22
  85.1 16.5 %all_to_all.37 = f16[4,1032,128]{2,1,0:T(8,128)(2,1)S(1)} all-to-all(f16[4,1032,128]{2,1,0:T(8,128)(2,1)S(1)} %convert_element_type.22), channel_id=1, replica_groups=mesh['zh'=4,'x'=4,'zl'=2,'y'=8,'k'=2] {'x'}, dimensions={0} | all-to-all | bytes 2113536 | tf_op jit(solution)/shard_map/all_to_all | solution.py:201
  101.6 0.1 convert_element_type.23.got
  101.7 0.4 shard_map.42
  102.2 0.8 convert_element_type.24
  102.9 3.4 %all-to-all-start.4 = ((f16[8,136,128]{2,1,0:T(8,128)(2,1)}), f16[8,136,128]{2,1,0:T(8,128)(2,1)S(1)}, u32[]{:S(2)}, u32[]{:S(2)}) async-start(f16[8,136,128]{2,1,0:T(8,128)(2,1)} %bitcast.3), calls=%async_computation.4 | async-start | bytes 557056 | tf_op jit(solution)/shard_map/all_to_all | solution.py:201
  106.3 0.5 shard_map.37
  106.9 12.5 %all-to-all-done.4 = f16[8,136,128]{2,1,0:T(8,128)(2,1)S(1)} async-done(((f16[8,136,128]{2,1,0:T(8,128)(2,1)}), f16[8,136,128]{2,1,0:T(8,128)(2,1)S(1)}, u32[]{:S(2)}, u32[]{:S(2)}) %all-to-all-start.4) | async-done | bytes 278560 | tf_op jit(solution)/shard_map/all_to_all | solution.py:201
  119.4 0.8 shard_map.43
  (7 shorter events, 0.0 us)
Async XLA Ops:
  0.0 34.0 %copy-start.1 = (bf16[1024,512]{1,0:T(8,128)(2,1)S(1)}, bf16[1024,512]{1,0:T(8,128)(2,1)}, u32[]{:S(2)}) copy-start(bf16[1024,512]{1,0:T(8,128)(2,1)} %fisher.1) | copy-start | bytes 3145732
  0.0 34.0 %collective-permute-start = (bf16[1024,512]{1,0:T(8,128)(2,1)}, bf16[1024,512]{1,0:T(8,128)(2,1)S(1)}, u32[]{:S(2)}, u32[]{:S(2)}) collective-permute-start(bf16[1024,512]{1,0:T(8,128)(2,1)} %fisher.1), channel_id=1, source_target_pairs={{0,1},{1,0},{2,3},{3,2},{4,5},{5,4},{6,7},{7,6},{8,9},{9,8},{10,11... | collective-permute-start | bytes 3145736 | tf_op jit(solution)/shard_map/ppermute | solution.py:185
  2.0 0.8 copy-start.2
  3.6 30.4 %all-to-all-start = ((bf16[32,16,512]{2,1,0:T(8,128)(2,1)}), bf16[32,16,512]{2,1,0:T(8,128)(2,1)S(1)}, u32[]{:S(2)}, u32[]{:S(2)}) async-start(bf16[32,16,512]{2,1,0:T(8,128)(2,1)} %bitcast.1), calls=%async_computation | async-start | bytes 1048576 | tf_op jit(solution)/shard_map/all_to_all | solution.py:204
  16.9 51.3 %collective-permute-start.1 = (bf16[1024,1024]{1,0:T(8,128)(2,1)}, bf16[1024,1024]{1,0:T(8,128)(2,1)}, u32[]{:S(2)}, u32[]{:S(2)}) collective-permute-start(bf16[1024,1024]{1,0:T(8,128)(2,1)} %index.1), channel_id=1, source_target_pairs={{0,1},{1,0},{2,3},{3,2},{4,5},{5,4},{6,7},{7,6},{8,9},{9,8},{10,11... | collective-permute-start | bytes 6291464 | tf_op jit(solution)/shard_map/ppermute | solution.py:185
  62.3 20.3 %copy-start = (bf16[1024,1024]{1,0:T(8,128)(2,1)S(1)}, bf16[1024,1024]{1,0:T(8,128)(2,1)}, u32[]{:S(2)}) copy-start(bf16[1024,1024]{1,0:T(8,128)(2,1)} %index.1) | copy-start | bytes 6291460
  63.5 19.0 %all-to-all-start.2 = ((bf16[16,136,128]{2,1,0:T(8,128)(2,1)}), bf16[16,136,128]{2,1,0:T(8,128)(2,1)S(1)}, u32[]{:S(2)}, u32[]{:S(2)}) async-start(bf16[16,136,128]{2,1,0:T(8,128)(2,1)} %shard_map.40), calls=%async_computation.2 | async-start | bytes 1114112 | tf_op jit(solution)/shard_map/all_to_all | solution.py:201
  102.9 16.4 %all-to-all-start.4 = ((f16[8,136,128]{2,1,0:T(8,128)(2,1)}), f16[8,136,128]{2,1,0:T(8,128)(2,1)S(1)}, u32[]{:S(2)}, u32[]{:S(2)}) async-start(f16[8,136,128]{2,1,0:T(8,128)(2,1)} %bitcast.3), calls=%async_computation.4 | async-start | bytes 557056 | tf_op jit(solution)/shard_map/all_to_all | solution.py:201

commit v10 on v5

--- a/solution.py
+++ b/solution.py
@@ -89,10 +89,15 @@
         out[copy, tiles * height :] = tail
 
 
-def score_kernel(height, got, index, other, out, held, sem):
+def score_kernel(height, got, index, other, out, held, sems):
     count, features = index.shape
-    copy = pltpu.make_async_copy(other, held, sem)
-    copy.start()
+    depth = count // sems.shape[0]
+    copies = [
+        pltpu.make_async_copy(other.at[pl.ds(i * depth, depth)], held.at[pl.ds(i * depth, depth)], sems.at[i])
+        for i in range(sems.shape[0])
+    ]
+    for copy in copies:
+        copy.start()
     sources, tiles = got.shape[0], features // LANES
     unit = jnp.concatenate(
         [got[:, c * height : (c + 1) * height].reshape(sources * height, LANES) for c in range(tiles)], axis=1
@@ -108,15 +113,16 @@
             tail += pltpu.roll(tails[i * per + z], z * height, 1)
         out[i, 2 * tiles * rows :] = tail
 
-    def put(block, scores):
+    def put(first, scores):
         for i in range(chunks):
-            for c in range(tiles):
-                at = (block * tiles + c) * rows
+            for c in range(scores.shape[1] // LANES):
+                at = (first + c) * rows
                 out[i, at : at + rows] = scores[i * rows : (i + 1) * rows, c * LANES : (c + 1) * LANES]
 
     put(0, dot_t(unit, index[...]) * 8.0)
-    copy.wait()
-    put(1, dot_t(unit, held[...]) * 8.0)
+    for i, copy in enumerate(copies):
+        copy.wait()
+        put(tiles + i * depth // LANES, dot_t(unit, held[i * depth : (i + 1) * depth]) * 8.0)
 
 
 def combine(tiles, height, factor, got):
@@ -203,7 +209,7 @@
 
     sent = call(
         functools.partial(score_kernel, height), (VMEM, VMEM, pl.ANY), (x, wide, LANES), F32, got, index, index_other,
-        scratch_shapes=[VMEM((count, features), BF16), pltpu.SemaphoreType.DMA],
+        scratch_shapes=[VMEM((count, features), BF16), pltpu.SemaphoreType.DMA((4,))],
     )
     got = exchange(sent.astype(F16), "x", sent.shape).astype(F32)
 

time: 119 us -> 120 us (level)
  no operation moved by 1% of the time
where the time goes in v10:
time: 120 us; the launch traced here: 119 us
  blocking collectives  60.1 us (50%)
  waiting for transfers between devices  28 us (23%)
  starting transfers between devices  22.4 us (19%)
  Pallas kernels  7.16 us (6%)
    all_to_all x3, blocking collectives, exchange(): lax.all_to_all(sent.reshape(-1, LANES), axes, 0, 0, tiled=True)  60.1 us
    all_to_all x1, waiting for transfers between devices, local(): held = lax.all_to_all(copies, (*ROW, 'k'), 0, 0, tiled=True)  14.7 us
    all_to_all x1, waiting for transfers between devices, exchange(): lax.all_to_all(sent.reshape(-1, LANES), axes, 0, 0, tiled=True)  13.3 us
    ppermute x2, starting transfers between devices, swap(): return lax.ppermute(array, 'k', [(0, 1), (1, 0)])  11 us
    all_to_all x1, starting transfers between devices, local(): held = lax.all_to_all(copies, (*ROW, 'k'), 0, 0, tiled=True)  7.69 us
    pallas_call x6, Pallas kernels, call(): pl.pallas_call(kernel, out_shape=jax.ShapeDtypeStruct(shape, dtype), in_s...  7.16 us
    all_to_all x1, starting transfers between devices, exchange(): lax.all_to_all(sent.reshape(-1, LANES), axes, 0, 0, tiled=True)  3.66 us
  transfers between devices with their start and end apart: 4, of which 2 were waited for; matrix products, arithmetic and copies ran while one was open for 0% of the time, Pallas kernels for 2%

profile of v10, /device:TPU:1, one launch (start us, length us, event | category | flops | bytes accessed | tf_op | source)
XLA Modules:
  0.0 119.0 jit_solution(16351917183356172565)
XLA Ops:
  0.0 8.9 %collective-permute-start = (bf16[1024,512]{1,0:T(8,128)(2,1)}, bf16[1024,512]{1,0:T(8,128)(2,1)S(1)}, u32[]{:S(2)}, u32[]{:S(2)}) collective-permute-start(bf16[1024,512]{1,0:T(8,128)(2,1)} %fisher.1), channel_id=1, source_target_pairs={{0,1},{1,0},{2,3},{3,2},{4,5},{5,4},{6,7},{7,6},{8,9},{9,8},{10,11... | collective-permute-start | bytes 3145736 | tf_op jit(solution)/shard_map/ppermute | solution.py:178
  8.9 0.0 copy-start.2
  8.9 0.7 copy-done.2
  9.6 0.8 shard_map.37
  10.5 7.7 %all-to-all-start = ((bf16[32,16,512]{2,1,0:T(8,128)(2,1)}), bf16[32,16,512]{2,1,0:T(8,128)(2,1)S(1)}, u32[]{:S(2)}, u32[]{:S(2)}) async-start(bf16[32,16,512]{2,1,0:T(8,128)(2,1)} %bitcast.1), calls=%async_computation | async-start | bytes 1048576 | tf_op jit(solution)/shard_map/all_to_all | solution.py:197
  18.2 2.1 %collective-permute-start.1 = (bf16[1024,1024]{1,0:T(8,128)(2,1)}, bf16[1024,1024]{1,0:T(8,128)(2,1)}, u32[]{:S(2)}, u32[]{:S(2)}) collective-permute-start(bf16[1024,1024]{1,0:T(8,128)(2,1)} %index.1), channel_id=1, source_target_pairs={{0,1},{1,0},{2,3},{3,2},{4,5},{5,4},{6,7},{7,6},{8,9},{9,8},{10,11... | collective-permute-start | bytes 6291464 | tf_op jit(solution)/shard_map/ppermute | solution.py:178
  20.3 14.7 %all-to-all-done = bf16[32,16,512]{2,1,0:T(8,128)(2,1)S(1)} async-done(((bf16[32,16,512]{2,1,0:T(8,128)(2,1)}), bf16[32,16,512]{2,1,0:T(8,128)(2,1)S(1)}, u32[]{:S(2)}, u32[]{:S(2)}) %all-to-all-start) | async-done | bytes 524320 | tf_op jit(solution)/shard_map/all_to_all | solution.py:197
  35.0 0.0 collective-permute-done.other
  35.0 0.0 copy-done.1
  35.0 0.9 shard_map.38
  35.9 0.1 convert_element_type.20
  36.0 26.2 %all_to_all.36 = f16[16,136,128]{2,1,0:T(8,128)(2,1)S(1)} all-to-all(f16[16,136,128]{2,1,0:T(8,128)(2,1)S(1)} %convert_element_type.20), channel_id=1, replica_groups=mesh['zh'=4,'x'=4,'zl'=2,'y'=8,'k'=2] {'zl','y'}, dimensions={0} | all-to-all | bytes 1114112 | tf_op jit(solution)/shard_map/all_to_all | solution.py:194
  62.2 0.1 convert_element_type.21.got
  62.2 1.2 shard_map.39
  63.4 3.7 %all-to-all-start.2 = ((bf16[16,136,128]{2,1,0:T(8,128)(2,1)}), bf16[16,136,128]{2,1,0:T(8,128)(2,1)S(1)}, u32[]{:S(2)}, u32[]{:S(2)}) async-start(bf16[16,136,128]{2,1,0:T(8,128)(2,1)} %shard_map.39), calls=%async_computation.2 | async-start | bytes 1114112 | tf_op jit(solution)/shard_map/all_to_all | solution.py:194
  67.1 0.0 collective-permute-done.1.other
  67.1 13.3 %all-to-all-done.2.got = bf16[16,136,128]{2,1,0:T(8,128)(2,1)S(1)} async-done(((bf16[16,136,128]{2,1,0:T(8,128)(2,1)}), bf16[16,136,128]{2,1,0:T(8,128)(2,1)S(1)}, u32[]{:S(2)}, u32[]{:S(2)}) %all-to-all-start.2) | async-done | bytes 557088 | tf_op jit(solution)/shard_map/all_to_all | solution.py:194
  80.4 3.0 %shard_map.40 = f32[4,1032,128]{2,1,0:T(8,128)S(1)} custom-call(bf16[16,136,128]{2,1,0:T(8,128)(2,1)S(1)} %all-to-all-done.2.got, bf16[1024,1024]{1,0:T(8,128)(2,1)S(1)} %copy-done, bf16[1024,1024]{1,0:T(8,128)(2,1)} %collective-permute-done.1.other), custom_call_target="tpu_custom_call" | custom-call | tf_op jit(solution)/shard_map/pallas_call | solution.py:167
  83.4 0.1 convert_element_type.22
  83.6 15.1 %all_to_all.37 = f16[4,1032,128]{2,1,0:T(8,128)(2,1)S(1)} all-to-all(f16[4,1032,128]{2,1,0:T(8,128)(2,1)S(1)} %convert_element_type.22), channel_id=1, replica_groups=mesh['zh'=4,'x'=4,'zl'=2,'y'=8,'k'=2] {'x'}, dimensions={0} | all-to-all | bytes 2113536 | tf_op jit(solution)/shard_map/all_to_all | solution.py:194
  98.7 0.1 convert_element_type.23.got
  98.8 0.4 shard_map.41
  99.3 18.8 %all_to_all.38 = f16[8,136,128]{2,1,0:T(8,128)(2,1)S(1)} all-to-all(f16[8,136,128]{2,1,0:T(8,128)(2,1)S(1)} %bitcast.7), channel_id=1, replica_groups=mesh['zh'=4,'x'=4,'zl'=2,'y'=8,'k'=2] {'zh','k'}, dimensions={0} | all-to-all | bytes 557056 | tf_op jit(solution)/shard_map/all_to_all | solution.py:194
  118.1 0.8 shard_map.42
  (5 shorter events, 0.1 us)
Async XLA Ops:
  0.0 35.0 %copy-start.1 = (bf16[1024,512]{1,0:T(8,128)(2,1)S(1)}, bf16[1024,512]{1,0:T(8,128)(2,1)}, u32[]{:S(2)}) copy-start(bf16[1024,512]{1,0:T(8,128)(2,1)} %fisher.1) | copy-start | bytes 3145732
  0.0 35.0 %collective-permute-start = (bf16[1024,512]{1,0:T(8,128)(2,1)}, bf16[1024,512]{1,0:T(8,128)(2,1)S(1)}, u32[]{:S(2)}, u32[]{:S(2)}) collective-permute-start(bf16[1024,512]{1,0:T(8,128)(2,1)} %fisher.1), channel_id=1, source_target_pairs={{0,1},{1,0},{2,3},{3,2},{4,5},{5,4},{6,7},{7,6},{8,9},{9,8},{10,11... | collective-permute-start | bytes 3145736 | tf_op jit(solution)/shard_map/ppermute | solution.py:178
  8.9 0.8 copy-start.2
  10.5 24.6 %all-to-all-start = ((bf16[32,16,512]{2,1,0:T(8,128)(2,1)}), bf16[32,16,512]{2,1,0:T(8,128)(2,1)S(1)}, u32[]{:S(2)}, u32[]{:S(2)}) async-start(bf16[32,16,512]{2,1,0:T(8,128)(2,1)} %bitcast.1), calls=%async_computation | async-start | bytes 1048576 | tf_op jit(solution)/shard_map/all_to_all | solution.py:197
  18.2 48.9 %collective-permute-start.1 = (bf16[1024,1024]{1,0:T(8,128)(2,1)}, bf16[1024,1024]{1,0:T(8,128)(2,1)}, u32[]{:S(2)}, u32[]{:S(2)}) collective-permute-start(bf16[1024,1024]{1,0:T(8,128)(2,1)} %index.1), channel_id=1, source_target_pairs={{0,1},{1,0},{2,3},{3,2},{4,5},{5,4},{6,7},{7,6},{8,9},{9,8},{10,11... | collective-permute-start | bytes 6291464 | tf_op jit(solution)/shard_map/ppermute | solution.py:178
  62.2 18.2 %copy-start = (bf16[1024,1024]{1,0:T(8,128)(2,1)S(1)}, bf16[1024,1024]{1,0:T(8,128)(2,1)}, u32[]{:S(2)}) copy-start(bf16[1024,1024]{1,0:T(8,128)(2,1)} %index.1) | copy-start | bytes 6291460
  63.4 17.0 %all-to-all-start.2 = ((bf16[16,136,128]{2,1,0:T(8,128)(2,1)}), bf16[16,136,128]{2,1,0:T(8,128)(2,1)S(1)}, u32[]{:S(2)}, u32[]{:S(2)}) async-start(bf16[16,136,128]{2,1,0:T(8,128)(2,1)} %shard_map.39), calls=%async_computation.2 | async-start | bytes 1114112 | tf_op jit(solution)/shard_map/all_to_all | solution.py:194

commit v11 on v5

--- a/solution.py
+++ b/solution.py
@@ -71,7 +71,7 @@
         out[to, tiles * height :] = across(e[rows])
 
 
-def unit_kernel(height, got, out):
+def unit_kernel(height, got, out, block, sems):
     tiles = (out.shape[1] - TAIL) // height
     full = [jnp.zeros((height, LANES), F32)] * tiles
     for i in range(got.shape[0]):
@@ -83,10 +83,14 @@
     squares = jnp.sum(unit * unit, axis=-1, keepdims=True)
     unit = unit.astype(BF16)
     tail = across(g, *pieces(squares)).astype(BF16)
-    for copy in range(out.shape[0]):
-        for c in range(tiles):
-            out[copy, c * height : (c + 1) * height] = unit[:, c * LANES : (c + 1) * LANES]
-        out[copy, tiles * height :] = tail
+    for c in range(tiles):
+        block[c * height : (c + 1) * height] = unit[:, c * LANES : (c + 1) * LANES]
+    block[tiles * height :] = tail
+    copies = [pltpu.make_async_copy(block, out.at[i], sems.at[i]) for i in range(out.shape[0])]
+    for copy in copies:
+        copy.start()
+    for copy in copies:
+        copy.wait()
 
 
 def score_kernel(height, got, index, other, out, held, sem):
@@ -157,12 +161,12 @@
             out[k * height : (k + 1) * height, c * LANES : (c + 1) * LANES] = total[c] / norm
 
 
-def call(kernel, spaces, shape, dtype, *args, **kwargs):
+def call(kernel, spaces, shape, dtype, *args, out_space=VMEM, **kwargs):
     return pl.pallas_call(
         kernel,
         out_shape=jax.ShapeDtypeStruct(shape, dtype),
         in_specs=[pl.BlockSpec(memory_space=space) for space in spaces],
-        out_specs=pl.BlockSpec(memory_space=VMEM),
+        out_specs=pl.BlockSpec(memory_space=out_space),
         compiler_params=pltpu.CompilerParams(vmem_limit_bytes=16 << 20),
         **kwargs,
     )(*args)
@@ -198,7 +202,10 @@
     )
     got = exchange(sent.astype(F16), PAIR, (pairs, deep, LANES)).astype(F32)
 
-    sent = call(functools.partial(unit_kernel, height), (VMEM,), got.shape, BF16, got)
+    sent = call(
+        functools.partial(unit_kernel, height), (VMEM,), got.shape, BF16, got, out_space=pl.ANY,
+        scratch_shapes=[VMEM((deep, LANES), BF16), pltpu.SemaphoreType.DMA((pairs,))],
+    )
     got = exchange(sent, PAIR, got.shape)
 
     sent = call(

time: 119 us -> 120 us (level)
  transfers between devices with their start and end apart: 4 -> 4, of which waited for: 2 -> 2; matrix products, arithmetic and copies ran while one was open for 0% -> 0% of each run, Pallas kernels for 2% -> 3%
where the time goes in v11:
time: 120 us; the launch traced here: 118 us
  blocking collectives  60.1 us (50%)
  waiting for transfers between devices  28 us (23%)
  starting transfers between devices  22.4 us (19%)
  Pallas kernels  6.61 us (6%)
    all_to_all x3, blocking collectives, exchange(): lax.all_to_all(sent.reshape(-1, LANES), axes, 0, 0, tiled=True)  60.1 us
    all_to_all x1, waiting for transfers between devices, local(): held = lax.all_to_all(copies, (*ROW, 'k'), 0, 0, tiled=True)  14.7 us
    all_to_all x1, waiting for transfers between devices, exchange(): lax.all_to_all(sent.reshape(-1, LANES), axes, 0, 0, tiled=True)  13.3 us
    ppermute x2, starting transfers between devices, swap(): return lax.ppermute(array, 'k', [(0, 1), (1, 0)])  11 us
    all_to_all x1, starting transfers between devices, local(): held = lax.all_to_all(copies, (*ROW, 'k'), 0, 0, tiled=True)  7.69 us
    pallas_call x6, Pallas kernels, call(): pl.pallas_call(kernel, out_shape=jax.ShapeDtypeStruct(shape, dtype), in_s...  6.61 us
    all_to_all x1, starting transfers between devices, exchange(): lax.all_to_all(sent.reshape(-1, LANES), axes, 0, 0, tiled=True)  3.67 us
  transfers between devices with their start and end apart: 4, of which 2 were waited for; matrix products, arithmetic and copies ran while one was open for 0% of the time, Pallas kernels for 3%

profile of v11, /device:TPU:1, one launch (start us, length us, event | category | flops | bytes accessed | tf_op | source)
XLA Modules:
  0.0 118.4 jit_solution(12932336620164008383)
XLA Ops:
  0.0 8.9 %collective-permute-start = (bf16[1024,512]{1,0:T(8,128)(2,1)}, bf16[1024,512]{1,0:T(8,128)(2,1)S(1)}, u32[]{:S(2)}, u32[]{:S(2)}) collective-permute-start(bf16[1024,512]{1,0:T(8,128)(2,1)} %fisher.1), channel_id=1, source_target_pairs={{0,1},{1,0},{2,3},{3,2},{4,5},{5,4},{6,7},{7,6},{8,9},{9,8},{10,11... | collective-permute-start | bytes 3145736 | tf_op jit(solution)/shard_map/ppermute | solution.py:176
  8.9 0.0 copy-start.2
  8.9 0.7 copy-done.2
  9.6 0.8 shard_map.37
  10.5 7.7 %all-to-all-start = ((bf16[32,16,512]{2,1,0:T(8,128)(2,1)}), bf16[32,16,512]{2,1,0:T(8,128)(2,1)S(1)}, u32[]{:S(2)}, u32[]{:S(2)}) async-start(bf16[32,16,512]{2,1,0:T(8,128)(2,1)} %bitcast.1), calls=%async_computation | async-start | bytes 1048576 | tf_op jit(solution)/shard_map/all_to_all | solution.py:195
  18.2 2.1 %collective-permute-start.1 = (bf16[1024,1024]{1,0:T(8,128)(2,1)}, bf16[1024,1024]{1,0:T(8,128)(2,1)}, u32[]{:S(2)}, u32[]{:S(2)}) collective-permute-start(bf16[1024,1024]{1,0:T(8,128)(2,1)} %index.1), channel_id=1, source_target_pairs={{0,1},{1,0},{2,3},{3,2},{4,5},{5,4},{6,7},{7,6},{8,9},{9,8},{10,11... | collective-permute-start | bytes 6291464 | tf_op jit(solution)/shard_map/ppermute | solution.py:176
  20.3 14.7 %all-to-all-done = bf16[32,16,512]{2,1,0:T(8,128)(2,1)S(1)} async-done(((bf16[32,16,512]{2,1,0:T(8,128)(2,1)}), bf16[32,16,512]{2,1,0:T(8,128)(2,1)S(1)}, u32[]{:S(2)}, u32[]{:S(2)}) %all-to-all-start) | async-done | bytes 524320 | tf_op jit(solution)/shard_map/all_to_all | solution.py:195
  35.0 0.0 collective-permute-done.other
  35.0 0.9 shard_map.38
  35.9 0.1 convert_element_type.20
  36.0 26.2 %all_to_all.36 = f16[16,136,128]{2,1,0:T(8,128)(2,1)S(1)} all-to-all(f16[16,136,128]{2,1,0:T(8,128)(2,1)S(1)} %convert_element_type.20), channel_id=1, replica_groups=mesh['zh'=4,'x'=4,'zl'=2,'y'=8,'k'=2] {'zl','y'}, dimensions={0} | all-to-all | bytes 1114112 | tf_op jit(solution)/shard_map/all_to_all | solution.py:192
  62.2 0.1 convert_element_type.21.got
  62.2 1.3 %shard_map.39 = bf16[16,136,128]{2,1,0:T(8,128)(2,1)} custom-call(f32[16,136,128]{2,1,0:T(8,128)S(1)} %convert_element_type.21.got), custom_call_target="tpu_custom_call" | custom-call | tf_op jit(solution)/shard_map/pallas_call | solution.py:165
  63.6 3.7 %all-to-all-start.2 = ((bf16[16,136,128]{2,1,0:T(8,128)(2,1)}), bf16[16,136,128]{2,1,0:T(8,128)(2,1)S(1)}, u32[]{:S(2)}, u32[]{:S(2)}) async-start(bf16[16,136,128]{2,1,0:T(8,128)(2,1)} %shard_map.39), calls=%async_computation.2 | async-start | bytes 1114112 | tf_op jit(solution)/shard_map/all_to_all | solution.py:192
  67.3 0.0 collective-permute-done.1.other
  67.3 13.3 %all-to-all-done.2.got = bf16[16,136,128]{2,1,0:T(8,128)(2,1)S(1)} async-done(((bf16[16,136,128]{2,1,0:T(8,128)(2,1)}), bf16[16,136,128]{2,1,0:T(8,128)(2,1)S(1)}, u32[]{:S(2)}, u32[]{:S(2)}) %all-to-all-start.2) | async-done | bytes 557088 | tf_op jit(solution)/shard_map/all_to_all | solution.py:192
  80.5 0.0 copy-done
  80.5 2.3 %shard_map.40 = f32[4,1032,128]{2,1,0:T(8,128)S(1)} custom-call(bf16[16,136,128]{2,1,0:T(8,128)(2,1)S(1)} %all-to-all-done.2.got, bf16[1024,1024]{1,0:T(8,128)(2,1)S(1)} %copy-done, bf16[1024,1024]{1,0:T(8,128)(2,1)} %collective-permute-done.1.other), custom_call_target="tpu_custom_call" | custom-call | tf_op jit(solution)/shard_map/pallas_call | solution.py:165
  82.9 0.1 convert_element_type.22
  83.0 15.1 %all_to_all.37 = f16[4,1032,128]{2,1,0:T(8,128)(2,1)S(1)} all-to-all(f16[4,1032,128]{2,1,0:T(8,128)(2,1)S(1)} %convert_element_type.22), channel_id=1, replica_groups=mesh['zh'=4,'x'=4,'zl'=2,'y'=8,'k'=2] {'x'}, dimensions={0} | all-to-all | bytes 2113536 | tf_op jit(solution)/shard_map/all_to_all | solution.py:192
  98.2 0.1 convert_element_type.23.got
  98.3 0.4 shard_map.41
  98.8 18.8 %all_to_all.38 = f16[8,136,128]{2,1,0:T(8,128)(2,1)S(1)} all-to-all(f16[8,136,128]{2,1,0:T(8,128)(2,1)S(1)} %bitcast.7), channel_id=1, replica_groups=mesh['zh'=4,'x'=4,'zl'=2,'y'=8,'k'=2] {'zh','k'}, dimensions={0} | all-to-all | bytes 557056 | tf_op jit(solution)/shard_map/all_to_all | solution.py:192
  117.6 0.8 shard_map.42
  (5 shorter events, 0.1 us)
Async XLA Ops:
  0.0 35.0 %copy-start.1 = (bf16[1024,512]{1,0:T(8,128)(2,1)S(1)}, bf16[1024,512]{1,0:T(8,128)(2,1)}, u32[]{:S(2)}) copy-start(bf16[1024,512]{1,0:T(8,128)(2,1)} %fisher.1) | copy-start | bytes 3145732
  0.0 35.0 %collective-permute-start = (bf16[1024,512]{1,0:T(8,128)(2,1)}, bf16[1024,512]{1,0:T(8,128)(2,1)S(1)}, u32[]{:S(2)}, u32[]{:S(2)}) collective-permute-start(bf16[1024,512]{1,0:T(8,128)(2,1)} %fisher.1), channel_id=1, source_target_pairs={{0,1},{1,0},{2,3},{3,2},{4,5},{5,4},{6,7},{7,6},{8,9},{9,8},{10,11... | collective-permute-start | bytes 3145736 | tf_op jit(solution)/shard_map/ppermute | solution.py:176
  8.9 0.8 copy-start.2
  10.5 24.6 %all-to-all-start = ((bf16[32,16,512]{2,1,0:T(8,128)(2,1)}), bf16[32,16,512]{2,1,0:T(8,128)(2,1)S(1)}, u32[]{:S(2)}, u32[]{:S(2)}) async-start(bf16[32,16,512]{2,1,0:T(8,128)(2,1)} %bitcast.1), calls=%async_computation | async-start | bytes 1048576 | tf_op jit(solution)/shard_map/all_to_all | solution.py:195
  18.2 49.1 %collective-permute-start.1 = (bf16[1024,1024]{1,0:T(8,128)(2,1)}, bf16[1024,1024]{1,0:T(8,128)(2,1)}, u32[]{:S(2)}, u32[]{:S(2)}) collective-permute-start(bf16[1024,1024]{1,0:T(8,128)(2,1)} %index.1), channel_id=1, source_target_pairs={{0,1},{1,0},{2,3},{3,2},{4,5},{5,4},{6,7},{7,6},{8,9},{9,8},{10,11... | collective-permute-start | bytes 6291464 | tf_op jit(solution)/shard_map/ppermute | solution.py:176
  62.2 18.4 %copy-start = (bf16[1024,1024]{1,0:T(8,128)(2,1)S(1)}, bf16[1024,1024]{1,0:T(8,128)(2,1)}, u32[]{:S(2)}) copy-start(bf16[1024,1024]{1,0:T(8,128)(2,1)} %index.1) | copy-start | bytes 6291460
  63.6 17.0 %all-to-all-start.2 = ((bf16[16,136,128]{2,1,0:T(8,128)(2,1)}), bf16[16,136,128]{2,1,0:T(8,128)(2,1)S(1)}, u32[]{:S(2)}, u32[]{:S(2)}) async-start(bf16[16,136,128]{2,1,0:T(8,128)(2,1)} %shard_map.39), calls=%async_computation.2 | async-start | bytes 1114112 | tf_op jit(solution)/shard_map/all_to_all | solution.py:192
